TPU v7x, 768 devices: a whole 4x8x12 slice. The times are simulated.
768 devices in a mesh: row: 24 (over x_lo, z), col: 32 (over y, x_hi, core).
Axes of the slice: x: 4 (x_hi: 2, x_lo: 2; x = x_hi * 2 + x_lo), y: 8, z: 12, core: 2. Of those that a mesh axis runs over, the one named last changes fastest.
Arguments:
- image_emb: bfloat16 [384, 32, 1024], P('row', 'col'), may hold values from -16 to 16
- text_emb: bfloat16 [512, 24, 1024], P('col', 'row'), may hold values from -16 to 16
- logit_scale: float32 [1], replicated, may hold values from 2.5 to 5
Outputs:
- loss: float32 [], replicated
- image_grad: float32 [384, 32, 1024], P('row', 'col')
- text_grad: float32 [512, 24, 1024], P('col', 'row')
All inputs are finite; a program needn't handle non-finite values.
Results may differ from a plain program's by a relative error of at most 0.0075.
Values may be sent and summed in bfloat16 or wider, within the bound.
No kernel may reach another device: no remote copies, remote signals or barrier semaphores. Data moves between devices by JAX's collectives and lax.ppermute only.
A program may use at most 32 MiB of HBM per device.

v0:
```python
import jax
import jax.numpy as jnp
from jax import lax
from jax.sharding import PartitionSpec as P


def shards(image_emb, text_emb, logit_scale):
    row_count = lax.axis_size("row")
    col_count = lax.axis_size("col")
    row_index = lax.axis_index("row")
    col_index = lax.axis_index("col")
    pairs_each = image_emb.shape[0]
    width = image_emb.shape[2]
    block_rows = pairs_each * col_count
    block_cols = pairs_each * row_count
    total_pairs = block_rows * row_count
    factor = logit_scale[0]
    images = lax.all_gather(image_emb, "col", axis=1, tiled=True).reshape(block_rows, width)
    texts = lax.all_gather(text_emb, "row", axis=1, tiled=True).reshape(block_cols, width)
    scores = factor * lax.dot_general(
        images, texts, (((1,), (1,)), ((), ())), preferred_element_type=jnp.float32
    )
    row_ids = row_index * block_rows + jnp.arange(block_rows, dtype=jnp.int32)
    col_ids = col_index * block_cols + jnp.arange(block_cols, dtype=jnp.int32)
    eye = row_ids[:, None] == col_ids[None, :]
    local_row_peak = jnp.max(scores, axis=1)
    local_col_peak = jnp.max(scores, axis=0)
    row_peak = lax.pmax(local_row_peak, "col")
    col_peak = lax.pmax(local_col_peak, "row")
    row_total = lax.psum(jnp.sum(jnp.exp(scores - row_peak[:, None]), axis=1), "col")
    col_total = lax.psum(jnp.sum(jnp.exp(scores - col_peak[None, :]), axis=0), "row")
    row_lse = row_peak + jnp.log(row_total)
    col_lse = col_peak + jnp.log(col_total)
    local_loss = jnp.where(col_index == 0, jnp.sum(row_lse), 0.0) + jnp.where(
        row_index == 0, jnp.sum(col_lse), 0.0
    )
    local_loss = local_loss - 2.0 * jnp.sum(jnp.where(eye, scores, 0.0))
    loss = lax.psum(local_loss, ("row", "col")) / (2.0 * total_pairs)
    delta = factor * (
        jnp.exp(scores - row_lse[:, None])
        + jnp.exp(scores - col_lse[None, :])
        - 2.0 * eye.astype(jnp.float32)
    )
    delta = delta.astype(jnp.bfloat16)
    image_part = jnp.dot(delta, texts, preferred_element_type=jnp.float32).reshape(
        pairs_each, col_count, width
    )
    text_part = lax.dot_general(
        delta, images, (((0,), (0,)), ((), ())), preferred_element_type=jnp.float32
    )
    text_part = text_part.reshape(pairs_each, row_count, width)
    image_grad = lax.psum_scatter(image_part, "col", scatter_dimension=1, tiled=True)
    text_grad = lax.psum_scatter(text_part, "row", scatter_dimension=1, tiled=True)
    return (loss, image_grad, text_grad)


def solution(mesh):
    placed = (P("row", "col", None), P("col", "row", None), P())
    return jax.shard_map(
        shards,
        mesh=mesh,
        in_specs=placed,
        out_specs=(P(), P("row", "col", None), P("col", "row", None)),
        check_vma=False,
    )
```

profile of v0, /device:TPU:16, one launch (start us, length us, event | category | flops | bytes accessed | tf_op | source)
XLA Modules:
  0.0 584.0 jit_solution(926770516509730380)
XLA Ops:
  7.2 0.0 all-gather.2.cloned.1.call-start
  7.2 0.7 all-gather.2.cloned.1.call-update
  7.9 0.0 reduce-scatter.5.cloned.1.call-start
  8.6 62.0 %all_gather.7 = bf16[16,24,1024]{2,0,1:T(8,128)(2,1)S(1)} all-gather(bf16[16,1,1024]{2,0,1:T(8,128)(2,1)} %param.4), channel_id=1, replica_groups=mesh['row'=24,'col'=32] {'row'}, dimensions={1}, use_global_device_ids=true | all-gather | bytes 819200 | tf_op jit(solution)/shard_map/all_gather | solution.py:19
  70.6 0.4 copy.13
  71.0 35.6 %all-gather.2.cloned.1.call-done = bf16[16,32,1024]{2,0,1:T(8,128)(2,1)} async-done(((bf16[16,1,1024]{2,0,1:T(8,128)(2,1)}), bf16[16,32,1024]{2,0,1:T(8,128)(2,1)}) %all-gather.2.cloned.1.call-update) | async-done | bytes 1048592 | tf_op jit(solution)/shard_map/all_gather | solution.py:18
  106.7 1.8 copy.12
  108.5 0.8 fusion.10
  109.3 50.0 %pmax.15 = f32[384]{0:T(512)S(1)} all-reduce(f32[384]{0:T(512)S(1)} %get-tuple-element.9), channel_id=1, replica_groups=mesh['row'=24,'col'=32] {'row'}, use_global_device_ids=true, to_apply=%region_6.0 | all-reduce | flops 384 | bytes 3072 | tf_op jit(solution)/shard_map/pmax | solution.py:29
  159.3 55.3 %pmax.14 = f32[512]{0:T(512)S(1)} all-reduce(f32[512]{0:T(512)S(1)} %get-tuple-element.10), channel_id=1, replica_groups=mesh['row'=24,'col'=32] {'col'}, use_global_device_ids=true, to_apply=%region_1.0 | all-reduce | flops 512 | bytes 4096 | tf_op jit(solution)/shard_map/pmax | solution.py:28
  214.6 0.9 fusion
  215.5 45.3 %psum.22 = f32[384]{0:T(512)S(1)} all-reduce(f32[384]{0:T(512)S(1)} %get-tuple-element.7), channel_id=1, replica_groups=mesh['row'=24,'col'=32] {'row'}, use_global_device_ids=true, to_apply=%region_8.0 | all-reduce | flops 384 | bytes 3072 | tf_op jit(solution)/shard_map/psum | solution.py:31
  260.8 0.7 fusion.11
  261.5 58.9 %psum.21 = f32[512]{0:T(512)S(1)} all-reduce(f32[512]{0:T(512)S(1)} %get-tuple-element.8), channel_id=1, replica_groups=mesh['row'=24,'col'=32] {'col'}, use_global_device_ids=true, to_apply=%region_3.0 | all-reduce | flops 512 | bytes 4096 | tf_op jit(solution)/shard_map/psum | solution.py:30
  320.3 0.6 fusion.12
  320.9 0.3 fusion.5
  321.3 0.2 copy.15
  321.5 1.7 fusion.6
  323.2 0.0 reduce-scatter.5.cloned.1.call-update
  323.2 0.0 reduce-scatter.3.cloned.1.call-start
  323.3 0.3 fusion.3
  323.6 2.1 fusion.8
  325.7 0.0 reduce-scatter.3.cloned.1.call-update
  327.7 116.0 %psum.23 = f32[]{:T(128)} all-reduce(f32[]{:T(128)S(6)} %sub.49), channel_id=1, replica_groups=mesh['row'=24,'col'=32] {'row','col'}, use_global_device_ids=true, to_apply=%region_11.12 | all-reduce | flops 1 | bytes 8 | tf_op jit(solution)/shard_map/psum | solution.py:38
  444.3 0.0 reduce-scatter.5.cloned.1.call-done
  444.3 1.5 copy.18
  445.8 128.9 %reduce-scatter.3.cloned.1.call-done = f32[16,1,1024]{2,0,1:T(8,128)} async-done(((f32[16,32,1024]{2,0,1:T(8,128)}), f32[16,1,1024]{2,0,1:T(8,128)}) %reduce-scatter.3.cloned.1.call-update) | async-done | bytes 65552 | tf_op jit(solution)/shard_map/reduce_scatter | solution.py:52
  574.8 1.5 copy.17
  (2 shorter events, 0.0 us)
Async XLA Ops:
  7.2 99.5 %all-gather.2.cloned.1.call-start = ((), (), s32[]{:S(2)}) async-start(), calls=%async_computation.2 | async-start | bytes 1081344 | tf_op jit(solution)/shard_map/all_gather | solution.py:18
  7.9 436.4 %reduce-scatter.5.cloned.1.call-start = ((), (), s32[]{:S(2)}) async-start(), calls=%async_computation.4 | async-start | bytes 1638400 | tf_op jit(solution)/shard_map/reduce_scatter | solution.py:53
  323.2 251.5 %reduce-scatter.3.cloned.1.call-start = ((), (), s32[]{:S(2)}) async-start(), calls=%async_computation.3 | async-start | bytes 2162688 | tf_op jit(solution)/shard_map/reduce_scatter | solution.py:52
Sparse Core Ops, SparseCore 0:
  11.9 94.6 all-gather.1
  323.4 116.8 reduce-scatter.4
  445.5 129.1 reduce-scatter.2
where the time goes:
time: 584 us
  blocking collectives  387 us (66%)
  waiting for transfers between devices  165 us (28%)
  between operations  18.2 us (3%)
    reduce_scatter x1, waiting for transfers between devices, shards(): lax.psum_scatter(image_part, 'col', scatter_dimension=1, tiled=True)  129 us
    psum x1, blocking collectives, shards(): loss = lax.psum(local_loss, ('row', 'col')) / (2.0 * total_pairs)  116 us
    all_gather x1, blocking collectives, shards(): lax.all_gather(text_emb, 'row', axis=1, tiled=True)  62 us
    psum x1, blocking collectives, shards(): lax.psum(jnp.sum(jnp.exp(scores - row_peak[:, None]), axis=1), 'col')  58.9 us
    pmax x1, blocking collectives, shards(): row_peak = lax.pmax(local_row_peak, 'col')  55.3 us
    pmax x1, blocking collectives, shards(): col_peak = lax.pmax(local_col_peak, 'row')  50 us
    psum x1, blocking collectives, shards(): lax.psum(jnp.sum(jnp.exp(scores - col_peak[None, :]), axis=0), 'row')  45.3 us
    all_gather x1, waiting for transfers between devices, shards(): lax.all_gather(image_emb, 'col', axis=1, tiled=True)  35.6 us
  transfers between devices with their start and end apart: 3, of which 2 were waited for; matrix products, arithmetic and copies ran while one was open for 1% of the time, Pallas kernels for 0%

commit v1 on v0

v1 whole, which is shorter than its diff:
```python
import jax
import jax.numpy as jnp
from jax import lax
from jax.sharding import Mesh, PartitionSpec as P

COL = ("y", "xh", "c")
ROW = ("xl", "z")


def exchange(x, axes):
    return lax.all_to_all(x, axes, 0, 0, tiled=False)


def spread(x, n):
    return jnp.broadcast_to(x[None], (n, *x.shape))


def pieces(v):
    hi = v.astype(jnp.bfloat16)
    rest = v - hi.astype(jnp.float32)
    mid = rest.astype(jnp.bfloat16)
    low = (rest - mid.astype(jnp.float32)).astype(jnp.bfloat16)
    return hi, mid, low


def lse(x, axis):
    peak = jnp.max(x, axis=axis)
    return peak + jnp.log(jnp.sum(jnp.exp(x - jnp.expand_dims(peak, axis)), axis=axis))


def with_scalar(part, v):
    n, b, w = part.shape
    hi, mid, low = pieces(v)
    lane = lax.broadcasted_iota(jnp.int32, (n, b, 128), 2)
    extra = jnp.where(lane == 0, hi, jnp.where(lane == 1, mid, jnp.where(lane == 2, low, jnp.zeros_like(hi))))
    return jnp.concatenate([part, extra], axis=2)


def split_scalar(got):
    w = got.shape[2] - 128
    got = got.astype(jnp.float32)
    total = jnp.sum(got[:, :, :w], axis=0)
    return total, jnp.sum(got[:, 0, w : w + 3])


def shards(image_emb, text_emb, logit_scale):
    n_row = lax.axis_size(ROW)
    n_col = lax.axis_size(COL)
    row_index = lax.axis_index(ROW)
    col_index = lax.axis_index(COL)
    each, _, width = image_emb.shape
    factor = logit_scale[0]
    block_rows, block_cols = each * n_col, each * n_row
    total_pairs = block_rows * n_row
    texts = exchange(spread(text_emb.reshape(each, width), n_row), ROW).reshape(block_cols, width)
    images = exchange(spread(image_emb.reshape(each, width), n_col), COL).reshape(block_rows, width)
    scores = factor * lax.dot_general(images, texts, (((1,), (1,)), ((), ())), preferred_element_type=jnp.float32)
    i = lax.broadcasted_iota(jnp.int32, (block_rows, 1), 0)
    j = lax.broadcasted_iota(jnp.int32, (1, block_cols), 1)
    row_ids = (each * row_index + i % each) * n_col + i // each
    col_ids = (each * col_index + j % each) * n_row + j // each
    eye = row_ids == col_ids
    local_row = lse(scores, 1)
    local_col = lse(scores, 0)
    diag = jnp.sum(jnp.where(eye, scores, 0.0))
    row_pack = jnp.concatenate([local_row, jnp.full((128,), diag)]).reshape(-1, 128)
    col_pack = local_col.reshape(-1, 128)
    row_got = exchange(spread(row_pack, n_col), COL).reshape(n_col, -1)
    col_got = exchange(spread(col_pack, n_row), ROW).reshape(n_row, -1)
    row_lse = lse(row_got[:, :block_rows], 0)
    col_lse = lse(col_got, 0)
    row_loss = jnp.sum(row_lse) - 2.0 * jnp.sum(row_got[:, block_rows])
    col_loss = jnp.sum(col_lse)
    delta = factor * (
        jnp.exp(scores - row_lse[:, None]) + jnp.exp(scores - col_lse[None, :]) - 2.0 * eye.astype(jnp.float32)
    )
    delta = delta.astype(jnp.bfloat16)
    image_part = jnp.dot(delta, texts, preferred_element_type=jnp.float32).astype(jnp.bfloat16)
    text_part = lax.dot_general(delta, images, (((0,), (0,)), ((), ())), preferred_element_type=jnp.float32).astype(jnp.bfloat16)
    text_got = exchange(with_scalar(text_part.reshape(n_row, each, width), row_loss), ROW)
    image_got = exchange(with_scalar(image_part.reshape(n_col, each, width), col_loss), COL)
    text_grad, row_total = split_scalar(text_got)
    image_grad, col_total = split_scalar(image_got)
    loss = (row_total + col_total) / (2.0 * total_pairs)
    return loss, image_grad.reshape(each, 1, width), text_grad.reshape(each, 1, width)


def solution(mesh):
    fine = Mesh(mesh.devices.reshape(2, 12, 8, 2, 2), ROW + COL)
    placed = (P(ROW, COL, None), P(COL, ROW, None), P())
    return jax.shard_map(
        shards,
        mesh=fine,
        in_specs=placed,
        out_specs=(P(), P(ROW, COL, None), P(COL, ROW, None)),
        check_vma=False,
    )
```

time: 584 us -> 206 us (0.35)
  the two profiles are of different devices: /device:TPU:16 before, /device:TPU:4 now
where the time goes in v1:
time: 206 us
  waiting for transfers between devices  110 us (53%)
  blocking collectives  41.2 us (20%)
  starting transfers between devices  33.5 us (16%)
  other arithmetic  6.95 us (3%)
  between operations  6.57 us (3%)
  local copies, waits for them, and re-layouts  5.15 us (2%)
  matrix products  2.47 us (1%)
    all_to_all x5, waiting for transfers between devices, exchange(): return lax.all_to_all(x, axes, 0, 0, tiled=False)  110 us
    all_to_all x1, blocking collectives, exchange(): return lax.all_to_all(x, axes, 0, 0, tiled=False)  41.2 us
    all_to_all x5, starting transfers between devices, exchange(): return lax.all_to_all(x, axes, 0, 0, tiled=False)  33.5 us
  transfers between devices with their start and end apart: 5, of which 5 were waited for; matrix products, arithmetic and copies ran while one was open for 3% of the time, Pallas kernels for 0%

profile of v1, /device:TPU:4, one launch (start us, length us, event | category | flops | bytes accessed | tf_op | source)
XLA Modules:
  0.0 205.5 jit_solution(9275283660999448874)
XLA Ops:
  0.6 0.0 copy-start
  0.6 0.9 broadcast_in_dim.66
  1.5 41.2 %all_to_all.30 = bf16[32,16,1024]{2,1,0:T(8,128)(2,1)S(1)} all-to-all(bf16[32,16,1024]{2,1,0:T(8,128)(2,1)S(1)} %broadcast_in_dim.66), channel_id=1, replica_groups=mesh['xl'=2,'z'=12,'y'=8,'xh'=2,'c'=2] {'y','xh','c'}, dimensions={0} | all-to-all | bytes 2097152 | tf_op jit(solution)/shard_map/all_to_all | solution.py:11
  42.7 0.0 copy-done
  42.7 1.0 broadcast_in_dim.68
  43.7 13.8 %all-to-all-start.1 = ((bf16[24,16,1024]{2,1,0:T(8,128)(2,1)}), bf16[24,16,1024]{2,1,0:T(8,128)(2,1)S(1)}, u32[]{:S(2)}, u32[]{:S(2)}) async-start(bf16[24,16,1024]{2,1,0:T(8,128)(2,1)} %broadcast_in_dim.68), calls=%async_computation.1 | async-start | bytes 1572864 | tf_op jit(solution)/shard_map/all_to_all | solution.py:11
  58.1 31.2 %all-to-all-done.1 = bf16[24,16,1024]{2,1,0:T(8,128)(2,1)S(1)} async-done(((bf16[24,16,1024]{2,1,0:T(8,128)(2,1)}), bf16[24,16,1024]{2,1,0:T(8,128)(2,1)S(1)}, u32[]{:S(2)}, u32[]{:S(2)}) %all-to-all-start.1) | async-done | bytes 786464 | tf_op jit(solution)/shard_map/all_to_all | solution.py:11
  89.3 0.8 fusion.24
  90.1 0.9 exponential_reduce_fusion
  91.1 0.6 broadcast_in_dim.72
  91.7 5.1 %all-to-all-start.3 = ((f32[24,3,128]{2,1,0:T(4,128)}), f32[24,3,128]{2,1,0:T(4,128)S(1)}, u32[]{:S(2)}, u32[]{:S(2)}) async-start(f32[24,3,128]{2,1,0:T(4,128)} %broadcast_in_dim.72), calls=%async_computation.3 | async-start | bytes 98304 | tf_op jit(solution)/shard_map/all_to_all | solution.py:11
  96.8 0.7 pad_bitcast_fusion
  97.5 10.1 %all-to-all-done.3 = f32[24,3,128]{2,1,0:T(4,128)S(1)} async-done(((f32[24,3,128]{2,1,0:T(4,128)}), f32[24,3,128]{2,1,0:T(4,128)S(1)}, u32[]{:S(2)}, u32[]{:S(2)}) %all-to-all-start.3) | async-done | bytes 36896 | tf_op jit(solution)/shard_map/all_to_all | solution.py:11
  107.6 0.6 broadcast_in_dim.71
  108.2 5.4 %all-to-all-start.2 = ((f32[32,5,128]{2,1,0:T(8,128)}), f32[32,5,128]{2,1,0:T(8,128)S(1)}, u32[]{:S(2)}, u32[]{:S(2)}) async-start(f32[32,5,128]{2,1,0:T(8,128)} %broadcast_in_dim.71), calls=%async_computation.2 | async-start | bytes 262144 | tf_op jit(solution)/shard_map/all_to_all | solution.py:11
  113.8 0.6 fusion.20
  115.8 7.2 %all-to-all-done.2 = f32[32,5,128]{2,1,0:T(8,128)S(1)} async-done(((f32[32,5,128]{2,1,0:T(8,128)}), f32[32,5,128]{2,1,0:T(8,128)S(1)}, u32[]{:S(2)}, u32[]{:S(2)}) %all-to-all-start.2) | async-done | bytes 81952 | tf_op jit(solution)/shard_map/all_to_all | solution.py:11
  123.0 0.6 fusion.25
  123.6 0.8 convolution_convert_fusion
  124.5 1.1 pad_maximum_fusion
  125.6 5.3 %all-to-all-start.5 = ((bf16[32,16,1152]{2,1,0:T(8,128)(2,1)}), bf16[32,16,1152]{2,1,0:T(8,128)(2,1)S(1)}, u32[]{:S(2)}, u32[]{:S(2)}) async-start(bf16[32,16,1152]{2,1,0:T(8,128)(2,1)} %pad_maximum_fusion), calls=%async_computation.5 | async-start | bytes 2359296 | tf_op jit(solution)/shard_map/all_to_all | solution.py:11
  130.9 0.6 slice_reduce_fusion.4
  132.9 0.8 convolution_convert_fusion.1
  133.7 1.1 pad_maximum_fusion.1
  134.7 28.0 %all-to-all-done.5 = bf16[32,16,1152]{2,1,0:T(8,128)(2,1)S(1)} async-done(((bf16[32,16,1152]{2,1,0:T(8,128)(2,1)}), bf16[32,16,1152]{2,1,0:T(8,128)(2,1)S(1)}, u32[]{:S(2)}, u32[]{:S(2)}) %all-to-all-start.5) | async-done | bytes 1179680 | tf_op jit(solution)/shard_map/all_to_all | solution.py:11
  162.7 3.9 %all-to-all-start.4 = ((bf16[24,16,1152]{2,1,0:T(8,128)(2,1)}), bf16[24,16,1152]{2,1,0:T(8,128)(2,1)S(1)}, u32[]{:S(2)}, u32[]{:S(2)}) async-start(bf16[24,16,1152]{2,1,0:T(8,128)(2,1)} %pad_maximum_fusion.1), calls=%async_computation.4 | async-start | bytes 1769472 | tf_op jit(solution)/shard_map/all_to_all | solution.py:11
  166.6 0.2 convert_element_type.60
  166.8 0.1 slice_reduce_fusion
  166.9 0.7 reshape.196
  167.6 0.7 slice_reduce_fusion.3
  168.3 33.3 %all-to-all-done.4 = bf16[24,16,1152]{2,1,0:T(8,128)(2,1)S(1)} async-done(((bf16[24,16,1152]{2,1,0:T(8,128)(2,1)}), bf16[24,16,1152]{2,1,0:T(8,128)(2,1)S(1)}, u32[]{:S(2)}, u32[]{:S(2)}) %all-to-all-start.4) | async-done | bytes 884768 | tf_op jit(solution)/shard_map/all_to_all | solution.py:11
  201.6 0.1 convert_element_type.53
  201.7 0.6 slice_reduce_fusion.5
  202.3 0.1 slice_reduce_fusion.1
  202.4 0.7 reshape.197
  (14 shorter events, 0.2 us)
Async XLA Ops:
  0.6 42.1 %copy-start = (bf16[16,1,1024]{2,0,1:T(8,128)(2,1)S(1)}, bf16[16,1,1024]{2,0,1:T(8,128)(2,1)}, u32[]{:S(2)}) copy-start(bf16[16,1,1024]{2,0,1:T(8,128)(2,1)} %param.4) | copy-start | bytes 98308
  43.7 45.7 %all-to-all-start.1 = ((bf16[24,16,1024]{2,1,0:T(8,128)(2,1)}), bf16[24,16,1024]{2,1,0:T(8,128)(2,1)S(1)}, u32[]{:S(2)}, u32[]{:S(2)}) async-start(bf16[24,16,1024]{2,1,0:T(8,128)(2,1)} %broadcast_in_dim.68), calls=%async_computation.1 | async-start | bytes 1572864 | tf_op jit(solution)/shard_map/all_to_all | solution.py:11
  91.7 15.9 %all-to-all-start.3 = ((f32[24,3,128]{2,1,0:T(4,128)}), f32[24,3,128]{2,1,0:T(4,128)S(1)}, u32[]{:S(2)}, u32[]{:S(2)}) async-start(f32[24,3,128]{2,1,0:T(4,128)} %broadcast_in_dim.72), calls=%async_computation.3 | async-start | bytes 98304 | tf_op jit(solution)/shard_map/all_to_all | solution.py:11
  108.2 14.7 %all-to-all-start.2 = ((f32[32,5,128]{2,1,0:T(8,128)}), f32[32,5,128]{2,1,0:T(8,128)S(1)}, u32[]{:S(2)}, u32[]{:S(2)}) async-start(f32[32,5,128]{2,1,0:T(8,128)} %broadcast_in_dim.71), calls=%async_computation.2 | async-start | bytes 262144 | tf_op jit(solution)/shard_map/all_to_all | solution.py:11
  125.6 37.1 %all-to-all-start.5 = ((bf16[32,16,1152]{2,1,0:T(8,128)(2,1)}), bf16[32,16,1152]{2,1,0:T(8,128)(2,1)S(1)}, u32[]{:S(2)}, u32[]{:S(2)}) async-start(bf16[32,16,1152]{2,1,0:T(8,128)(2,1)} %pad_maximum_fusion), calls=%async_computation.5 | async-start | bytes 2359296 | tf_op jit(solution)/shard_map/all_to_all | solution.py:11
  162.7 38.9 %all-to-all-start.4 = ((bf16[24,16,1152]{2,1,0:T(8,128)(2,1)}), bf16[24,16,1152]{2,1,0:T(8,128)(2,1)S(1)}, u32[]{:S(2)}, u32[]{:S(2)}) async-start(bf16[24,16,1152]{2,1,0:T(8,128)(2,1)} %pad_maximum_fusion.1), calls=%async_computation.4 | async-start | bytes 1769472 | tf_op jit(solution)/shard_map/all_to_all | solution.py:11

commit v2 on v1

v2 whole, which is shorter than its diff:
```python
import jax
import jax.numpy as jnp
from jax import lax
from jax.sharding import Mesh, PartitionSpec as P


COL = ("y", "xh", "c")
ROW = ("xl", "z")
COL_OUT = ("c", "xh", "y")
ROW_OUT = ("z", "xl")
BF16 = jnp.bfloat16
F32 = jnp.float32


def exchange(x, axes):
    return lax.all_to_all(x, axes, 0, 0, tiled=False)


def spread(x, n):
    return jnp.broadcast_to(x[None], (n, *x.shape))


def shift(x, axis, k):
    n = lax.axis_size(axis)
    return lax.ppermute(x, axis, [(i, (i + k) % n) for i in range(n)])


def pieces(v):
    hi = v.astype(BF16)
    rest = v - hi.astype(F32)
    mid = rest.astype(BF16)
    low = (rest - mid.astype(F32)).astype(BF16)
    return hi, mid, low


def lse(x, axis):
    peak = jnp.max(x, axis=axis)
    return peak + jnp.log(jnp.sum(jnp.exp(x - jnp.expand_dims(peak, axis)), axis=axis))


def with_scalar(part, v):
    n, b, _ = part.shape
    hi, mid, low = pieces(v)
    lane = lax.broadcasted_iota(jnp.int32, (n, b, 128), 2)
    extra = jnp.where(lane == 0, hi, jnp.where(lane == 1, mid, jnp.where(lane == 2, low, jnp.zeros_like(hi))))
    return jnp.concatenate([part, extra], axis=2)


def pick(x, k):
    return lax.dynamic_index_in_dim(x, k, 0, keepdims=False)


def body(image_emb, text_emb, logit_scale):
    n_row, n_col = lax.axis_size(ROW), lax.axis_size(COL)
    n_xl, n_z, n_y, n_xh, n_c = (lax.axis_size(a) for a in ROW + COL)
    row_index, col_index = lax.axis_index(ROW), lax.axis_index(COL)
    y, xh, c = (lax.axis_index(a) for a in COL)
    each, _, width = image_emb.shape
    factor = logit_scale[0]
    block_rows, block_cols = each * n_col, each * n_row
    total_pairs = block_rows * n_row
    images = exchange(spread(image_emb.reshape(each, width), n_col), COL_OUT).reshape(block_rows, width)
    texts = lax.all_gather(text_emb.reshape(each, width), "xl")
    texts = lax.all_gather(texts, "z").reshape(block_cols, width)
    scores = factor * lax.dot_general(images, texts, (((1,), (1,)), ((), ())), preferred_element_type=F32)
    i = lax.broadcasted_iota(jnp.int32, (block_rows, 1), 0)
    j = lax.broadcasted_iota(jnp.int32, (1, block_cols), 1)
    i_dev = (i // each) % n_y * (n_xh * n_c) + (i // (each * n_y)) % n_xh * n_c + i // (each * n_y * n_xh)
    j_dev = (j // each) % n_xl * n_z + j // (each * n_xl)
    row_ids = (each * row_index + i % each) * n_col + i_dev
    col_ids = (each * col_index + j % each) * n_row + j_dev
    eye = row_ids == col_ids
    local_row, local_col = lse(scores, 1), lse(scores, 0)
    diag = jnp.sum(jnp.where(eye, scores, 0.0))
    col_got = exchange(spread(local_col.reshape(-1, 128), n_row), ROW).reshape(n_row, -1)
    col_lse = lse(col_got, 0)
    extra = jnp.concatenate([jnp.full((64,), diag), jnp.full((64,), jnp.sum(col_lse))])
    row_pack = jnp.concatenate([local_row, extra]).reshape(-1, 128)
    row_got = exchange(spread(row_pack, n_col), COL).reshape(n_col, -1)
    row_lse = lse(row_got[:, :block_rows], 0)
    row_loss = jnp.sum(row_lse) - 2.0 * jnp.sum(row_got[:, block_rows])
    col_loss = jnp.sum(row_got[:, block_rows + 64])
    delta = factor * (
        jnp.exp(scores - row_lse[:, None]) + jnp.exp(scores - col_lse[None, :]) - 2.0 * eye.astype(F32)
    )
    delta = delta.astype(BF16)
    text_part = lax.dot_general(delta, images, (((0,), (0,)), ((), ())), preferred_element_type=F32).astype(BF16)
    text_got = exchange(with_scalar(text_part.reshape(n_row, each, width), row_loss), ROW_OUT)
    halves = delta.reshape(n_c, block_rows // n_c, block_cols)
    away = jnp.dot(pick(halves, 1 - c), texts, preferred_element_type=F32).astype(BF16)
    came = shift(away, "c", 1).reshape(n_xh, n_y, each, width)
    here = jnp.dot(pick(halves, c), texts, preferred_element_type=F32).reshape(n_xh, n_y, each, width)
    away = (pick(here, 1 - xh) + pick(came, 1 - xh).astype(F32)).astype(BF16)
    got = shift(away, "xh", 1)
    here = pick(here, xh) + pick(came, xh).astype(F32) + got.astype(F32)
    here = jnp.concatenate([here, here], axis=0)
    ahead = lax.dynamic_slice_in_dim(here, y + 2, 3, 0).astype(BF16)
    behind = lax.dynamic_slice_in_dim(here, y + 5, 2, 0).astype(BF16)
    low = shift(ahead, "y", 3).astype(F32)
    high = shift(behind, "y", 5).astype(F32)
    up = (pick(here, y + 1) + low[2] + high[1]).astype(BF16)
    down = (pick(here, y + n_y - 1) + low[0]).astype(BF16)
    left = shift(up, "y", 1)
    right = shift(down, "y", 7)
    image_grad = pick(here, y) + low[1] + high[0] + left.astype(F32) + right.astype(F32)
    text_got = text_got.astype(F32)
    text_grad = jnp.sum(text_got[:, :, :width], axis=0)
    row_total = jnp.sum(text_got[:, 0, width : width + 3])
    loss = (row_total + col_loss) / (2.0 * total_pairs)
    return loss, image_grad.reshape(each, 1, width), text_grad.reshape(each, 1, width)


def solution(mesh):
    fine = Mesh(mesh.devices.reshape(2, 12, 8, 2, 2), ROW + COL)
    placed = (P(ROW, COL, None), P(COL, ROW, None), P())
    return jax.shard_map(
        body,
        mesh=fine,
        in_specs=placed,
        out_specs=(P(), P(ROW, COL, None), P(COL, ROW, None)),
        check_vma=False,
    )
```

time: 206 us -> 154 us (0.75)
  the two profiles are of different devices: /device:TPU:4 before, /device:TPU:24 now
where the time goes in v2:
time: 154 us; the launch traced here: 153 us
  starting transfers between devices  48.7 us (32%)
  waiting for transfers between devices  43.7 us (28%)
  blocking collectives  39.1 us (25%)
  other arithmetic  7.5 us (5%)
  local copies, waits for them, and re-layouts  5.88 us (4%)
  between operations  5.28 us (3%)
  matrix products  3.08 us (2%)
    all_gather x1, blocking collectives, body(): texts = lax.all_gather(texts, 'z').reshape(block_cols, width)  34.3 us
    all_to_all x4, starting transfers between devices, exchange(): return lax.all_to_all(x, axes, 0, 0, tiled=False)  30.9 us
    ppermute x6, waiting for transfers between devices, shift(): return lax.ppermute(x, axis, [(i, (i + k) % n) for i in range(n)])  24.1 us
    all_to_all x4, waiting for transfers between devices, exchange(): return lax.all_to_all(x, axes, 0, 0, tiled=False)  19.6 us
    ppermute x6, starting transfers between devices, shift(): return lax.ppermute(x, axis, [(i, (i + k) % n) for i in range(n)])  17.9 us
    all_gather x1, blocking collectives, body(): texts = lax.all_gather(text_emb.reshape(each, width), 'xl')  4.85 us
    broadcast_in_dim x3, local copies, waits for them, and re-layouts, spread(): return jnp.broadcast_to(x[None], (n, *x.shape))  3.16 us
  transfers between devices with their start and end apart: 10, of which 6 were waited for; matrix products, arithmetic and copies ran while one was open for 3% of the time, Pallas kernels for 0%

profile of v2, /device:TPU:24, one launch (start us, length us, event | category | flops | bytes accessed | tf_op | source)
XLA Modules:
  0.0 153.3 jit_solution(9430424916731162214)
XLA Ops:
  0.6 0.0 copy-start
  0.6 1.9 %broadcast_in_dim.51 = bf16[32,16,1024]{2,1,0:T(8,128)(2,1)} broadcast(bf16[16,1024]{1,0:T(8,128)(2,1)} %bitcast.65), dimensions={1,2} | broadcast | bytes 1081344 | tf_op jit(solution)/shard_map/broadcast_in_dim | solution.py:20
  2.5 12.8 %all-to-all-start = ((bf16[32,16,1024]{2,1,0:T(8,128)(2,1)}), bf16[32,16,1024]{2,1,0:T(8,128)(2,1)S(1)}, u32[]{:S(2)}, u32[]{:S(2)}) async-start(bf16[32,16,1024]{2,1,0:T(8,128)(2,1)} %broadcast_in_dim.51), calls=%async_computation | async-start | bytes 2097152 | tf_op jit(solution)/shard_map/all_to_all | solution.py:16
  16.0 0.0 copy-done
  16.0 4.8 %all-gather = bf16[32,1,1024]{2,0,1:T(8,128)(2,1)S(1)} all-gather(bf16[16,1,1024]{2,0,1:T(8,128)(2,1)S(1)} %copy-done), channel_id=2, replica_groups=mesh['xl'=2,'z'=12,'y'=8,'xh'=2,'c'=2] {'xl'}, dimensions={0}, use_global_device_ids=true | all-gather | bytes 98304 | tf_op jit(solution)/shard_map/all_gather | solution.py:63
  20.9 34.3 %all-gather.1 = bf16[24,16,1024]{2,1,0:T(8,128)(2,1)S(1)} all-gather(bf16[2,16,1024]{2,1,0:T(8,128)(2,1)S(1)} %bitcast.64), channel_id=3, replica_groups=mesh['xl'=2,'z'=12,'y'=8,'xh'=2,'c'=2] {'z'}, dimensions={0}, use_global_device_ids=true | all-gather | bytes 851968 | tf_op jit(solution)/shard_map/all_gather | solution.py:64
  55.1 0.0 all-to-all-done
  55.2 0.8 fusion.57
  56.0 0.9 exponential_reduce_fusion.1
  56.9 0.6 broadcast_in_dim.54
  57.5 3.8 %all-to-all-start.1 = ((f32[24,3,128]{2,1,0:T(4,128)}), f32[24,3,128]{2,1,0:T(4,128)S(1)}, u32[]{:S(2)}, u32[]{:S(2)}) async-start(f32[24,3,128]{2,1,0:T(4,128)} %broadcast_in_dim.54), calls=%async_computation.1 | async-start | bytes 98304 | tf_op jit(solution)/shard_map/all_to_all | solution.py:16
  61.4 10.8 %all-to-all-done.1 = f32[24,3,128]{2,1,0:T(4,128)S(1)} async-done(((f32[24,3,128]{2,1,0:T(4,128)}), f32[24,3,128]{2,1,0:T(4,128)S(1)}, u32[]{:S(2)}, u32[]{:S(2)}) %all-to-all-start.1) | async-done | bytes 36896 | tf_op jit(solution)/shard_map/all_to_all | solution.py:16
  72.3 0.6 fusion.55
  72.9 0.6 broadcast_in_dim.53
  73.5 0.6 broadcast_in_dim.55
  74.2 0.1 maximum_bitcast_fusion
  74.3 0.6 broadcast_in_dim.57
  74.9 10.3 %all-to-all-start.2 = ((f32[32,5,128]{2,1,0:T(8,128)}), f32[32,5,128]{2,1,0:T(8,128)S(1)}, u32[]{:S(2)}, u32[]{:S(2)}) async-start(f32[32,5,128]{2,1,0:T(8,128)} %broadcast_in_dim.57), calls=%async_computation.2 | async-start | bytes 262144 | tf_op jit(solution)/shard_map/all_to_all | solution.py:16
  85.3 8.8 %all-to-all-done.2 = f32[32,5,128]{2,1,0:T(8,128)S(1)} async-done(((f32[32,5,128]{2,1,0:T(8,128)}), f32[32,5,128]{2,1,0:T(8,128)S(1)}, u32[]{:S(2)}, u32[]{:S(2)}) %all-to-all-start.2) | async-done | bytes 81952 | tf_op jit(solution)/shard_map/all_to_all | solution.py:16
  94.1 0.7 slice_reduce_fusion.2
  94.9 0.6 fusion.58
  96.8 0.3 fusion.3
  97.2 0.6 convolution_convert_fusion
  97.8 1.0 pad_maximum_fusion
  98.8 3.9 %all-to-all-start.3 = ((bf16[24,16,1152]{2,1,0:T(8,128)(2,1)}), bf16[24,16,1152]{2,1,0:T(8,128)(2,1)S(1)}, u32[]{:S(2)}, u32[]{:S(2)}) async-start(bf16[24,16,1152]{2,1,0:T(8,128)(2,1)} %pad_maximum_fusion), calls=%async_computation.3 | async-start | bytes 1769472 | tf_op jit(solution)/shard_map/all_to_all | solution.py:16
  102.7 1.2 convolution_convert_fusion.1
  104.0 1.9 %collective-permute-start = (bf16[256,1024]{1,0:T(8,128)(2,1)}, bf16[256,1024]{1,0:T(8,128)(2,1)}, u32[]{:S(2)}, u32[]{:S(2)}) collective-permute-start(bf16[256,1024]{1,0:T(8,128)(2,1)} %convolution_convert_fusion.1), channel_id=1, source_target_pairs={{0,1},{1,0},{2,3},{3,2},{4,5},{5,4},{6,7},{7,6},{8,9},{9,8},{10,11... | collective-permute-start | bytes 1572872 | tf_op jit(solution)/shard_map/ppermute | solution.py:25
  105.9 0.4 fusion.59
  106.4 1.7 %collective-permute-done = bf16[256,1024]{1,0:T(8,128)(2,1)} collective-permute-done((bf16[256,1024]{1,0:T(8,128)(2,1)}, bf16[256,1024]{1,0:T(8,128)(2,1)}, u32[]{:S(2)}, u32[]{:S(2)}) %collective-permute-start) | collective-permute-done | bytes 524320 | tf_op jit(solution)/shard_map/ppermute | solution.py:25
  108.1 1.0 fusion.4
  109.1 2.5 %collective-permute-start.1 = (bf16[8,16,1024]{2,1,0:T(8,128)(2,1)S(1)}, bf16[8,16,1024]{2,1,0:T(8,128)(2,1)S(1)}, u32[]{:S(2)}, u32[]{:S(2)}) collective-permute-start(bf16[8,16,1024]{2,1,0:T(8,128)(2,1)S(1)} %fusion.4), channel_id=1, source_target_pairs={{0,2},{2,0},{1,3},{3,1},{4,6},{6,4},{5,7},{7,5},{8,10},{10,8},{9,1... | collective-permute-start | bytes 786440 | tf_op jit(solution)/shard_map/ppermute | solution.py:25
  111.6 11.4 %collective-permute-done.1 = bf16[8,16,1024]{2,1,0:T(8,128)(2,1)S(1)} collective-permute-done((bf16[8,16,1024]{2,1,0:T(8,128)(2,1)S(1)}, bf16[8,16,1024]{2,1,0:T(8,128)(2,1)S(1)}, u32[]{:S(2)}, u32[]{:S(2)}) %collective-permute-start.1) | collective-permute-done | bytes 262176 | tf_op jit(solution)/shard_map/ppermute | solution.py:25
  123.0 1.0 bitcast_add_fusion
  124.1 3.9 %collective-permute-start.2 = (bf16[3,16,1024]{2,1,0:T(8,128)(2,1)S(1)}, bf16[3,16,1024]{2,1,0:T(8,128)(2,1)S(1)}, u32[]{:S(2)}, u32[]{:S(2)}) collective-permute-start(bf16[3,16,1024]{2,1,0:T(8,128)(2,1)S(1)} %fusion.6), channel_id=1, source_target_pairs={{0,12},{4,16},{8,20},{12,24},{16,28},{20,0},{24,4},{28,8},{1,13},{... | collective-permute-start | bytes 294920 | tf_op jit(solution)/shard_map/ppermute | solution.py:25
  128.1 3.7 %collective-permute-start.3 = (bf16[2,16,1024]{2,1,0:T(8,128)(2,1)S(1)}, bf16[2,16,1024]{2,1,0:T(8,128)(2,1)S(1)}, u32[]{:S(2)}, u32[]{:S(2)}) collective-permute-start(bf16[2,16,1024]{2,1,0:T(8,128)(2,1)S(1)} %fusion.10), channel_id=1, source_target_pairs={{0,20},{4,24},{8,28},{12,0},{16,4},{20,8},{24,12},{28,16},{1,21},{... | collective-permute-start | bytes 196616 | tf_op jit(solution)/shard_map/ppermute | solution.py:25
  131.8 6.2 %collective-permute-done.3 = bf16[2,16,1024]{2,1,0:T(8,128)(2,1)S(1)} collective-permute-done((bf16[2,16,1024]{2,1,0:T(8,128)(2,1)S(1)}, bf16[2,16,1024]{2,1,0:T(8,128)(2,1)S(1)}, u32[]{:S(2)}, u32[]{:S(2)}) %collective-permute-start.3) | collective-permute-done | bytes 65568 | tf_op jit(solution)/shard_map/ppermute | solution.py:25
  138.1 0.0 collective-permute-done.2
  138.1 1.9 %collective-permute-start.4 = (bf16[16,1024]{1,0:T(8,128)(2,1)S(1)}, bf16[16,1024]{1,0:T(8,128)(2,1)S(1)}, u32[]{:S(2)}, u32[]{:S(2)}) collective-permute-start(bf16[16,1024]{1,0:T(8,128)(2,1)S(1)} %get-tuple-element.27), channel_id=1, source_target_pairs={{0,4},{4,8},{8,12},{12,16},{16,20},{20,24},{24,28},{28,0},{1,5},{5... | collective-permute-start | bytes 98312 | tf_op jit(solution)/shard_map/ppermute | solution.py:25
  140.1 3.9 %collective-permute-start.5 = (bf16[16,1024]{1,0:T(8,128)(2,1)S(1)}, bf16[16,1024]{1,0:T(8,128)(2,1)S(1)}, u32[]{:S(2)}, u32[]{:S(2)}) collective-permute-start(bf16[16,1024]{1,0:T(8,128)(2,1)S(1)} %get-tuple-element.28), channel_id=1, source_target_pairs={{0,28},{4,0},{8,4},{12,8},{16,12},{20,16},{24,20},{28,24},{1,29},{... | collective-permute-start | bytes 98312 | tf_op jit(solution)/shard_map/ppermute | solution.py:25
  144.0 0.0 collective-permute-done.4
  144.0 4.7 %collective-permute-done.5 = bf16[16,1024]{1,0:T(8,128)(2,1)S(1)} collective-permute-done((bf16[16,1024]{1,0:T(8,128)(2,1)S(1)}, bf16[16,1024]{1,0:T(8,128)(2,1)S(1)}, u32[]{:S(2)}, u32[]{:S(2)}) %collective-permute-start.5) | collective-permute-done | bytes 32800 | tf_op jit(solution)/shard_map/ppermute | solution.py:25
  148.7 0.7 copy.12
  149.4 0.0 all-to-all-done.3
  149.4 0.1 convert_element_type.82
  149.6 0.6 slice_reduce_fusion.4
  150.2 0.1 slice_reduce_fusion
  150.3 0.7 reshape.371
  (19 shorter events, 0.4 us)
Async XLA Ops:
  0.6 15.4 %copy-start = (bf16[16,1,1024]{2,0,1:T(8,128)(2,1)S(1)}, bf16[16,1,1024]{2,0,1:T(8,128)(2,1)}, u32[]{:S(2)}) copy-start(bf16[16,1,1024]{2,0,1:T(8,128)(2,1)} %param.4) | copy-start | bytes 98308
  2.5 52.6 %all-to-all-start = ((bf16[32,16,1024]{2,1,0:T(8,128)(2,1)}), bf16[32,16,1024]{2,1,0:T(8,128)(2,1)S(1)}, u32[]{:S(2)}, u32[]{:S(2)}) async-start(bf16[32,16,1024]{2,1,0:T(8,128)(2,1)} %broadcast_in_dim.51), calls=%async_computation | async-start | bytes 2097152 | tf_op jit(solution)/shard_map/all_to_all | solution.py:16
  57.5 14.6 %all-to-all-start.1 = ((f32[24,3,128]{2,1,0:T(4,128)}), f32[24,3,128]{2,1,0:T(4,128)S(1)}, u32[]{:S(2)}, u32[]{:S(2)}) async-start(f32[24,3,128]{2,1,0:T(4,128)} %broadcast_in_dim.54), calls=%async_computation.1 | async-start | bytes 98304 | tf_op jit(solution)/shard_map/all_to_all | solution.py:16
  74.9 19.2 %all-to-all-start.2 = ((f32[32,5,128]{2,1,0:T(8,128)}), f32[32,5,128]{2,1,0:T(8,128)S(1)}, u32[]{:S(2)}, u32[]{:S(2)}) async-start(f32[32,5,128]{2,1,0:T(8,128)} %broadcast_in_dim.57), calls=%async_computation.2 | async-start | bytes 262144 | tf_op jit(solution)/shard_map/all_to_all | solution.py:16
  98.8 50.6 %all-to-all-start.3 = ((bf16[24,16,1152]{2,1,0:T(8,128)(2,1)}), bf16[24,16,1152]{2,1,0:T(8,128)(2,1)S(1)}, u32[]{:S(2)}, u32[]{:S(2)}) async-start(bf16[24,16,1152]{2,1,0:T(8,128)(2,1)} %pad_maximum_fusion), calls=%async_computation.3 | async-start | bytes 1769472 | tf_op jit(solution)/shard_map/all_to_all | solution.py:16
  104.0 4.1 %collective-permute-start = (bf16[256,1024]{1,0:T(8,128)(2,1)}, bf16[256,1024]{1,0:T(8,128)(2,1)}, u32[]{:S(2)}, u32[]{:S(2)}) collective-permute-start(bf16[256,1024]{1,0:T(8,128)(2,1)} %convolution_convert_fusion.1), channel_id=1, source_target_pairs={{0,1},{1,0},{2,3},{3,2},{4,5},{5,4},{6,7},{7,6},{8,9},{9,8},{10,11... | collective-permute-start | bytes 1572872 | tf_op jit(solution)/shard_map/ppermute | solution.py:25
  109.1 13.9 %collective-permute-start.1 = (bf16[8,16,1024]{2,1,0:T(8,128)(2,1)S(1)}, bf16[8,16,1024]{2,1,0:T(8,128)(2,1)S(1)}, u32[]{:S(2)}, u32[]{:S(2)}) collective-permute-start(bf16[8,16,1024]{2,1,0:T(8,128)(2,1)S(1)} %fusion.4), channel_id=1, source_target_pairs={{0,2},{2,0},{1,3},{3,1},{4,6},{6,4},{5,7},{7,5},{8,10},{10,8},{9,1... | collective-permute-start | bytes 786440 | tf_op jit(solution)/shard_map/ppermute | solution.py:25
  124.1 14.0 %collective-permute-start.2 = (bf16[3,16,1024]{2,1,0:T(8,128)(2,1)S(1)}, bf16[3,16,1024]{2,1,0:T(8,128)(2,1)S(1)}, u32[]{:S(2)}, u32[]{:S(2)}) collective-permute-start(bf16[3,16,1024]{2,1,0:T(8,128)(2,1)S(1)} %fusion.6), channel_id=1, source_target_pairs={{0,12},{4,16},{8,20},{12,24},{16,28},{20,0},{24,4},{28,8},{1,13},{... | collective-permute-start | bytes 294920 | tf_op jit(solution)/shard_map/ppermute | solution.py:25
  128.1 10.0 %collective-permute-start.3 = (bf16[2,16,1024]{2,1,0:T(8,128)(2,1)S(1)}, bf16[2,16,1024]{2,1,0:T(8,128)(2,1)S(1)}, u32[]{:S(2)}, u32[]{:S(2)}) collective-permute-start(bf16[2,16,1024]{2,1,0:T(8,128)(2,1)S(1)} %fusion.10), channel_id=1, source_target_pairs={{0,20},{4,24},{8,28},{12,0},{16,4},{20,8},{24,12},{28,16},{1,21},{... | collective-permute-start | bytes 196616 | tf_op jit(solution)/shard_map/ppermute | solution.py:25
  138.1 5.9 %collective-permute-start.4 = (bf16[16,1024]{1,0:T(8,128)(2,1)S(1)}, bf16[16,1024]{1,0:T(8,128)(2,1)S(1)}, u32[]{:S(2)}, u32[]{:S(2)}) collective-permute-start(bf16[16,1024]{1,0:T(8,128)(2,1)S(1)} %get-tuple-element.27), channel_id=1, source_target_pairs={{0,4},{4,8},{8,12},{12,16},{16,20},{20,24},{24,28},{28,0},{1,5},{5... | collective-permute-start | bytes 98312 | tf_op jit(solution)/shard_map/ppermute | solution.py:25
  140.1 8.6 %collective-permute-start.5 = (bf16[16,1024]{1,0:T(8,128)(2,1)S(1)}, bf16[16,1024]{1,0:T(8,128)(2,1)S(1)}, u32[]{:S(2)}, u32[]{:S(2)}) collective-permute-start(bf16[16,1024]{1,0:T(8,128)(2,1)S(1)} %get-tuple-element.28), channel_id=1, source_target_pairs={{0,28},{4,0},{8,4},{12,8},{16,12},{20,16},{24,20},{28,24},{1,29},{... | collective-permute-start | bytes 98312 | tf_op jit(solution)/shard_map/ppermute | solution.py:25

commit v3 on v2

--- a/solution.py
+++ b/solution.py
@@ -73,25 +73,28 @@
     local_row, local_col = lse(scores, 1), lse(scores, 0)
     diag = jnp.sum(jnp.where(eye, scores, 0.0))
     col_got = exchange(spread(local_col.reshape(-1, 128), n_row), ROW).reshape(n_row, -1)
+    row_pack = jnp.concatenate([local_row, jnp.full((128,), diag)]).reshape(-1, 128)
+    row_got = lax.all_gather(row_pack, ("xh", "c")).reshape(n_xh * n_c, -1)
+    near_row, near_diag = lse(row_got[:, :block_rows], 0), jnp.sum(row_got[:, block_rows])
     col_lse = lse(col_got, 0)
-    extra = jnp.concatenate([jnp.full((64,), diag), jnp.full((64,), jnp.sum(col_lse))])
-    row_pack = jnp.concatenate([local_row, extra]).reshape(-1, 128)
-    row_got = exchange(spread(row_pack, n_col), COL).reshape(n_col, -1)
+    extra = jnp.concatenate([jnp.full((64,), near_diag), jnp.full((64,), jnp.sum(col_lse))])
+    row_pack = jnp.concatenate([near_row, extra]).reshape(-1, 128)
+    row_got = exchange(spread(row_pack, n_y), "y").reshape(n_y, -1)
     row_lse = lse(row_got[:, :block_rows], 0)
     row_loss = jnp.sum(row_lse) - 2.0 * jnp.sum(row_got[:, block_rows])
-    col_loss = jnp.sum(row_got[:, block_rows + 64])
+    col_loss = jnp.full((8, 128), jnp.sum(row_got[:, block_rows + 64]))
     delta = factor * (
         jnp.exp(scores - row_lse[:, None]) + jnp.exp(scores - col_lse[None, :]) - 2.0 * eye.astype(F32)
     )
     delta = delta.astype(BF16)
-    text_part = lax.dot_general(delta, images, (((0,), (0,)), ((), ())), preferred_element_type=F32).astype(BF16)
-    text_got = exchange(with_scalar(text_part.reshape(n_row, each, width), row_loss), ROW_OUT)
     halves = delta.reshape(n_c, block_rows // n_c, block_cols)
     away = jnp.dot(pick(halves, 1 - c), texts, preferred_element_type=F32).astype(BF16)
     came = shift(away, "c", 1).reshape(n_xh, n_y, each, width)
     here = jnp.dot(pick(halves, c), texts, preferred_element_type=F32).reshape(n_xh, n_y, each, width)
     away = (pick(here, 1 - xh) + pick(came, 1 - xh).astype(F32)).astype(BF16)
     got = shift(away, "xh", 1)
+    text_part = lax.dot_general(delta, images, (((0,), (0,)), ((), ())), preferred_element_type=F32).astype(BF16)
+    text_got = exchange(with_scalar(text_part.reshape(n_row, each, width), row_loss), ROW_OUT)
     here = pick(here, xh) + pick(came, xh).astype(F32) + got.astype(F32)
     here = jnp.concatenate([here, here], axis=0)
     ahead = lax.dynamic_slice_in_dim(here, y + 2, 3, 0).astype(BF16)
@@ -102,11 +105,13 @@
     down = (pick(here, y + n_y - 1) + low[0]).astype(BF16)
     left = shift(up, "y", 1)
     right = shift(down, "y", 7)
+    col_loss = col_loss + shift(col_loss, "c", 1)
+    col_loss = col_loss + shift(col_loss, "xh", 1)
     image_grad = pick(here, y) + low[1] + high[0] + left.astype(F32) + right.astype(F32)
     text_got = text_got.astype(F32)
     text_grad = jnp.sum(text_got[:, :, :width], axis=0)
     row_total = jnp.sum(text_got[:, 0, width : width + 3])
-    loss = (row_total + col_loss) / (2.0 * total_pairs)
+    loss = (row_total + col_loss[0, 0]) / (2.0 * total_pairs)
     return loss, image_grad.reshape(each, 1, width), text_grad.reshape(each, 1, width)
 
 

time: 154 us -> 161 us (1.045)
  the two profiles are of different devices: /device:TPU:24 before, /device:TPU:30 now
where the time goes in v3:
time: 161 us; the launch traced here: 160 us
  starting transfers between devices  52.3 us (32%)
  blocking collectives  48.6 us (30%)
  waiting for transfers between devices  33.5 us (21%)
  other arithmetic  9.51 us (6%)
  local copies, waits for them, and re-layouts  7.65 us (5%)
  between operations  5.31 us (3%)
  matrix products  3.09 us (2%)
    all_gather x1, blocking collectives, body(): texts = lax.all_gather(texts, 'z').reshape(block_cols, width)  34.4 us
    all_to_all x4, starting transfers between devices, exchange(): return lax.all_to_all(x, axes, 0, 0, tiled=False)  27.1 us
    ppermute x8, starting transfers between devices, shift(): return lax.ppermute(x, axis, [(i, (i + k) % n) for i in range(n)])  25.1 us
    ppermute x8, waiting for transfers between devices, shift(): return lax.ppermute(x, axis, [(i, (i + k) % n) for i in range(n)])  19.3 us
    all_to_all x4, waiting for transfers between devices, exchange(): return lax.all_to_all(x, axes, 0, 0, tiled=False)  14.3 us
    all_gather x1, blocking collectives, body(): texts = lax.all_gather(text_emb.reshape(each, width), 'xl')  7.47 us
    all_gather x1, blocking collectives, body(): row_got = lax.all_gather(row_pack, ('xh', 'c')).reshape(n_xh * n_c, -1)  6.71 us
  transfers between devices with their start and end apart: 12, of which 6 were waited for; matrix products, arithmetic and copies ran while one was open for 5% of the time, Pallas kernels for 0%

profile of v3, /device:TPU:30, one launch (start us, length us, event | category | flops | bytes accessed | tf_op | source)
XLA Modules:
  0.0 159.9 jit_solution(2102476272094687616)
XLA Ops:
  0.6 0.0 copy-start
  0.6 1.9 %broadcast_in_dim.56 = bf16[32,16,1024]{2,1,0:T(8,128)(2,1)} broadcast(bf16[16,1024]{1,0:T(8,128)(2,1)} %bitcast.76), dimensions={1,2} | broadcast | bytes 1081344 | tf_op jit(solution)/shard_map/broadcast_in_dim | solution.py:20
  2.5 9.9 %all-to-all-start = ((bf16[32,16,1024]{2,1,0:T(8,128)(2,1)}), bf16[32,16,1024]{2,1,0:T(8,128)(2,1)S(1)}, u32[]{:S(2)}, u32[]{:S(2)}) async-start(bf16[32,16,1024]{2,1,0:T(8,128)(2,1)} %broadcast_in_dim.56), calls=%async_computation | async-start | bytes 2097152 | tf_op jit(solution)/shard_map/all_to_all | solution.py:16
  13.1 0.0 copy-done
  13.1 7.5 %all-gather = bf16[32,1,1024]{2,0,1:T(8,128)(2,1)S(1)} all-gather(bf16[16,1,1024]{2,0,1:T(8,128)(2,1)S(1)} %copy-done), channel_id=2, replica_groups=mesh['xl'=2,'z'=12,'y'=8,'xh'=2,'c'=2] {'xl'}, dimensions={0}, use_global_device_ids=true | all-gather | bytes 98304 | tf_op jit(solution)/shard_map/all_gather | solution.py:63
  20.6 34.4 %all-gather.1 = bf16[24,16,1024]{2,1,0:T(8,128)(2,1)S(1)} all-gather(bf16[2,16,1024]{2,1,0:T(8,128)(2,1)S(1)} %bitcast.67), channel_id=3, replica_groups=mesh['xl'=2,'z'=12,'y'=8,'xh'=2,'c'=2] {'z'}, dimensions={0}, use_global_device_ids=true | all-gather | bytes 851968 | tf_op jit(solution)/shard_map/all_gather | solution.py:64
  55.0 0.0 all-to-all-done
  55.0 0.8 fusion.57
  55.8 0.9 fusion
  56.8 0.7 pad_bitcast_fusion
  57.4 6.7 %all_gather.15 = f32[4,5,128]{2,1,0:T(8,128)S(1)} all-gather(f32[1,5,128]{2,1,0:T(8,128)S(1)} %pad_bitcast_fusion), channel_id=1, replica_groups=mesh['xl'=2,'z'=12,'y'=8,'xh'=2,'c'=2] {'xh','c'}, dimensions={0}, use_global_device_ids=true | all-gather | bytes 12800 | tf_op jit(solution)/shard_map/all_gather | solution.py:77
  64.2 0.6 broadcast_in_dim.59
  64.8 4.9 %all-to-all-start.1 = ((f32[24,3,128]{2,1,0:T(4,128)}), f32[24,3,128]{2,1,0:T(4,128)S(1)}, u32[]{:S(2)}, u32[]{:S(2)}) async-start(f32[24,3,128]{2,1,0:T(4,128)} %broadcast_in_dim.59), calls=%async_computation.1 | async-start | bytes 98304 | tf_op jit(solution)/shard_map/all_to_all | solution.py:16
  69.7 0.6 slice_reduce_fusion.6
  70.3 9.5 %all-to-all-done.1 = f32[24,3,128]{2,1,0:T(4,128)S(1)} async-done(((f32[24,3,128]{2,1,0:T(4,128)}), f32[24,3,128]{2,1,0:T(4,128)S(1)}, u32[]{:S(2)}, u32[]{:S(2)}) %all-to-all-start.1) | async-done | bytes 36896 | tf_op jit(solution)/shard_map/all_to_all | solution.py:16
  79.9 0.6 fusion.55
  80.5 0.6 broadcast_in_dim.58
  81.1 0.6 broadcast_in_dim.60
  81.8 0.1 maximum_bitcast_fusion
  81.9 0.6 broadcast_in_dim.62
  82.5 7.4 %all-to-all-start.2 = ((f32[8,5,128]{2,1,0:T(8,128)}), f32[8,5,128]{2,1,0:T(8,128)S(1)}, u32[]{:S(2)}, u32[]{:S(2)}) async-start(f32[8,5,128]{2,1,0:T(8,128)} %broadcast_in_dim.62), calls=%async_computation.2 | async-start | bytes 65536 | tf_op jit(solution)/shard_map/all_to_all | solution.py:16
  89.9 4.7 %all-to-all-done.2 = f32[8,5,128]{2,1,0:T(8,128)S(1)} async-done(((f32[8,5,128]{2,1,0:T(8,128)}), f32[8,5,128]{2,1,0:T(8,128)S(1)}, u32[]{:S(2)}, u32[]{:S(2)}) %all-to-all-start.2) | async-done | bytes 20512 | tf_op jit(solution)/shard_map/all_to_all | solution.py:16
  94.7 0.8 slice_reduce_fusion.4
  95.5 0.6 fusion.58
  97.5 0.3 fusion.3
  97.8 0.6 convolution_convert_fusion
  98.5 1.0 pad_maximum_fusion
  99.5 4.9 %all-to-all-start.3 = ((bf16[24,16,1152]{2,1,0:T(8,128)(2,1)}), bf16[24,16,1152]{2,1,0:T(8,128)(2,1)S(1)}, u32[]{:S(2)}, u32[]{:S(2)}) async-start(bf16[24,16,1152]{2,1,0:T(8,128)(2,1)} %pad_maximum_fusion), calls=%async_computation.3 | async-start | bytes 1769472 | tf_op jit(solution)/shard_map/all_to_all | solution.py:16
  104.4 1.2 convolution_convert_fusion.1
  105.6 1.9 %collective-permute-start.2 = (bf16[256,1024]{1,0:T(8,128)(2,1)}, bf16[256,1024]{1,0:T(8,128)(2,1)}, u32[]{:S(2)}, u32[]{:S(2)}) collective-permute-start(bf16[256,1024]{1,0:T(8,128)(2,1)} %convolution_convert_fusion.1), channel_id=1, source_target_pairs={{0,1},{1,0},{2,3},{3,2},{4,5},{5,4},{6,7},{7,6},{8,9},{9,8},{10,11... | collective-permute-start | bytes 1572872 | tf_op jit(solution)/shard_map/ppermute | solution.py:25
  107.6 0.4 fusion.59
  108.0 1.7 %collective-permute-done.2 = bf16[256,1024]{1,0:T(8,128)(2,1)} collective-permute-done((bf16[256,1024]{1,0:T(8,128)(2,1)}, bf16[256,1024]{1,0:T(8,128)(2,1)}, u32[]{:S(2)}, u32[]{:S(2)}) %collective-permute-start.2) | collective-permute-done | bytes 524320 | tf_op jit(solution)/shard_map/ppermute | solution.py:25
  109.8 1.0 fusion.4
  110.8 2.6 %collective-permute-start.3 = (bf16[8,16,1024]{2,1,0:T(8,128)(2,1)S(1)}, bf16[8,16,1024]{2,1,0:T(8,128)(2,1)S(1)}, u32[]{:S(2)}, u32[]{:S(2)}) collective-permute-start(bf16[8,16,1024]{2,1,0:T(8,128)(2,1)S(1)} %fusion.4), channel_id=1, source_target_pairs={{0,2},{2,0},{1,3},{3,1},{4,6},{6,4},{5,7},{7,5},{8,10},{10,8},{9,1... | collective-permute-start | bytes 786440 | tf_op jit(solution)/shard_map/ppermute | solution.py:25
  113.4 0.6 broadcast_in_dim.67
  114.1 1.9 %collective-permute-start = (f32[8,128]{1,0:T(8,128)S(1)}, f32[8,128]{1,0:T(8,128)S(1)}, u32[]{:S(2)}, u32[]{:S(2)}) collective-permute-start(f32[8,128]{1,0:T(8,128)S(1)} %broadcast_in_dim.67), channel_id=1, source_target_pairs={{0,1},{1,0},{2,3},{3,2},{4,5},{5,4},{6,7},{7,6},{8,9},{9,8},{10,11... | collective-permute-start | bytes 12296 | tf_op jit(solution)/shard_map/ppermute | solution.py:25
  116.0 10.0 %collective-permute-done.3 = bf16[8,16,1024]{2,1,0:T(8,128)(2,1)S(1)} collective-permute-done((bf16[8,16,1024]{2,1,0:T(8,128)(2,1)S(1)}, bf16[8,16,1024]{2,1,0:T(8,128)(2,1)S(1)}, u32[]{:S(2)}, u32[]{:S(2)}) %collective-permute-start.3) | collective-permute-done | bytes 262176 | tf_op jit(solution)/shard_map/ppermute | solution.py:25
  126.0 1.0 bitcast_add_fusion
  127.0 5.2 %collective-permute-start.5 = (bf16[2,16,1024]{2,1,0:T(8,128)(2,1)S(1)}, bf16[2,16,1024]{2,1,0:T(8,128)(2,1)S(1)}, u32[]{:S(2)}, u32[]{:S(2)}) collective-permute-start(bf16[2,16,1024]{2,1,0:T(8,128)(2,1)S(1)} %fusion.10), channel_id=1, source_target_pairs={{0,20},{4,24},{8,28},{12,0},{16,4},{20,8},{24,12},{28,16},{1,21},{... | collective-permute-start | bytes 196616 | tf_op jit(solution)/shard_map/ppermute | solution.py:25
  132.3 3.7 %collective-permute-start.4 = (bf16[3,16,1024]{2,1,0:T(8,128)(2,1)S(1)}, bf16[3,16,1024]{2,1,0:T(8,128)(2,1)S(1)}, u32[]{:S(2)}, u32[]{:S(2)}) collective-permute-start(bf16[3,16,1024]{2,1,0:T(8,128)(2,1)S(1)} %fusion.6), channel_id=1, source_target_pairs={{0,12},{4,16},{8,20},{12,24},{16,28},{20,0},{24,4},{28,8},{1,13},{... | collective-permute-start | bytes 294920 | tf_op jit(solution)/shard_map/ppermute | solution.py:25
  136.0 0.0 collective-permute-done
  136.0 0.7 broadcast_add_fusion
  136.6 2.2 %collective-permute-start.1 = (f32[8,128]{1,0:T(8,128)S(1)}, f32[8,128]{1,0:T(8,128)S(1)}, u32[]{:S(2)}, u32[]{:S(2)}) collective-permute-start(f32[8,128]{1,0:T(8,128)S(1)} %broadcast_add_fusion), channel_id=1, source_target_pairs={{0,2},{2,0},{1,3},{3,1},{4,6},{6,4},{5,7},{7,5},{8,10},{10,8},{9,1... | collective-permute-start | bytes 12296 | tf_op jit(solution)/shard_map/ppermute | solution.py:25
  138.9 0.0 collective-permute-done.5
  138.9 3.6 %collective-permute-done.4 = bf16[3,16,1024]{2,1,0:T(8,128)(2,1)S(1)} collective-permute-done((bf16[3,16,1024]{2,1,0:T(8,128)(2,1)S(1)}, bf16[3,16,1024]{2,1,0:T(8,128)(2,1)S(1)}, u32[]{:S(2)}, u32[]{:S(2)}) %collective-permute-start.4) | collective-permute-done | bytes 98336 | tf_op jit(solution)/shard_map/ppermute | solution.py:25
  142.6 5.7 %collective-permute-start.6 = (bf16[16,1024]{1,0:T(8,128)(2,1)S(1)}, bf16[16,1024]{1,0:T(8,128)(2,1)S(1)}, u32[]{:S(2)}, u32[]{:S(2)}) collective-permute-start(bf16[16,1024]{1,0:T(8,128)(2,1)S(1)} %get-tuple-element.27), channel_id=1, source_target_pairs={{0,4},{4,8},{8,12},{12,16},{16,20},{20,24},{24,28},{28,0},{1,5},{5... | collective-permute-start | bytes 98312 | tf_op jit(solution)/shard_map/ppermute | solution.py:25
  148.3 1.9 %collective-permute-start.7 = (bf16[16,1024]{1,0:T(8,128)(2,1)S(1)}, bf16[16,1024]{1,0:T(8,128)(2,1)S(1)}, u32[]{:S(2)}, u32[]{:S(2)}) collective-permute-start(bf16[16,1024]{1,0:T(8,128)(2,1)S(1)} %get-tuple-element.28), channel_id=1, source_target_pairs={{0,28},{4,0},{8,4},{12,8},{16,12},{20,16},{24,20},{28,24},{1,29},{... | collective-permute-start | bytes 98312 | tf_op jit(solution)/shard_map/ppermute | solution.py:25
  150.2 0.0 collective-permute-done.1
  150.3 0.7 fusion.67
  150.9 0.5 slice.45
  151.4 0.0 collective-permute-done.6
  151.4 3.9 %collective-permute-done.7 = bf16[16,1024]{1,0:T(8,128)(2,1)S(1)} collective-permute-done((bf16[16,1024]{1,0:T(8,128)(2,1)S(1)}, bf16[16,1024]{1,0:T(8,128)(2,1)S(1)}, u32[]{:S(2)}, u32[]{:S(2)}) %collective-permute-start.7) | collective-permute-done | bytes 32800 | tf_op jit(solution)/shard_map/ppermute | solution.py:25
  155.4 0.7 copy.12
  156.1 0.0 all-to-all-done.3
  156.1 0.1 convert_element_type.82
  156.2 0.6 slice_reduce_fusion.2
  156.8 0.1 slice_reduce_fusion
  156.9 0.7 reshape.376
  (23 shorter events, 0.4 us)
Async XLA Ops:
  0.6 12.5 %copy-start = (bf16[16,1,1024]{2,0,1:T(8,128)(2,1)S(1)}, bf16[16,1,1024]{2,0,1:T(8,128)(2,1)}, u32[]{:S(2)}) copy-start(bf16[16,1,1024]{2,0,1:T(8,128)(2,1)} %param.4) | copy-start | bytes 98308
  2.5 52.5 %all-to-all-start = ((bf16[32,16,1024]{2,1,0:T(8,128)(2,1)}), bf16[32,16,1024]{2,1,0:T(8,128)(2,1)S(1)}, u32[]{:S(2)}, u32[]{:S(2)}) async-start(bf16[32,16,1024]{2,1,0:T(8,128)(2,1)} %broadcast_in_dim.56), calls=%async_computation | async-start | bytes 2097152 | tf_op jit(solution)/shard_map/all_to_all | solution.py:16
  64.8 15.0 %all-to-all-start.1 = ((f32[24,3,128]{2,1,0:T(4,128)}), f32[24,3,128]{2,1,0:T(4,128)S(1)}, u32[]{:S(2)}, u32[]{:S(2)}) async-start(f32[24,3,128]{2,1,0:T(4,128)} %broadcast_in_dim.59), calls=%async_computation.1 | async-start | bytes 98304 | tf_op jit(solution)/shard_map/all_to_all | solution.py:16
  82.5 12.2 %all-to-all-start.2 = ((f32[8,5,128]{2,1,0:T(8,128)}), f32[8,5,128]{2,1,0:T(8,128)S(1)}, u32[]{:S(2)}, u32[]{:S(2)}) async-start(f32[8,5,128]{2,1,0:T(8,128)} %broadcast_in_dim.62), calls=%async_computation.2 | async-start | bytes 65536 | tf_op jit(solution)/shard_map/all_to_all | solution.py:16
  99.5 56.6 %all-to-all-start.3 = ((bf16[24,16,1152]{2,1,0:T(8,128)(2,1)}), bf16[24,16,1152]{2,1,0:T(8,128)(2,1)S(1)}, u32[]{:S(2)}, u32[]{:S(2)}) async-start(bf16[24,16,1152]{2,1,0:T(8,128)(2,1)} %pad_maximum_fusion), calls=%async_computation.3 | async-start | bytes 1769472 | tf_op jit(solution)/shard_map/all_to_all | solution.py:16
  105.6 4.1 %collective-permute-start.2 = (bf16[256,1024]{1,0:T(8,128)(2,1)}, bf16[256,1024]{1,0:T(8,128)(2,1)}, u32[]{:S(2)}, u32[]{:S(2)}) collective-permute-start(bf16[256,1024]{1,0:T(8,128)(2,1)} %convolution_convert_fusion.1), channel_id=1, source_target_pairs={{0,1},{1,0},{2,3},{3,2},{4,5},{5,4},{6,7},{7,6},{8,9},{9,8},{10,11... | collective-permute-start | bytes 1572872 | tf_op jit(solution)/shard_map/ppermute | solution.py:25
  110.8 15.2 %collective-permute-start.3 = (bf16[8,16,1024]{2,1,0:T(8,128)(2,1)S(1)}, bf16[8,16,1024]{2,1,0:T(8,128)(2,1)S(1)}, u32[]{:S(2)}, u32[]{:S(2)}) collective-permute-start(bf16[8,16,1024]{2,1,0:T(8,128)(2,1)S(1)} %fusion.4), channel_id=1, source_target_pairs={{0,2},{2,0},{1,3},{3,1},{4,6},{6,4},{5,7},{7,5},{8,10},{10,8},{9,1... | collective-permute-start | bytes 786440 | tf_op jit(solution)/shard_map/ppermute | solution.py:25
  114.1 21.9 %collective-permute-start = (f32[8,128]{1,0:T(8,128)S(1)}, f32[8,128]{1,0:T(8,128)S(1)}, u32[]{:S(2)}, u32[]{:S(2)}) collective-permute-start(f32[8,128]{1,0:T(8,128)S(1)} %broadcast_in_dim.67), channel_id=1, source_target_pairs={{0,1},{1,0},{2,3},{3,2},{4,5},{5,4},{6,7},{7,6},{8,9},{9,8},{10,11... | collective-permute-start | bytes 12296 | tf_op jit(solution)/shard_map/ppermute | solution.py:25
  127.0 11.8 %collective-permute-start.5 = (bf16[2,16,1024]{2,1,0:T(8,128)(2,1)S(1)}, bf16[2,16,1024]{2,1,0:T(8,128)(2,1)S(1)}, u32[]{:S(2)}, u32[]{:S(2)}) collective-permute-start(bf16[2,16,1024]{2,1,0:T(8,128)(2,1)S(1)} %fusion.10), channel_id=1, source_target_pairs={{0,20},{4,24},{8,28},{12,0},{16,4},{20,8},{24,12},{28,16},{1,21},{... | collective-permute-start | bytes 196616 | tf_op jit(solution)/shard_map/ppermute | solution.py:25
  132.3 10.3 %collective-permute-start.4 = (bf16[3,16,1024]{2,1,0:T(8,128)(2,1)S(1)}, bf16[3,16,1024]{2,1,0:T(8,128)(2,1)S(1)}, u32[]{:S(2)}, u32[]{:S(2)}) collective-permute-start(bf16[3,16,1024]{2,1,0:T(8,128)(2,1)S(1)} %fusion.6), channel_id=1, source_target_pairs={{0,12},{4,16},{8,20},{12,24},{16,28},{20,0},{24,4},{28,8},{1,13},{... | collective-permute-start | bytes 294920 | tf_op jit(solution)/shard_map/ppermute | solution.py:25
  136.6 13.6 %collective-permute-start.1 = (f32[8,128]{1,0:T(8,128)S(1)}, f32[8,128]{1,0:T(8,128)S(1)}, u32[]{:S(2)}, u32[]{:S(2)}) collective-permute-start(f32[8,128]{1,0:T(8,128)S(1)} %broadcast_add_fusion), channel_id=1, source_target_pairs={{0,2},{2,0},{1,3},{3,1},{4,6},{6,4},{5,7},{7,5},{8,10},{10,8},{9,1... | collective-permute-start | bytes 12296 | tf_op jit(solution)/shard_map/ppermute | solution.py:25
  142.6 8.8 %collective-permute-start.6 = (bf16[16,1024]{1,0:T(8,128)(2,1)S(1)}, bf16[16,1024]{1,0:T(8,128)(2,1)S(1)}, u32[]{:S(2)}, u32[]{:S(2)}) collective-permute-start(bf16[16,1024]{1,0:T(8,128)(2,1)S(1)} %get-tuple-element.27), channel_id=1, source_target_pairs={{0,4},{4,8},{8,12},{12,16},{16,20},{20,24},{24,28},{28,0},{1,5},{5... | collective-permute-start | bytes 98312 | tf_op jit(solution)/shard_map/ppermute | solution.py:25
  148.3 7.0 %collective-permute-start.7 = (bf16[16,1024]{1,0:T(8,128)(2,1)S(1)}, bf16[16,1024]{1,0:T(8,128)(2,1)S(1)}, u32[]{:S(2)}, u32[]{:S(2)}) collective-permute-start(bf16[16,1024]{1,0:T(8,128)(2,1)S(1)} %get-tuple-element.28), channel_id=1, source_target_pairs={{0,28},{4,0},{8,4},{12,8},{16,12},{20,16},{24,20},{28,24},{1,29},{... | collective-permute-start | bytes 98312 | tf_op jit(solution)/shard_map/ppermute | solution.py:25

commit v4 on v0

v4 whole, which is shorter than its diff:
```python
import functools

import jax
import jax.numpy as jnp
from jax import lax
from jax.experimental import pallas as pl
from jax.experimental.pallas import tpu as pltpu
from jax.sharding import Mesh, PartitionSpec as P


COL = ("y", "xh", "c")
ROW = ("xl", "z")
N_XL, N_Z, N_Y, N_XH, N_C = 2, 12, 8, 2, 2
N_ROW, N_COL = N_XL * N_Z, N_Y * N_XH * N_C
EACH = 16
WIDTH = 1024
ROWS, COLS = EACH * N_COL, EACH * N_ROW
PAIRS = ROWS * N_ROW
LANES = 128
TAIL = 8
BF16 = jnp.bfloat16
F32 = jnp.float32
VMEM = pl.BlockSpec(memory_space=pltpu.VMEM)
SMEM = pl.BlockSpec(memory_space=pltpu.SMEM)


def exchange(x, axes):
    return lax.all_to_all(x, axes, 0, 0, tiled=False)


def shift(x, axis, k):
    n = lax.axis_size(axis)
    return lax.ppermute(x, axis, [(i, (i + k) % n) for i in range(n)])


def call(kernel, outs, scratch, *args):
    in_specs = [SMEM if a.ndim == 1 else VMEM for a in args]
    return pl.pallas_call(
        kernel,
        out_shape=[jax.ShapeDtypeStruct(s, d) for s, d in outs],
        in_specs=in_specs,
        out_specs=[VMEM] * len(outs),
        scratch_shapes=[pltpu.VMEM(s, d) for s, d in scratch],
        compiler_params=pltpu.CompilerParams(vmem_limit_bytes=24 << 20),
    )(*args)


def lanes(shape):
    return lax.broadcasted_iota(jnp.int32, shape, 1)


def merged(parts):
    peak = functools.reduce(jnp.maximum, parts)
    return peak + jnp.log(sum(jnp.exp(p - peak) for p in parts))


def pieces(v):
    v = jnp.broadcast_to(v, (TAIL, LANES))
    hi = v.astype(BF16).astype(F32)
    mid = (v - hi).astype(BF16).astype(F32)
    low = v - hi - mid
    at = lanes((TAIL, LANES))
    return jnp.where(at == 0, hi, jnp.where(at == 1, mid, jnp.where(at == 2, low, 0.0))).astype(BF16)


def value(tile):
    row = tile.astype(F32)[0:1]
    return jnp.sum(jnp.where(lanes((1, LANES)) < 3, row, 0.0))


def put_tail(ref, at, v):
    ref[at : at + TAIL, :] = jnp.zeros((TAIL, WIDTH), BF16)
    ref[at : at + TAIL, 0:LANES] = pieces(v)


def diagonal(idx, start, count):
    i = lax.broadcasted_iota(jnp.int32, (count, COLS), 0) + start
    j = lax.broadcasted_iota(jnp.int32, (count, COLS), 1)
    i_dev = ((i >> 4) & 7) * (N_XH * N_C) + ((i >> 7) & 1) * N_C + (i >> 8)
    j_dev = ((j >> 4) & 1) * N_Z + (j >> 5)
    row_ids = (EACH * idx[0] + (i & 15)) * N_COL + i_dev
    col_ids = (EACH * idx[1] + (j & 15)) * N_ROW + j_dev
    return row_ids == col_ids


def score_kernel(idx, fac, im, tx, sc, cpack, rpack):
    s = fac[0] * lax.dot_general(im[...], tx[...], (((1,), (1,)), ((), ())), preferred_element_type=F32)
    sc[...] = s
    peak = jnp.max(s, axis=0, keepdims=True)
    col = peak + jnp.log(jnp.sum(jnp.exp(s - peak), axis=0, keepdims=True))
    for k in range(COLS // LANES):
        tile = jnp.broadcast_to(col[:, k * LANES : (k + 1) * LANES], (N_ROW, LANES))
        for n in range(N_ROW):
            cpack[n, k : k + 1, :] = tile[n : n + 1]
    peak = jnp.max(s, axis=1, keepdims=True)
    row = peak + jnp.log(jnp.sum(jnp.exp(s - peak), axis=1, keepdims=True))
    for k in range(ROWS // LANES):
        tile = jnp.broadcast_to(row[k * LANES : (k + 1) * LANES], (LANES, LANES))
        rpack[k : k + 1, :] = tile.T[0:1]
    diag = jnp.sum(jnp.where(diagonal(idx, 0, ROWS), s, 0.0))
    rpack[4:5, :] = jnp.full((1, LANES), diag)


def merge_kernel(col, near, clse, pack):
    lse = merged([col[n] for n in range(N_ROW)])
    total = jnp.zeros((1, LANES), F32)
    for k in range(COLS // LANES):
        clse[:, k * LANES : (k + 1) * LANES] = jnp.broadcast_to(lse[k : k + 1], (8, LANES))
        total = total + lse[k : k + 1]
    total = jnp.full((1, LANES), jnp.sum(total))
    rows = merged([near[n] for n in range(N_XH * N_C)])
    diag = sum(near[n, 4:5, :] for n in range(N_XH * N_C))
    for n in range(N_Y):
        pack[n, 0:4, :] = rows[0:4]
        pack[n, 4:5, :] = diag
        pack[n, 5:6, :] = total


def grad_kernel(idx, fac, sc, im, tx, got, clse, iaway, ihere, taway, there, scal, delta, part):
    rows = merged([got[n] for n in range(N_Y)])[0:4]
    diag = sum(got[n, 4:5, :] for n in range(N_Y))
    total = sum(got[n, 5:6, :] for n in range(N_Y))
    row_loss = jnp.full((1, LANES), jnp.sum(rows)) - 2.0 * diag
    scal[0:8, :] = jnp.broadcast_to(row_loss, (8, LANES))
    scal[8:16, :] = jnp.broadcast_to(total, (8, LANES))
    c, xl = idx[2], idx[5]
    col = clse[0:1, :]
    for k in range(ROWS // LANES):
        s = sc[k * LANES : (k + 1) * LANES, :]
        tile = jnp.broadcast_to(rows[k : k + 1], (LANES, LANES)).T
        lse = jnp.concatenate([tile] * (COLS // LANES), axis=1)
        eye = diagonal(idx, k * LANES, LANES)
        d = jnp.exp(s - lse) + jnp.exp(s - col) - jnp.where(eye, 2.0, 0.0)
        delta[k // 2, (k % 2) * LANES : (k % 2 + 1) * LANES, :] = (fac[0] * d).astype(BF16)
    iaway[0 : ROWS // 2, :] = jnp.dot(delta[1 - c], tx[...], preferred_element_type=F32).astype(BF16)
    put_tail(iaway, ROWS // 2, total)
    whole = delta[...].reshape(ROWS, COLS)
    part[...] = lax.dot_general(
        whole, im[...], (((0,), (0,)), ((), ())), preferred_element_type=F32
    ).reshape(N_Z, N_XL, EACH, WIDTH)
    for z in range(N_Z):
        taway[z * EACH : (z + 1) * EACH, :] = part[z, 1 - xl].astype(BF16)
        there[z * EACH : (z + 1) * EACH, :] = part[z, xl]
    put_tail(taway, COLS // 2, row_loss)
    ihere[...] = jnp.dot(delta[c], tx[...], preferred_element_type=F32)


def across_kernel(idx, scal, here, came, away, keep, out):
    half = ROWS // 4
    xh = idx[3]
    go = pl.multiple_of((1 - xh) * half, half)
    stay = pl.multiple_of(xh * half, half)
    total = scal[8:16, :] + value(came[ROWS // 2 : ROWS // 2 + TAIL, 0:LANES])
    out[...] = total
    away[0:half, :] = (here[pl.ds(go, half), :] + came[pl.ds(go, half), :].astype(F32)).astype(BF16)
    put_tail(away, half, total[0:1])
    keep[...] = here[pl.ds(stay, half), :] + came[pl.ds(stay, half), :].astype(F32)


def text_kernel(scal, here, came, out):
    half = COLS // 2
    loss = scal[0:8, :] + value(came[half : half + TAIL, 0:LANES])
    both = (here[...] + came[0:half, :].astype(F32)).astype(BF16)
    out[:, :, 0:WIDTH] = both.reshape(N_Z, EACH, WIDTH)
    tile = pieces(loss[0:1])
    for z in range(N_Z):
        out[z, 0:8, WIDTH:] = tile
        out[z, 8:16, WIDTH:] = jnp.zeros((8, LANES), BF16)


def ring_kernel(idx, total, keep, got, ahead, behind, near, out):
    y = idx[4]
    half = ROWS // 4
    out[...] = total[...] + value(got[half : half + TAIL, 0:LANES])

    def block(k):
        at = pl.multiple_of(((y + k) & (N_Y - 1)) * EACH, EACH)
        return keep[pl.ds(at, EACH), :] + got[pl.ds(at, EACH), :].astype(F32)

    for n, k in enumerate((2, 3, 4)):
        ahead[n * EACH : (n + 1) * EACH, :] = block(k).astype(BF16)
    for n, k in enumerate((5, 6)):
        behind[n * EACH : (n + 1) * EACH, :] = block(k).astype(BF16)
    for n, k in enumerate((7, 0, 1)):
        near[n * EACH : (n + 1) * EACH, :] = block(k)


def side_kernel(near, low, high, up, down, mid):
    e = EACH
    down[...] = (near[0:e, :] + low[0:e, :].astype(F32)).astype(BF16)
    mid[...] = near[e : 2 * e, :] + low[e : 2 * e, :].astype(F32) + high[0:e, :].astype(F32)
    up[...] = (near[2 * e :, :] + low[2 * e :, :].astype(F32) + high[e:, :].astype(F32)).astype(BF16)


def image_kernel(mid, left, right, out):
    out[...] = (mid[...] + left[...].astype(F32) + right[...].astype(F32)).reshape(EACH, 1, WIDTH)


def final_kernel(got, total, out, loss):
    acc = got[0, :, 0:WIDTH].astype(F32)
    row = got[0, 0:8, WIDTH:].astype(F32)
    for z in range(1, N_Z):
        acc = acc + got[z, :, 0:WIDTH].astype(F32)
        row = row + got[z, 0:8, WIDTH:].astype(F32)
    out[...] = acc.reshape(EACH, 1, WIDTH)
    whole = jnp.sum(jnp.where(lanes((1, LANES)) < 3, row[0:1], 0.0))
    loss[...] = (total[...] + whole) / (2.0 * PAIRS)


def body(image_emb, text_emb, logit_scale):
    places = [lax.axis_index(a) for a in (ROW, COL, "c", "xh", "y", "xl")]
    idx = jnp.stack(places).astype(jnp.int32)
    spread = jnp.broadcast_to(image_emb.reshape(1, EACH, WIDTH), (N_COL, EACH, WIDTH))
    images = exchange(spread, ("c", "xh", "y")).reshape(ROWS, WIDTH)
    texts = lax.all_gather(text_emb.reshape(EACH, WIDTH), "xl")
    texts = lax.all_gather(texts, "z").reshape(COLS, WIDTH)
    scores, cpack, rpack = call(
        score_kernel,
        [((ROWS, COLS), F32), ((N_ROW, 8, LANES), F32), ((8, LANES), F32)],
        [],
        idx, logit_scale, images, texts,
    )
    col_got = exchange(cpack, ROW)
    near = lax.all_gather(rpack, ("xh", "c"))
    col_lse, ypack = call(merge_kernel, [((8, COLS), F32), ((N_Y, 8, LANES), F32)], [], col_got, near)
    row_got = exchange(ypack, "y")
    iaway, ihere, taway, there, scal = call(
        grad_kernel,
        [
            ((ROWS // 2 + TAIL, WIDTH), BF16),
            ((ROWS // 2, WIDTH), F32),
            ((COLS // 2 + TAIL, WIDTH), BF16),
            ((COLS // 2, WIDTH), F32),
            ((16, LANES), F32),
        ],
        [((N_C, ROWS // 2, COLS), BF16), ((N_Z, N_XL, EACH, WIDTH), F32)],
        idx, logit_scale, scores, images, texts, row_got, col_lse,
    )
    tcame = shift(taway, "xl", 1)
    icame = shift(iaway, "c", 1)
    xaway, keep, total = call(
        across_kernel,
        [((ROWS // 4 + TAIL, WIDTH), BF16), ((ROWS // 4, WIDTH), F32), ((8, LANES), F32)],
        [],
        idx, scal, ihere, icame,
    )
    xcame = shift(xaway, "xh", 1)
    (tpack,) = call(text_kernel, [((N_Z, EACH, WIDTH + LANES), BF16)], [], scal, there, tcame)
    text_got = exchange(tpack, "z")
    ahead, behind, near3, total = call(
        ring_kernel,
        [((3 * EACH, WIDTH), BF16), ((2 * EACH, WIDTH), BF16), ((3 * EACH, WIDTH), F32), ((8, LANES), F32)],
        [],
        idx, total, keep, xcame,
    )
    low = shift(ahead, "y", 3)
    high = shift(behind, "y", 5)
    up, down, mid = call(
        side_kernel,
        [((EACH, WIDTH), BF16), ((EACH, WIDTH), BF16), ((EACH, WIDTH), F32)],
        [],
        near3, low, high,
    )
    left = shift(up, "y", 1)
    right = shift(down, "y", 7)
    (image_grad,) = call(image_kernel, [((EACH, 1, WIDTH), F32)], [], mid, left, right)
    text_grad, loss = call(final_kernel, [((EACH, 1, WIDTH), F32), ((8, LANES), F32)], [], text_got, total)
    return loss[0, 0], image_grad, text_grad


def solution(mesh):
    fine = Mesh(mesh.devices.reshape(N_XL, N_Z, N_Y, N_XH, N_C), ROW + COL)
    placed = (P(ROW, COL, None), P(COL, ROW, None), P())
    return jax.shard_map(
        body,
        mesh=fine,
        in_specs=placed,
        out_specs=(P(), P(ROW, COL, None), P(COL, ROW, None)),
        check_vma=False,
    )
```

time: 584 us -> 152 us (0.26)
  the two profiles are of different devices: /device:TPU:16 before, /device:TPU:30 now
where the time goes in v4:
time: 152 us; the launch traced here: 151 us
  blocking collectives  60.4 us (40%)
  starting transfers between devices  43.1 us (28%)
  waiting for transfers between devices  33.7 us (22%)
  Pallas kernels  8.36 us (6%)
  local copies, waits for them, and re-layouts  4.51 us (3%)
    all_gather x1, blocking collectives, body(): texts = lax.all_gather(texts, 'z').reshape(COLS, WIDTH)  34.3 us
    ppermute x7, waiting for transfers between devices, shift(): return lax.ppermute(x, axis, [(i, (i + k) % n) for i in range(n)])  30 us
    all_to_all x3, starting transfers between devices, exchange(): return lax.all_to_all(x, axes, 0, 0, tiled=False)  22.5 us
    ppermute x7, starting transfers between devices, shift(): return lax.ppermute(x, axis, [(i, (i + k) % n) for i in range(n)])  20.6 us
    all_to_all x1, blocking collectives, exchange(): return lax.all_to_all(x, axes, 0, 0, tiled=False)  12 us
    pallas_call x9, Pallas kernels, call(): pl.pallas_call(kernel, out_shape=[jax.ShapeDtypeStruct(s, d) for s, d in...  8.36 us
    all_gather x1, blocking collectives, body(): texts = lax.all_gather(text_emb.reshape(EACH, WIDTH), 'xl')  7.38 us
    all_gather x1, blocking collectives, body(): near = lax.all_gather(rpack, ('xh', 'c'))  6.71 us
  transfers between devices with their start and end apart: 10, of which 6 were waited for; matrix products, arithmetic and copies ran while one was open for 0% of the time, Pallas kernels for 1%

profile of v4, /device:TPU:30, one launch (start us, length us, event | category | flops | bytes accessed | tf_op | source)
XLA Modules:
  0.0 151.5 jit_solution(3964393415352618674)
XLA Ops:
  0.6 1.9 %broadcast_in_dim.8 = bf16[32,16,1024]{2,1,0:T(8,128)(2,1)} broadcast(bf16[16,1024]{1,0:T(8,128)(2,1)} %bitcast.18), dimensions={1,2} | broadcast | bytes 1081344 | tf_op jit(solution)/shard_map/broadcast_in_dim | solution.py:213
  2.5 9.9 %all-to-all-start = ((bf16[32,16,1024]{2,1,0:T(8,128)(2,1)}), bf16[32,16,1024]{2,1,0:T(8,128)(2,1)S(1)}, u32[]{:S(2)}, u32[]{:S(2)}) async-start(bf16[32,16,1024]{2,1,0:T(8,128)(2,1)} %broadcast_in_dim.8), calls=%async_computation | async-start | bytes 2097152 | tf_op jit(solution)/shard_map/all_to_all | solution.py:28
  12.4 0.0 copy-start.2
  13.1 0.1 stack.27.idx
  13.2 0.0 copy-done.2
  13.2 7.4 %all-gather = bf16[32,1,1024]{2,0,1:T(8,128)(2,1)S(1)} all-gather(bf16[16,1,1024]{2,0,1:T(8,128)(2,1)S(1)} %copy-done.2), channel_id=2, replica_groups=mesh['xl'=2,'z'=12,'y'=8,'xh'=2,'c'=2] {'xl'}, dimensions={0}, use_global_device_ids=true | all-gather | bytes 98304 | tf_op jit(solution)/shard_map/all_gather | solution.py:215
  20.6 34.3 %all-gather.1 = bf16[24,16,1024]{2,1,0:T(8,128)(2,1)S(1)} all-gather(bf16[2,16,1024]{2,1,0:T(8,128)(2,1)S(1)} %bitcast.17), channel_id=3, replica_groups=mesh['xl'=2,'z'=12,'y'=8,'xh'=2,'c'=2] {'z'}, dimensions={0}, use_global_device_ids=true | all-gather | bytes 851968 | tf_op jit(solution)/shard_map/all_gather | solution.py:216
  54.9 0.0 all-to-all-done
  54.9 2.2 %shard_map.58 = (f32[512,384]{1,0:T(8,128)S(1)}, f32[24,8,128]{2,1,0:T(8,128)}, f32[8,128]{1,0:T(8,128)S(1)}) custom-call(s32[6]{0:T(128)S(1)} %stack.27.idx, f32[1]{0:T(128)S(6)} %copy.6.fac, bf16[512,1024]{1,0:T(8,128)(2,1)S(1)} %bitcast.12, bf16[384,1024]{1,0:T(8,128)(2,1)S(1)} %bitcast.14), custom_call_target="tpu_custom_call" | custom-call | tf_op jit(solution)/shard_map/pallas_call | solution.py:38
  57.1 0.0 copy-start
  57.1 0.9 copy-done
  58.0 4.9 %all-to-all-start.1 = ((f32[24,8,128]{2,1,0:T(8,128)}), f32[24,8,128]{2,1,0:T(8,128)S(1)}, u32[]{:S(2)}, u32[]{:S(2)}) async-start(f32[24,8,128]{2,1,0:T(8,128)} %get-tuple-element.26), calls=%async_computation.1 | async-start | bytes 196608 | tf_op jit(solution)/shard_map/all_to_all | solution.py:28
  62.9 6.7 %all-gather.2 = f32[32,128]{1,0:T(8,128)S(1)} all-gather(f32[8,128]{1,0:T(8,128)S(1)} %get-tuple-element.27), channel_id=4, replica_groups=mesh['xl'=2,'z'=12,'y'=8,'xh'=2,'c'=2] {'xh','c'}, dimensions={0}, use_global_device_ids=true | all-gather | bytes 20480 | tf_op jit(solution)/shard_map/all_gather | solution.py:224
  69.6 3.8 %all-to-all-done.1.col = f32[24,8,128]{2,1,0:T(8,128)S(1)} async-done(((f32[24,8,128]{2,1,0:T(8,128)}), f32[24,8,128]{2,1,0:T(8,128)S(1)}, u32[]{:S(2)}, u32[]{:S(2)}) %all-to-all-start.1) | async-done | bytes 98336 | tf_op jit(solution)/shard_map/all_to_all | solution.py:28
  73.4 0.2 shard_map.59
  73.6 12.0 %all_to_all.20.got = f32[8,8,128]{2,1,0:T(8,128)S(1)} all-to-all(f32[8,8,128]{2,1,0:T(8,128)S(1)} %get-tuple-element.28), channel_id=1, replica_groups=mesh['xl'=2,'z'=12,'y'=8,'xh'=2,'c'=2] {'y'}, dimensions={0} | all-to-all | bytes 65536 | tf_op jit(solution)/shard_map/all_to_all | solution.py:28
  85.5 0.0 copy-start.1
  85.5 1.1 copy-done.1
  86.7 2.2 %shard_map.60 = (bf16[264,1024]{1,0:T(8,128)(2,1)S(1)}, f32[256,1024]{1,0:T(8,128)S(1)}, bf16[200,1024]{1,0:T(8,128)(2,1)S(1)}, f32[192,1024]{1,0:T(8,128)S(1)}, f32[16,128]{1,0:T(8,128)S(1)}) custom-call(s32[6]{0:T(128)S(1)} %stack.27.idx, f32[1]{0:T(128)S(6)} %copy.6.fac, f32[512,384]{1,0:T(8,128)S(1)} %copy-done.1, bf16[512,1024]{1,0:T(8,128)(2,1)S(1)} %bitcast.13, ...), custom_call_target="tpu_custom_call" | custom-call | tf_op jit(solution)/shard_map/pallas_call | solution.py:38
  88.9 2.6 %collective-permute-start = (bf16[200,1024]{1,0:T(8,128)(2,1)S(1)}, bf16[200,1024]{1,0:T(8,128)(2,1)S(1)}, u32[]{:S(2)}, u32[]{:S(2)}) collective-permute-start(bf16[200,1024]{1,0:T(8,128)(2,1)S(1)} %get-tuple-element.32), channel_id=1, source_target_pairs={{0,384},{384,0},{1,385},{385,1},{2,386},{386,2},{3,387},{387,3},{4... | collective-permute-start | bytes 1228808 | tf_op jit(solution)/shard_map/ppermute | solution.py:33
  91.5 7.2 %collective-permute-done.came = bf16[200,1024]{1,0:T(8,128)(2,1)S(1)} collective-permute-done((bf16[200,1024]{1,0:T(8,128)(2,1)S(1)}, bf16[200,1024]{1,0:T(8,128)(2,1)S(1)}, u32[]{:S(2)}, u32[]{:S(2)}) %collective-permute-start) | collective-permute-done | bytes 409632 | tf_op jit(solution)/shard_map/ppermute | solution.py:33
  98.7 1.0 shard_map.61
  99.7 7.7 %all-to-all-start.3 = ((bf16[12,16,1152]{2,1,0:T(8,128)(2,1)}), bf16[12,16,1152]{2,1,0:T(8,128)(2,1)S(1)}, u32[]{:S(2)}, u32[]{:S(2)}) async-start(bf16[12,16,1152]{2,1,0:T(8,128)(2,1)} %shard_map.61), calls=%async_computation.3 | async-start | bytes 884736 | tf_op jit(solution)/shard_map/all_to_all | solution.py:28
  107.4 1.9 %collective-permute-start.1 = (bf16[264,1024]{1,0:T(8,128)(2,1)S(1)}, bf16[264,1024]{1,0:T(8,128)(2,1)S(1)}, u32[]{:S(2)}, u32[]{:S(2)}) collective-permute-start(bf16[264,1024]{1,0:T(8,128)(2,1)S(1)} %get-tuple-element.34), channel_id=1, source_target_pairs={{0,1},{1,0},{2,3},{3,2},{4,5},{5,4},{6,7},{7,6},{8,9},{9,8},{10,11... | collective-permute-start | bytes 1622024 | tf_op jit(solution)/shard_map/ppermute | solution.py:33
  109.3 1.9 %collective-permute-done.1.came = bf16[264,1024]{1,0:T(8,128)(2,1)S(1)} collective-permute-done((bf16[264,1024]{1,0:T(8,128)(2,1)S(1)}, bf16[264,1024]{1,0:T(8,128)(2,1)S(1)}, u32[]{:S(2)}, u32[]{:S(2)}) %collective-permute-start.1) | collective-permute-done | bytes 540704 | tf_op jit(solution)/shard_map/ppermute | solution.py:33
  111.2 0.7 shard_map.62
  112.0 2.5 %collective-permute-start.2 = (bf16[136,1024]{1,0:T(8,128)(2,1)S(1)}, bf16[136,1024]{1,0:T(8,128)(2,1)S(1)}, u32[]{:S(2)}, u32[]{:S(2)}) collective-permute-start(bf16[136,1024]{1,0:T(8,128)(2,1)S(1)} %get-tuple-element.37), channel_id=1, source_target_pairs={{0,2},{2,0},{1,3},{3,1},{4,6},{6,4},{5,7},{7,5},{8,10},{10,8},{9,1... | collective-permute-start | bytes 835592 | tf_op jit(solution)/shard_map/ppermute | solution.py:33
  114.5 9.5 %collective-permute-done.2.got = bf16[136,1024]{1,0:T(8,128)(2,1)S(1)} collective-permute-done((bf16[136,1024]{1,0:T(8,128)(2,1)S(1)}, bf16[136,1024]{1,0:T(8,128)(2,1)S(1)}, u32[]{:S(2)}, u32[]{:S(2)}) %collective-permute-start.2) | collective-permute-done | bytes 278560 | tf_op jit(solution)/shard_map/ppermute | solution.py:33
  124.1 0.7 shard_map.63
  124.7 4.3 %collective-permute-start.3 = (bf16[48,1024]{1,0:T(8,128)(2,1)S(1)}, bf16[48,1024]{1,0:T(8,128)(2,1)S(1)}, u32[]{:S(2)}, u32[]{:S(2)}) collective-permute-start(bf16[48,1024]{1,0:T(8,128)(2,1)S(1)} %get-tuple-element.41), channel_id=1, source_target_pairs={{0,12},{4,16},{8,20},{12,24},{16,28},{20,0},{24,4},{28,8},{1,13},{... | collective-permute-start | bytes 294920 | tf_op jit(solution)/shard_map/ppermute | solution.py:33
  129.1 3.3 %collective-permute-start.4 = (bf16[32,1024]{1,0:T(8,128)(2,1)S(1)}, bf16[32,1024]{1,0:T(8,128)(2,1)S(1)}, u32[]{:S(2)}, u32[]{:S(2)}) collective-permute-start(bf16[32,1024]{1,0:T(8,128)(2,1)S(1)} %get-tuple-element.42), channel_id=1, source_target_pairs={{0,20},{4,24},{8,28},{12,0},{16,4},{20,8},{24,12},{28,16},{1,21},{... | collective-permute-start | bytes 196616 | tf_op jit(solution)/shard_map/ppermute | solution.py:33
  132.4 6.3 %collective-permute-done.4.high = bf16[32,1024]{1,0:T(8,128)(2,1)S(1)} collective-permute-done((bf16[32,1024]{1,0:T(8,128)(2,1)S(1)}, bf16[32,1024]{1,0:T(8,128)(2,1)S(1)}, u32[]{:S(2)}, u32[]{:S(2)}) %collective-permute-start.4) | collective-permute-done | bytes 65568 | tf_op jit(solution)/shard_map/ppermute | solution.py:33
  138.7 0.0 collective-permute-done.3.low
  138.7 1.9 %collective-permute-start.5 = (bf16[16,1024]{1,0:T(8,128)(2,1)S(1)}, bf16[16,1024]{1,0:T(8,128)(2,1)S(1)}, u32[]{:S(2)}, u32[]{:S(2)}) collective-permute-start(bf16[16,1024]{1,0:T(8,128)(2,1)S(1)} %get-tuple-element.44), channel_id=1, source_target_pairs={{0,4},{4,8},{8,12},{12,16},{16,20},{20,24},{24,28},{28,0},{1,5},{5... | collective-permute-start | bytes 98312 | tf_op jit(solution)/shard_map/ppermute | solution.py:33
  140.7 3.9 %collective-permute-start.6 = (bf16[16,1024]{1,0:T(8,128)(2,1)S(1)}, bf16[16,1024]{1,0:T(8,128)(2,1)S(1)}, u32[]{:S(2)}, u32[]{:S(2)}) collective-permute-start(bf16[16,1024]{1,0:T(8,128)(2,1)S(1)} %get-tuple-element.45), channel_id=1, source_target_pairs={{0,28},{4,0},{8,4},{12,8},{16,12},{20,16},{24,20},{28,24},{1,29},{... | collective-permute-start | bytes 98312 | tf_op jit(solution)/shard_map/ppermute | solution.py:33
  144.6 0.0 collective-permute-done.5.left
  144.6 5.0 %collective-permute-done.6.right = bf16[16,1024]{1,0:T(8,128)(2,1)S(1)} collective-permute-done((bf16[16,1024]{1,0:T(8,128)(2,1)S(1)}, bf16[16,1024]{1,0:T(8,128)(2,1)S(1)}, u32[]{:S(2)}, u32[]{:S(2)}) %collective-permute-start.6) | collective-permute-done | bytes 32800 | tf_op jit(solution)/shard_map/ppermute | solution.py:33
  149.6 0.7 shard_map.66
  150.3 0.0 all-to-all-done.3.got
  150.3 0.7 shard_map.64
  151.0 0.5 slice.3
  (1 shorter events, 0.0 us)
Async XLA Ops:
  2.5 52.4 %all-to-all-start = ((bf16[32,16,1024]{2,1,0:T(8,128)(2,1)}), bf16[32,16,1024]{2,1,0:T(8,128)(2,1)S(1)}, u32[]{:S(2)}, u32[]{:S(2)}) async-start(bf16[32,16,1024]{2,1,0:T(8,128)(2,1)} %broadcast_in_dim.8), calls=%async_computation | async-start | bytes 2097152 | tf_op jit(solution)/shard_map/all_to_all | solution.py:28
  12.4 0.8 copy-start.2
  57.1 0.9 copy-start
  58.0 15.4 %all-to-all-start.1 = ((f32[24,8,128]{2,1,0:T(8,128)}), f32[24,8,128]{2,1,0:T(8,128)S(1)}, u32[]{:S(2)}, u32[]{:S(2)}) async-start(f32[24,8,128]{2,1,0:T(8,128)} %get-tuple-element.26), calls=%async_computation.1 | async-start | bytes 196608 | tf_op jit(solution)/shard_map/all_to_all | solution.py:28
  85.5 1.1 copy-start.1
  88.9 9.8 %collective-permute-start = (bf16[200,1024]{1,0:T(8,128)(2,1)S(1)}, bf16[200,1024]{1,0:T(8,128)(2,1)S(1)}, u32[]{:S(2)}, u32[]{:S(2)}) collective-permute-start(bf16[200,1024]{1,0:T(8,128)(2,1)S(1)} %get-tuple-element.32), channel_id=1, source_target_pairs={{0,384},{384,0},{1,385},{385,1},{2,386},{386,2},{3,387},{387,3},{4... | collective-permute-start | bytes 1228808 | tf_op jit(solution)/shard_map/ppermute | solution.py:33
  99.7 50.6 %all-to-all-start.3 = ((bf16[12,16,1152]{2,1,0:T(8,128)(2,1)}), bf16[12,16,1152]{2,1,0:T(8,128)(2,1)S(1)}, u32[]{:S(2)}, u32[]{:S(2)}) async-start(bf16[12,16,1152]{2,1,0:T(8,128)(2,1)} %shard_map.61), calls=%async_computation.3 | async-start | bytes 884736 | tf_op jit(solution)/shard_map/all_to_all | solution.py:28
  107.4 3.8 %collective-permute-start.1 = (bf16[264,1024]{1,0:T(8,128)(2,1)S(1)}, bf16[264,1024]{1,0:T(8,128)(2,1)S(1)}, u32[]{:S(2)}, u32[]{:S(2)}) collective-permute-start(bf16[264,1024]{1,0:T(8,128)(2,1)S(1)} %get-tuple-element.34), channel_id=1, source_target_pairs={{0,1},{1,0},{2,3},{3,2},{4,5},{5,4},{6,7},{7,6},{8,9},{9,8},{10,11... | collective-permute-start | bytes 1622024 | tf_op jit(solution)/shard_map/ppermute | solution.py:33
  112.0 12.1 %collective-permute-start.2 = (bf16[136,1024]{1,0:T(8,128)(2,1)S(1)}, bf16[136,1024]{1,0:T(8,128)(2,1)S(1)}, u32[]{:S(2)}, u32[]{:S(2)}) collective-permute-start(bf16[136,1024]{1,0:T(8,128)(2,1)S(1)} %get-tuple-element.37), channel_id=1, source_target_pairs={{0,2},{2,0},{1,3},{3,1},{4,6},{6,4},{5,7},{7,5},{8,10},{10,8},{9,1... | collective-permute-start | bytes 835592 | tf_op jit(solution)/shard_map/ppermute | solution.py:33
  124.7 13.9 %collective-permute-start.3 = (bf16[48,1024]{1,0:T(8,128)(2,1)S(1)}, bf16[48,1024]{1,0:T(8,128)(2,1)S(1)}, u32[]{:S(2)}, u32[]{:S(2)}) collective-permute-start(bf16[48,1024]{1,0:T(8,128)(2,1)S(1)} %get-tuple-element.41), channel_id=1, source_target_pairs={{0,12},{4,16},{8,20},{12,24},{16,28},{20,0},{24,4},{28,8},{1,13},{... | collective-permute-start | bytes 294920 | tf_op jit(solution)/shard_map/ppermute | solution.py:33
  129.1 9.6 %collective-permute-start.4 = (bf16[32,1024]{1,0:T(8,128)(2,1)S(1)}, bf16[32,1024]{1,0:T(8,128)(2,1)S(1)}, u32[]{:S(2)}, u32[]{:S(2)}) collective-permute-start(bf16[32,1024]{1,0:T(8,128)(2,1)S(1)} %get-tuple-element.42), channel_id=1, source_target_pairs={{0,20},{4,24},{8,28},{12,0},{16,4},{20,8},{24,12},{28,16},{1,21},{... | collective-permute-start | bytes 196616 | tf_op jit(solution)/shard_map/ppermute | solution.py:33
  138.7 5.9 %collective-permute-start.5 = (bf16[16,1024]{1,0:T(8,128)(2,1)S(1)}, bf16[16,1024]{1,0:T(8,128)(2,1)S(1)}, u32[]{:S(2)}, u32[]{:S(2)}) collective-permute-start(bf16[16,1024]{1,0:T(8,128)(2,1)S(1)} %get-tuple-element.44), channel_id=1, source_target_pairs={{0,4},{4,8},{8,12},{12,16},{16,20},{20,24},{24,28},{28,0},{1,5},{5... | collective-permute-start | bytes 98312 | tf_op jit(solution)/shard_map/ppermute | solution.py:33
  140.7 9.0 %collective-permute-start.6 = (bf16[16,1024]{1,0:T(8,128)(2,1)S(1)}, bf16[16,1024]{1,0:T(8,128)(2,1)S(1)}, u32[]{:S(2)}, u32[]{:S(2)}) collective-permute-start(bf16[16,1024]{1,0:T(8,128)(2,1)S(1)} %get-tuple-element.45), channel_id=1, source_target_pairs={{0,28},{4,0},{8,4},{12,8},{16,12},{20,16},{24,20},{28,24},{1,29},{... | collective-permute-start | bytes 98312 | tf_op jit(solution)/shard_map/ppermute | solution.py:33

commit v5 on v4

--- a/solution.py
+++ b/solution.py
@@ -39,7 +39,7 @@
         kernel,
         out_shape=[jax.ShapeDtypeStruct(s, d) for s, d in outs],
         in_specs=in_specs,
-        out_specs=[VMEM] * len(outs),
+        out_specs=[SMEM if s == (1, 1) else VMEM for s, _ in outs],
         scratch_shapes=[pltpu.VMEM(s, d) for s, d in scratch],
         compiler_params=pltpu.CompilerParams(vmem_limit_bytes=24 << 20),
     )(*args)
@@ -81,6 +81,12 @@
     row_ids = (EACH * idx[0] + (i & 15)) * N_COL + i_dev
     col_ids = (EACH * idx[1] + (j & 15)) * N_ROW + j_dev
     return row_ids == col_ids
+
+
+def spread_kernel(block, out):
+    tile = block[...]
+    for n in range(N_COL):
+        out[n] = tile
 
 
 def score_kernel(idx, fac, im, tx, sc, cpack, rpack):
@@ -204,13 +210,13 @@
         row = row + got[z, 0:8, WIDTH:].astype(F32)
     out[...] = acc.reshape(EACH, 1, WIDTH)
     whole = jnp.sum(jnp.where(lanes((1, LANES)) < 3, row[0:1], 0.0))
-    loss[...] = (total[...] + whole) / (2.0 * PAIRS)
+    loss[0, 0] = (jnp.max(total[...]) + whole) / (2.0 * PAIRS)
 
 
 def body(image_emb, text_emb, logit_scale):
     places = [lax.axis_index(a) for a in (ROW, COL, "c", "xh", "y", "xl")]
     idx = jnp.stack(places).astype(jnp.int32)
-    spread = jnp.broadcast_to(image_emb.reshape(1, EACH, WIDTH), (N_COL, EACH, WIDTH))
+    (spread,) = call(spread_kernel, [((N_COL, EACH, WIDTH), BF16)], [], image_emb.reshape(EACH, WIDTH))
     images = exchange(spread, ("c", "xh", "y")).reshape(ROWS, WIDTH)
     texts = lax.all_gather(text_emb.reshape(EACH, WIDTH), "xl")
     texts = lax.all_gather(texts, "z").reshape(COLS, WIDTH)
@@ -264,7 +270,7 @@
     left = shift(up, "y", 1)
     right = shift(down, "y", 7)
     (image_grad,) = call(image_kernel, [((EACH, 1, WIDTH), F32)], [], mid, left, right)
-    text_grad, loss = call(final_kernel, [((EACH, 1, WIDTH), F32), ((8, LANES), F32)], [], text_got, total)
+    text_grad, loss = call(final_kernel, [((EACH, 1, WIDTH), F32), ((1, 1), F32)], [], text_got, total)
     return loss[0, 0], image_grad, text_grad
 
 

time: 152 us -> 152 us (level)
  local copies, waits for them, and re-layouts: 4.51 us -> 2.86 us
    broadcast_in_dim x1 -> x0, local copies, waits for them, and re-layouts: 1.89 us -> none  [body(): jnp.broadcast_to(image_emb.reshape(1, EACH, WIDTH), (N_COL, EACH, WIDTH))]
    pallas_call x9 -> x10, Pallas kernels: 8.36 us -> 9.52 us  [call(): pl.pallas_call(kernel, out_shape=[jax.ShapeDtypeStruct(s, d) for s, d in...]
where the time goes in v5:
time: 152 us; the launch traced here: 151 us
  blocking collectives  60.4 us (40%)
  starting transfers between devices  43.1 us (28%)
  waiting for transfers between devices  33.7 us (22%)
  Pallas kernels  9.52 us (6%)
  local copies, waits for them, and re-layouts  2.86 us (2%)
    all_gather x1, blocking collectives, body(): texts = lax.all_gather(texts, 'z').reshape(COLS, WIDTH)  34.3 us
    ppermute x7, waiting for transfers between devices, shift(): return lax.ppermute(x, axis, [(i, (i + k) % n) for i in range(n)])  30 us
    all_to_all x3, starting transfers between devices, exchange(): return lax.all_to_all(x, axes, 0, 0, tiled=False)  22.5 us
    ppermute x7, starting transfers between devices, shift(): return lax.ppermute(x, axis, [(i, (i + k) % n) for i in range(n)])  20.6 us
    all_to_all x1, blocking collectives, exchange(): return lax.all_to_all(x, axes, 0, 0, tiled=False)  12 us
    pallas_call x10, Pallas kernels, call(): pl.pallas_call(kernel, out_shape=[jax.ShapeDtypeStruct(s, d) for s, d in...  9.52 us
    all_gather x1, blocking collectives, body(): texts = lax.all_gather(text_emb.reshape(EACH, WIDTH), 'xl')  7.38 us
    all_gather x1, blocking collectives, body(): near = lax.all_gather(rpack, ('xh', 'c'))  6.71 us
  transfers between devices with their start and end apart: 10, of which 6 were waited for; matrix products, arithmetic and copies ran while one was open for 0% of the time, Pallas kernels for 1%

profile of v5, /device:TPU:30, one launch (start us, length us, event | category | flops | bytes accessed | tf_op | source)
XLA Modules:
  0.0 151.0 jit_solution(11164746447984032562)
XLA Ops:
  0.6 0.0 copy-start.2
  0.6 0.7 copy-done.2
  1.4 1.1 shard_map.58
  2.5 9.9 %all-to-all-start = ((bf16[32,16,1024]{2,1,0:T(8,128)(2,1)}), bf16[32,16,1024]{2,1,0:T(8,128)(2,1)S(1)}, u32[]{:S(2)}, u32[]{:S(2)}) async-start(bf16[32,16,1024]{2,1,0:T(8,128)(2,1)} %shard_map.58), calls=%async_computation | async-start | bytes 2097152 | tf_op jit(solution)/shard_map/all_to_all | solution.py:28
  12.4 0.0 copy-start.3
  13.1 0.1 stack.27.idx
  13.2 0.0 copy-done.3
  13.2 7.4 %all-gather = bf16[32,1,1024]{2,0,1:T(8,128)(2,1)S(1)} all-gather(bf16[16,1,1024]{2,0,1:T(8,128)(2,1)S(1)} %copy-done.3), channel_id=2, replica_groups=mesh['xl'=2,'z'=12,'y'=8,'xh'=2,'c'=2] {'xl'}, dimensions={0}, use_global_device_ids=true | all-gather | bytes 98304 | tf_op jit(solution)/shard_map/all_gather | solution.py:221
  20.5 34.3 %all-gather.1 = bf16[24,16,1024]{2,1,0:T(8,128)(2,1)S(1)} all-gather(bf16[2,16,1024]{2,1,0:T(8,128)(2,1)S(1)} %bitcast.18), channel_id=3, replica_groups=mesh['xl'=2,'z'=12,'y'=8,'xh'=2,'c'=2] {'z'}, dimensions={0}, use_global_device_ids=true | all-gather | bytes 851968 | tf_op jit(solution)/shard_map/all_gather | solution.py:222
  54.9 0.0 all-to-all-done
  54.9 2.2 %shard_map.59 = (f32[512,384]{1,0:T(8,128)S(1)}, f32[24,8,128]{2,1,0:T(8,128)}, f32[8,128]{1,0:T(8,128)S(1)}) custom-call(s32[6]{0:T(128)S(1)} %stack.27.idx, f32[1]{0:T(128)S(6)} %copy.6.fac, bf16[512,1024]{1,0:T(8,128)(2,1)S(1)} %bitcast.12, bf16[384,1024]{1,0:T(8,128)(2,1)S(1)} %bitcast.14), custom_call_target="tpu_custom_call" | custom-call | tf_op jit(solution)/shard_map/pallas_call | solution.py:38
  57.1 0.0 copy-start
  57.1 0.9 copy-done
  58.0 4.9 %all-to-all-start.1 = ((f32[24,8,128]{2,1,0:T(8,128)}), f32[24,8,128]{2,1,0:T(8,128)S(1)}, u32[]{:S(2)}, u32[]{:S(2)}) async-start(f32[24,8,128]{2,1,0:T(8,128)} %get-tuple-element.26), calls=%async_computation.1 | async-start | bytes 196608 | tf_op jit(solution)/shard_map/all_to_all | solution.py:28
  62.9 6.7 %all-gather.2 = f32[32,128]{1,0:T(8,128)S(1)} all-gather(f32[8,128]{1,0:T(8,128)S(1)} %get-tuple-element.27), channel_id=4, replica_groups=mesh['xl'=2,'z'=12,'y'=8,'xh'=2,'c'=2] {'xh','c'}, dimensions={0}, use_global_device_ids=true | all-gather | bytes 20480 | tf_op jit(solution)/shard_map/all_gather | solution.py:230
  69.6 3.8 %all-to-all-done.1.col = f32[24,8,128]{2,1,0:T(8,128)S(1)} async-done(((f32[24,8,128]{2,1,0:T(8,128)}), f32[24,8,128]{2,1,0:T(8,128)S(1)}, u32[]{:S(2)}, u32[]{:S(2)}) %all-to-all-start.1) | async-done | bytes 98336 | tf_op jit(solution)/shard_map/all_to_all | solution.py:28
  73.3 0.2 shard_map.60
  73.5 12.0 %all_to_all.20.got = f32[8,8,128]{2,1,0:T(8,128)S(1)} all-to-all(f32[8,8,128]{2,1,0:T(8,128)S(1)} %get-tuple-element.28), channel_id=1, replica_groups=mesh['xl'=2,'z'=12,'y'=8,'xh'=2,'c'=2] {'y'}, dimensions={0} | all-to-all | bytes 65536 | tf_op jit(solution)/shard_map/all_to_all | solution.py:28
  85.5 0.0 copy-start.1
  85.5 1.1 copy-done.1
  86.6 2.2 %shard_map.61 = (bf16[264,1024]{1,0:T(8,128)(2,1)S(1)}, f32[256,1024]{1,0:T(8,128)S(1)}, bf16[200,1024]{1,0:T(8,128)(2,1)S(1)}, f32[192,1024]{1,0:T(8,128)S(1)}, f32[16,128]{1,0:T(8,128)S(1)}) custom-call(s32[6]{0:T(128)S(1)} %stack.27.idx, f32[1]{0:T(128)S(6)} %copy.6.fac, f32[512,384]{1,0:T(8,128)S(1)} %copy-done.1, bf16[512,1024]{1,0:T(8,128)(2,1)S(1)} %bitcast.13, ...), custom_call_target="tpu_custom_call" | custom-call | tf_op jit(solution)/shard_map/pallas_call | solution.py:38
  88.8 2.6 %collective-permute-start = (bf16[200,1024]{1,0:T(8,128)(2,1)S(1)}, bf16[200,1024]{1,0:T(8,128)(2,1)S(1)}, u32[]{:S(2)}, u32[]{:S(2)}) collective-permute-start(bf16[200,1024]{1,0:T(8,128)(2,1)S(1)} %get-tuple-element.32), channel_id=1, source_target_pairs={{0,384},{384,0},{1,385},{385,1},{2,386},{386,2},{3,387},{387,3},{4... | collective-permute-start | bytes 1228808 | tf_op jit(solution)/shard_map/ppermute | solution.py:33
  91.5 7.2 %collective-permute-done.came = bf16[200,1024]{1,0:T(8,128)(2,1)S(1)} collective-permute-done((bf16[200,1024]{1,0:T(8,128)(2,1)S(1)}, bf16[200,1024]{1,0:T(8,128)(2,1)S(1)}, u32[]{:S(2)}, u32[]{:S(2)}) %collective-permute-start) | collective-permute-done | bytes 409632 | tf_op jit(solution)/shard_map/ppermute | solution.py:33
  98.7 1.0 shard_map.62
  99.7 7.7 %all-to-all-start.3 = ((bf16[12,16,1152]{2,1,0:T(8,128)(2,1)}), bf16[12,16,1152]{2,1,0:T(8,128)(2,1)S(1)}, u32[]{:S(2)}, u32[]{:S(2)}) async-start(bf16[12,16,1152]{2,1,0:T(8,128)(2,1)} %shard_map.62), calls=%async_computation.3 | async-start | bytes 884736 | tf_op jit(solution)/shard_map/all_to_all | solution.py:28
  107.4 1.9 %collective-permute-start.1 = (bf16[264,1024]{1,0:T(8,128)(2,1)S(1)}, bf16[264,1024]{1,0:T(8,128)(2,1)S(1)}, u32[]{:S(2)}, u32[]{:S(2)}) collective-permute-start(bf16[264,1024]{1,0:T(8,128)(2,1)S(1)} %get-tuple-element.34), channel_id=1, source_target_pairs={{0,1},{1,0},{2,3},{3,2},{4,5},{5,4},{6,7},{7,6},{8,9},{9,8},{10,11... | collective-permute-start | bytes 1622024 | tf_op jit(solution)/shard_map/ppermute | solution.py:33
  109.3 1.9 %collective-permute-done.1.came = bf16[264,1024]{1,0:T(8,128)(2,1)S(1)} collective-permute-done((bf16[264,1024]{1,0:T(8,128)(2,1)S(1)}, bf16[264,1024]{1,0:T(8,128)(2,1)S(1)}, u32[]{:S(2)}, u32[]{:S(2)}) %collective-permute-start.1) | collective-permute-done | bytes 540704 | tf_op jit(solution)/shard_map/ppermute | solution.py:33
  111.2 0.7 shard_map.63
  112.0 2.5 %collective-permute-start.2 = (bf16[136,1024]{1,0:T(8,128)(2,1)S(1)}, bf16[136,1024]{1,0:T(8,128)(2,1)S(1)}, u32[]{:S(2)}, u32[]{:S(2)}) collective-permute-start(bf16[136,1024]{1,0:T(8,128)(2,1)S(1)} %get-tuple-element.37), channel_id=1, source_target_pairs={{0,2},{2,0},{1,3},{3,1},{4,6},{6,4},{5,7},{7,5},{8,10},{10,8},{9,1... | collective-permute-start | bytes 835592 | tf_op jit(solution)/shard_map/ppermute | solution.py:33
  114.5 9.5 %collective-permute-done.2.got = bf16[136,1024]{1,0:T(8,128)(2,1)S(1)} collective-permute-done((bf16[136,1024]{1,0:T(8,128)(2,1)S(1)}, bf16[136,1024]{1,0:T(8,128)(2,1)S(1)}, u32[]{:S(2)}, u32[]{:S(2)}) %collective-permute-start.2) | collective-permute-done | bytes 278560 | tf_op jit(solution)/shard_map/ppermute | solution.py:33
  124.1 0.7 shard_map.64
  124.7 4.3 %collective-permute-start.3 = (bf16[48,1024]{1,0:T(8,128)(2,1)S(1)}, bf16[48,1024]{1,0:T(8,128)(2,1)S(1)}, u32[]{:S(2)}, u32[]{:S(2)}) collective-permute-start(bf16[48,1024]{1,0:T(8,128)(2,1)S(1)} %get-tuple-element.41), channel_id=1, source_target_pairs={{0,12},{4,16},{8,20},{12,24},{16,28},{20,0},{24,4},{28,8},{1,13},{... | collective-permute-start | bytes 294920 | tf_op jit(solution)/shard_map/ppermute | solution.py:33
  129.1 3.3 %collective-permute-start.4 = (bf16[32,1024]{1,0:T(8,128)(2,1)S(1)}, bf16[32,1024]{1,0:T(8,128)(2,1)S(1)}, u32[]{:S(2)}, u32[]{:S(2)}) collective-permute-start(bf16[32,1024]{1,0:T(8,128)(2,1)S(1)} %get-tuple-element.42), channel_id=1, source_target_pairs={{0,20},{4,24},{8,28},{12,0},{16,4},{20,8},{24,12},{28,16},{1,21},{... | collective-permute-start | bytes 196616 | tf_op jit(solution)/shard_map/ppermute | solution.py:33
  132.4 6.3 %collective-permute-done.4.high = bf16[32,1024]{1,0:T(8,128)(2,1)S(1)} collective-permute-done((bf16[32,1024]{1,0:T(8,128)(2,1)S(1)}, bf16[32,1024]{1,0:T(8,128)(2,1)S(1)}, u32[]{:S(2)}, u32[]{:S(2)}) %collective-permute-start.4) | collective-permute-done | bytes 65568 | tf_op jit(solution)/shard_map/ppermute | solution.py:33
  138.7 0.0 collective-permute-done.3.low
  138.7 1.9 %collective-permute-start.5 = (bf16[16,1024]{1,0:T(8,128)(2,1)S(1)}, bf16[16,1024]{1,0:T(8,128)(2,1)S(1)}, u32[]{:S(2)}, u32[]{:S(2)}) collective-permute-start(bf16[16,1024]{1,0:T(8,128)(2,1)S(1)} %get-tuple-element.44), channel_id=1, source_target_pairs={{0,4},{4,8},{8,12},{12,16},{16,20},{20,24},{24,28},{28,0},{1,5},{5... | collective-permute-start | bytes 98312 | tf_op jit(solution)/shard_map/ppermute | solution.py:33
  140.6 3.9 %collective-permute-start.6 = (bf16[16,1024]{1,0:T(8,128)(2,1)S(1)}, bf16[16,1024]{1,0:T(8,128)(2,1)S(1)}, u32[]{:S(2)}, u32[]{:S(2)}) collective-permute-start(bf16[16,1024]{1,0:T(8,128)(2,1)S(1)} %get-tuple-element.45), channel_id=1, source_target_pairs={{0,28},{4,0},{8,4},{12,8},{16,12},{20,16},{24,20},{28,24},{1,29},{... | collective-permute-start | bytes 98312 | tf_op jit(solution)/shard_map/ppermute | solution.py:33
  144.6 0.0 collective-permute-done.5.left
  144.6 5.0 %collective-permute-done.6.right = bf16[16,1024]{1,0:T(8,128)(2,1)S(1)} collective-permute-done((bf16[16,1024]{1,0:T(8,128)(2,1)S(1)}, bf16[16,1024]{1,0:T(8,128)(2,1)S(1)}, u32[]{:S(2)}, u32[]{:S(2)}) %collective-permute-start.6) | collective-permute-done | bytes 32800 | tf_op jit(solution)/shard_map/ppermute | solution.py:33
  149.6 0.7 shard_map.67
  150.3 0.0 all-to-all-done.3.got
  150.3 0.7 shard_map.65
  (1 shorter events, 0.0 us)
Async XLA Ops:
  0.6 0.8 copy-start.2
  2.5 52.4 %all-to-all-start = ((bf16[32,16,1024]{2,1,0:T(8,128)(2,1)}), bf16[32,16,1024]{2,1,0:T(8,128)(2,1)S(1)}, u32[]{:S(2)}, u32[]{:S(2)}) async-start(bf16[32,16,1024]{2,1,0:T(8,128)(2,1)} %shard_map.58), calls=%async_computation | async-start | bytes 2097152 | tf_op jit(solution)/shard_map/all_to_all | solution.py:28
  12.4 0.8 copy-start.3
  57.1 0.9 copy-start
  58.0 15.4 %all-to-all-start.1 = ((f32[24,8,128]{2,1,0:T(8,128)}), f32[24,8,128]{2,1,0:T(8,128)S(1)}, u32[]{:S(2)}, u32[]{:S(2)}) async-start(f32[24,8,128]{2,1,0:T(8,128)} %get-tuple-element.26), calls=%async_computation.1 | async-start | bytes 196608 | tf_op jit(solution)/shard_map/all_to_all | solution.py:28
  85.5 1.1 copy-start.1
  88.8 9.8 %collective-permute-start = (bf16[200,1024]{1,0:T(8,128)(2,1)S(1)}, bf16[200,1024]{1,0:T(8,128)(2,1)S(1)}, u32[]{:S(2)}, u32[]{:S(2)}) collective-permute-start(bf16[200,1024]{1,0:T(8,128)(2,1)S(1)} %get-tuple-element.32), channel_id=1, source_target_pairs={{0,384},{384,0},{1,385},{385,1},{2,386},{386,2},{3,387},{387,3},{4... | collective-permute-start | bytes 1228808 | tf_op jit(solution)/shard_map/ppermute | solution.py:33
  99.7 50.6 %all-to-all-start.3 = ((bf16[12,16,1152]{2,1,0:T(8,128)(2,1)}), bf16[12,16,1152]{2,1,0:T(8,128)(2,1)S(1)}, u32[]{:S(2)}, u32[]{:S(2)}) async-start(bf16[12,16,1152]{2,1,0:T(8,128)(2,1)} %shard_map.62), calls=%async_computation.3 | async-start | bytes 884736 | tf_op jit(solution)/shard_map/all_to_all | solution.py:28
  107.4 3.8 %collective-permute-start.1 = (bf16[264,1024]{1,0:T(8,128)(2,1)S(1)}, bf16[264,1024]{1,0:T(8,128)(2,1)S(1)}, u32[]{:S(2)}, u32[]{:S(2)}) collective-permute-start(bf16[264,1024]{1,0:T(8,128)(2,1)S(1)} %get-tuple-element.34), channel_id=1, source_target_pairs={{0,1},{1,0},{2,3},{3,2},{4,5},{5,4},{6,7},{7,6},{8,9},{9,8},{10,11... | collective-permute-start | bytes 1622024 | tf_op jit(solution)/shard_map/ppermute | solution.py:33
  112.0 12.1 %collective-permute-start.2 = (bf16[136,1024]{1,0:T(8,128)(2,1)S(1)}, bf16[136,1024]{1,0:T(8,128)(2,1)S(1)}, u32[]{:S(2)}, u32[]{:S(2)}) collective-permute-start(bf16[136,1024]{1,0:T(8,128)(2,1)S(1)} %get-tuple-element.37), channel_id=1, source_target_pairs={{0,2},{2,0},{1,3},{3,1},{4,6},{6,4},{5,7},{7,5},{8,10},{10,8},{9,1... | collective-permute-start | bytes 835592 | tf_op jit(solution)/shard_map/ppermute | solution.py:33
  124.7 13.9 %collective-permute-start.3 = (bf16[48,1024]{1,0:T(8,128)(2,1)S(1)}, bf16[48,1024]{1,0:T(8,128)(2,1)S(1)}, u32[]{:S(2)}, u32[]{:S(2)}) collective-permute-start(bf16[48,1024]{1,0:T(8,128)(2,1)S(1)} %get-tuple-element.41), channel_id=1, source_target_pairs={{0,12},{4,16},{8,20},{12,24},{16,28},{20,0},{24,4},{28,8},{1,13},{... | collective-permute-start | bytes 294920 | tf_op jit(solution)/shard_map/ppermute | solution.py:33
  129.1 9.6 %collective-permute-start.4 = (bf16[32,1024]{1,0:T(8,128)(2,1)S(1)}, bf16[32,1024]{1,0:T(8,128)(2,1)S(1)}, u32[]{:S(2)}, u32[]{:S(2)}) collective-permute-start(bf16[32,1024]{1,0:T(8,128)(2,1)S(1)} %get-tuple-element.42), channel_id=1, source_target_pairs={{0,20},{4,24},{8,28},{12,0},{16,4},{20,8},{24,12},{28,16},{1,21},{... | collective-permute-start | bytes 196616 | tf_op jit(solution)/shard_map/ppermute | solution.py:33
  138.7 5.9 %collective-permute-start.5 = (bf16[16,1024]{1,0:T(8,128)(2,1)S(1)}, bf16[16,1024]{1,0:T(8,128)(2,1)S(1)}, u32[]{:S(2)}, u32[]{:S(2)}) collective-permute-start(bf16[16,1024]{1,0:T(8,128)(2,1)S(1)} %get-tuple-element.44), channel_id=1, source_target_pairs={{0,4},{4,8},{8,12},{12,16},{16,20},{20,24},{24,28},{28,0},{1,5},{5... | collective-permute-start | bytes 98312 | tf_op jit(solution)/shard_map/ppermute | solution.py:33
  140.6 9.0 %collective-permute-start.6 = (bf16[16,1024]{1,0:T(8,128)(2,1)S(1)}, bf16[16,1024]{1,0:T(8,128)(2,1)S(1)}, u32[]{:S(2)}, u32[]{:S(2)}) collective-permute-start(bf16[16,1024]{1,0:T(8,128)(2,1)S(1)} %get-tuple-element.45), channel_id=1, source_target_pairs={{0,28},{4,0},{8,4},{12,8},{16,12},{20,16},{24,20},{28,24},{1,29},{... | collective-permute-start | bytes 98312 | tf_op jit(solution)/shard_map/ppermute | solution.py:33

commit v6 on v5

--- a/solution.py
+++ b/solution.py
@@ -18,6 +18,7 @@
 PAIRS = ROWS * N_ROW
 LANES = 128
 TAIL = 8
+SLABS = WIDTH // LANES
 BF16 = jnp.bfloat16
 F32 = jnp.float32
 VMEM = pl.BlockSpec(memory_space=pltpu.VMEM)
@@ -122,7 +123,7 @@
         pack[n, 5:6, :] = total
 
 
-def grad_kernel(idx, fac, sc, im, tx, got, clse, iaway, ihere, taway, there, scal, delta, part):
+def grad_kernel(idx, fac, sc, im, tx, got, clse, iaway, taway, there, scal, delta, part):
     rows = merged([got[n] for n in range(N_Y)])[0:4]
     diag = sum(got[n, 4:5, :] for n in range(N_Y))
     total = sum(got[n, 5:6, :] for n in range(N_Y))
@@ -148,7 +149,10 @@
         taway[z * EACH : (z + 1) * EACH, :] = part[z, 1 - xl].astype(BF16)
         there[z * EACH : (z + 1) * EACH, :] = part[z, xl]
     put_tail(taway, COLS // 2, row_loss)
-    ihere[...] = jnp.dot(delta[c], tx[...], preferred_element_type=F32)
+
+
+def keep_kernel(idx, delta, tx, ihere):
+    ihere[...] = jnp.dot(delta[idx[2]], tx[...], preferred_element_type=F32)
 
 
 def across_kernel(idx, scal, here, came, away, keep, out):
@@ -167,11 +171,11 @@
     half = COLS // 2
     loss = scal[0:8, :] + value(came[half : half + TAIL, 0:LANES])
     both = (here[...] + came[0:half, :].astype(F32)).astype(BF16)
-    out[:, :, 0:WIDTH] = both.reshape(N_Z, EACH, WIDTH)
     tile = pieces(loss[0:1])
     for z in range(N_Z):
-        out[z, 0:8, WIDTH:] = tile
-        out[z, 8:16, WIDTH:] = jnp.zeros((8, LANES), BF16)
+        for k in range(SLABS):
+            out[z, k * EACH : (k + 1) * EACH, :] = both[z * EACH : (z + 1) * EACH, k * LANES : (k + 1) * LANES]
+        out[z, SLABS * EACH :, :] = tile
 
 
 def ring_kernel(idx, total, keep, got, ahead, behind, near, out):
@@ -183,19 +187,19 @@
         at = pl.multiple_of(((y + k) & (N_Y - 1)) * EACH, EACH)
         return keep[pl.ds(at, EACH), :] + got[pl.ds(at, EACH), :].astype(F32)
 
-    for n, k in enumerate((2, 3, 4)):
+    for n, k in enumerate((1, 4, 6)):
         ahead[n * EACH : (n + 1) * EACH, :] = block(k).astype(BF16)
-    for n, k in enumerate((5, 6)):
+    for n, k in enumerate((7, 2)):
         behind[n * EACH : (n + 1) * EACH, :] = block(k).astype(BF16)
-    for n, k in enumerate((7, 0, 1)):
+    for n, k in enumerate((0, 3, 5)):
         near[n * EACH : (n + 1) * EACH, :] = block(k)
 
 
 def side_kernel(near, low, high, up, down, mid):
     e = EACH
-    down[...] = (near[0:e, :] + low[0:e, :].astype(F32)).astype(BF16)
-    mid[...] = near[e : 2 * e, :] + low[e : 2 * e, :].astype(F32) + high[0:e, :].astype(F32)
-    up[...] = (near[2 * e :, :] + low[2 * e :, :].astype(F32) + high[e:, :].astype(F32)).astype(BF16)
+    mid[...] = near[0:e, :] + low[0:e, :].astype(F32) + high[0:e, :].astype(F32)
+    up[...] = (near[e : 2 * e, :] + low[e : 2 * e, :].astype(F32) + high[e:, :].astype(F32)).astype(BF16)
+    down[...] = (near[2 * e :, :] + low[2 * e :, :].astype(F32)).astype(BF16)
 
 
 def image_kernel(mid, left, right, out):
@@ -203,11 +207,11 @@
 
 
 def final_kernel(got, total, out, loss):
-    acc = got[0, :, 0:WIDTH].astype(F32)
-    row = got[0, 0:8, WIDTH:].astype(F32)
+    acc = got[0].astype(F32)
     for z in range(1, N_Z):
-        acc = acc + got[z, :, 0:WIDTH].astype(F32)
-        row = row + got[z, 0:8, WIDTH:].astype(F32)
+        acc = acc + got[z].astype(F32)
+    row = acc[SLABS * EACH :]
+    acc = jnp.concatenate([acc[k * EACH : (k + 1) * EACH] for k in range(SLABS)], axis=1)
     out[...] = acc.reshape(EACH, 1, WIDTH)
     whole = jnp.sum(jnp.where(lanes((1, LANES)) < 3, row[0:1], 0.0))
     loss[0, 0] = (jnp.max(total[...]) + whole) / (2.0 * PAIRS)
@@ -230,20 +234,21 @@
     near = lax.all_gather(rpack, ("xh", "c"))
     col_lse, ypack = call(merge_kernel, [((8, COLS), F32), ((N_Y, 8, LANES), F32)], [], col_got, near)
     row_got = exchange(ypack, "y")
-    iaway, ihere, taway, there, scal = call(
+    iaway, taway, there, scal, delta = call(
         grad_kernel,
         [
             ((ROWS // 2 + TAIL, WIDTH), BF16),
-            ((ROWS // 2, WIDTH), F32),
             ((COLS // 2 + TAIL, WIDTH), BF16),
             ((COLS // 2, WIDTH), F32),
             ((16, LANES), F32),
+            ((N_C, ROWS // 2, COLS), BF16),
         ],
-        [((N_C, ROWS // 2, COLS), BF16), ((N_Z, N_XL, EACH, WIDTH), F32)],
+        [((N_Z, N_XL, EACH, WIDTH), F32)],
         idx, logit_scale, scores, images, texts, row_got, col_lse,
     )
     tcame = shift(taway, "xl", 1)
     icame = shift(iaway, "c", 1)
+    (ihere,) = call(keep_kernel, [((ROWS // 2, WIDTH), F32)], [], idx, delta, texts)
     xaway, keep, total = call(
         across_kernel,
         [((ROWS // 4 + TAIL, WIDTH), BF16), ((ROWS // 4, WIDTH), F32), ((8, LANES), F32)],
@@ -251,7 +256,7 @@
         idx, scal, ihere, icame,
     )
     xcame = shift(xaway, "xh", 1)
-    (tpack,) = call(text_kernel, [((N_Z, EACH, WIDTH + LANES), BF16)], [], scal, there, tcame)
+    (tpack,) = call(text_kernel, [((N_Z, SLABS * EACH + TAIL, LANES), BF16)], [], scal, there, tcame)
     text_got = exchange(tpack, "z")
     ahead, behind, near3, total = call(
         ring_kernel,
@@ -259,16 +264,16 @@
         [],
         idx, total, keep, xcame,
     )
-    low = shift(ahead, "y", 3)
-    high = shift(behind, "y", 5)
+    low = shift(ahead, "y", 1)
+    high = shift(behind, "y", 7)
     up, down, mid = call(
         side_kernel,
         [((EACH, WIDTH), BF16), ((EACH, WIDTH), BF16), ((EACH, WIDTH), F32)],
         [],
         near3, low, high,
     )
-    left = shift(up, "y", 1)
-    right = shift(down, "y", 7)
+    left = shift(up, "y", 3)
+    right = shift(down, "y", 5)
     (image_grad,) = call(image_kernel, [((EACH, 1, WIDTH), F32)], [], mid, left, right)
     text_grad, loss = call(final_kernel, [((EACH, 1, WIDTH), F32), ((1, 1), F32)], [], text_got, total)
     return loss[0, 0], image_grad, text_grad

time: 152 us -> 149 us (0.980)
  the two profiles are of different devices: /device:TPU:30 before, /device:TPU:14 now
where the time goes in v6:
time: 149 us; the launch traced here: 148 us
  blocking collectives  62.2 us (42%)
  starting transfers between devices  45 us (30%)
  waiting for transfers between devices  27.9 us (19%)
  Pallas kernels  10.2 us (7%)
  local copies, waits for them, and re-layouts  1.65 us (1%)
    all_gather x1, blocking collectives, body(): texts = lax.all_gather(texts, 'z').reshape(COLS, WIDTH)  36.4 us
    ppermute x7, waiting for transfers between devices, shift(): return lax.ppermute(x, axis, [(i, (i + k) % n) for i in range(n)])  24.4 us
    all_to_all x3, starting transfers between devices, exchange(): return lax.all_to_all(x, axes, 0, 0, tiled=False)  23.2 us
    ppermute x7, starting transfers between devices, shift(): return lax.ppermute(x, axis, [(i, (i + k) % n) for i in range(n)])  21.8 us
    all_to_all x1, blocking collectives, exchange(): return lax.all_to_all(x, axes, 0, 0, tiled=False)  12.8 us
    pallas_call x11, Pallas kernels, call(): pl.pallas_call(kernel, out_shape=[jax.ShapeDtypeStruct(s, d) for s, d in...  10.2 us
    all_gather x1, blocking collectives, body(): near = lax.all_gather(rpack, ('xh', 'c'))  6.71 us
    all_gather x1, blocking collectives, body(): texts = lax.all_gather(text_emb.reshape(EACH, WIDTH), 'xl')  6.26 us
  transfers between devices with their start and end apart: 10, of which 7 were waited for; matrix products, arithmetic and copies ran while one was open for 0% of the time, Pallas kernels for 2%

profile of v6, /device:TPU:14, one launch (start us, length us, event | category | flops | bytes accessed | tf_op | source)
XLA Modules:
  0.0 148.3 jit_solution(15883311867123674935)
XLA Ops:
  0.6 0.0 copy-start
  0.6 0.7 copy-done
  1.4 1.1 shard_map.58
  2.5 10.1 %all-to-all-start = ((bf16[32,16,1024]{2,1,0:T(8,128)(2,1)}), bf16[32,16,1024]{2,1,0:T(8,128)(2,1)S(1)}, u32[]{:S(2)}, u32[]{:S(2)}) async-start(bf16[32,16,1024]{2,1,0:T(8,128)(2,1)} %shard_map.58), calls=%async_computation | async-start | bytes 2097152 | tf_op jit(solution)/shard_map/all_to_all | solution.py:29
  12.6 0.0 copy-start.3
  13.3 0.1 stack.27.idx
  13.4 0.0 copy-done.3
  13.4 6.3 %all-gather = bf16[32,1,1024]{2,0,1:T(8,128)(2,1)S(1)} all-gather(bf16[16,1,1024]{2,0,1:T(8,128)(2,1)S(1)} %copy-done.3), channel_id=2, replica_groups=mesh['xl'=2,'z'=12,'y'=8,'xh'=2,'c'=2] {'xl'}, dimensions={0}, use_global_device_ids=true | all-gather | bytes 98304 | tf_op jit(solution)/shard_map/all_gather | solution.py:225
  19.7 36.4 %all-gather.1 = bf16[24,16,1024]{2,1,0:T(8,128)(2,1)S(1)} all-gather(bf16[2,16,1024]{2,1,0:T(8,128)(2,1)S(1)} %bitcast.19), channel_id=3, replica_groups=mesh['xl'=2,'z'=12,'y'=8,'xh'=2,'c'=2] {'z'}, dimensions={0}, use_global_device_ids=true | all-gather | bytes 851968 | tf_op jit(solution)/shard_map/all_gather | solution.py:226
  56.0 0.0 all-to-all-done
  56.0 2.2 %shard_map.59 = (f32[512,384]{1,0:T(8,128)S(1)}, f32[24,8,128]{2,1,0:T(8,128)}, f32[8,128]{1,0:T(8,128)S(1)}) custom-call(s32[6]{0:T(128)S(1)} %stack.27.idx, f32[1]{0:T(128)S(6)} %copy.6.fac, bf16[512,1024]{1,0:T(8,128)(2,1)S(1)} %bitcast.15, bf16[384,1024]{1,0:T(8,128)(2,1)S(1)} %bitcast.12), custom_call_target="tpu_custom_call" | custom-call | tf_op jit(solution)/shard_map/pallas_call | solution.py:39
  58.2 5.1 %all-to-all-start.1 = ((f32[24,8,128]{2,1,0:T(8,128)}), f32[24,8,128]{2,1,0:T(8,128)S(1)}, u32[]{:S(2)}, u32[]{:S(2)}) async-start(f32[24,8,128]{2,1,0:T(8,128)} %get-tuple-element.26), calls=%async_computation.1 | async-start | bytes 196608 | tf_op jit(solution)/shard_map/all_to_all | solution.py:29
  63.4 6.7 %all-gather.2 = f32[32,128]{1,0:T(8,128)S(1)} all-gather(f32[8,128]{1,0:T(8,128)S(1)} %get-tuple-element.27), channel_id=4, replica_groups=mesh['xl'=2,'z'=12,'y'=8,'xh'=2,'c'=2] {'xh','c'}, dimensions={0}, use_global_device_ids=true | all-gather | bytes 20480 | tf_op jit(solution)/shard_map/all_gather | solution.py:234
  70.1 3.6 %all-to-all-done.1.col = f32[24,8,128]{2,1,0:T(8,128)S(1)} async-done(((f32[24,8,128]{2,1,0:T(8,128)}), f32[24,8,128]{2,1,0:T(8,128)S(1)}, u32[]{:S(2)}, u32[]{:S(2)}) %all-to-all-start.1) | async-done | bytes 98336 | tf_op jit(solution)/shard_map/all_to_all | solution.py:29
  73.6 0.2 shard_map.60
  73.8 12.8 %all_to_all.20.got = f32[8,8,128]{2,1,0:T(8,128)S(1)} all-to-all(f32[8,8,128]{2,1,0:T(8,128)S(1)} %get-tuple-element.28), channel_id=1, replica_groups=mesh['xl'=2,'z'=12,'y'=8,'xh'=2,'c'=2] {'y'}, dimensions={0} | all-to-all | bytes 65536 | tf_op jit(solution)/shard_map/all_to_all | solution.py:29
  86.6 1.9 %shard_map.61 = (bf16[264,1024]{1,0:T(8,128)(2,1)S(1)}, bf16[200,1024]{1,0:T(8,128)(2,1)S(1)}, f32[192,1024]{1,0:T(8,128)S(1)}, f32[16,128]{1,0:T(8,128)S(1)}, bf16[2,256,384]{2,1,0:T(8,128)(2,1)S(1)}) custom-call(s32[6]{0:T(128)S(1)} %stack.27.idx, f32[1]{0:T(128)S(6)} %copy.6.fac, f32[512,384]{1,0:T(8,128)S(1)} %get-tuple-element.25.sc, ...), custom_call_target="tpu_custom_call" | custom-call | tf_op jit(solution)/shard_map/pallas_call | solution.py:39
  88.6 0.0 copy-start.1
  88.6 0.8 copy-done.1
  89.4 2.6 %collective-permute-start = (bf16[200,1024]{1,0:T(8,128)(2,1)S(1)}, bf16[200,1024]{1,0:T(8,128)(2,1)S(1)}, u32[]{:S(2)}, u32[]{:S(2)}) collective-permute-start(bf16[200,1024]{1,0:T(8,128)(2,1)S(1)} %get-tuple-element.32), channel_id=1, source_target_pairs={{0,384},{384,0},{1,385},{385,1},{2,386},{386,2},{3,387},{387,3},{4... | collective-permute-start | bytes 1228808 | tf_op jit(solution)/shard_map/ppermute | solution.py:34
  92.0 7.2 %collective-permute-done.came = bf16[200,1024]{1,0:T(8,128)(2,1)S(1)} collective-permute-done((bf16[200,1024]{1,0:T(8,128)(2,1)S(1)}, bf16[200,1024]{1,0:T(8,128)(2,1)S(1)}, u32[]{:S(2)}, u32[]{:S(2)}) %collective-permute-start) | collective-permute-done | bytes 409632 | tf_op jit(solution)/shard_map/ppermute | solution.py:34
  99.2 1.0 shard_map.62
  100.2 0.0 copy-start.2
  100.2 7.9 %all-to-all-start.3 = ((bf16[12,136,128]{2,1,0:T(8,128)(2,1)}), bf16[12,136,128]{2,1,0:T(8,128)(2,1)S(1)}, u32[]{:S(2)}, u32[]{:S(2)}) async-start(bf16[12,136,128]{2,1,0:T(8,128)(2,1)} %shard_map.62), calls=%async_computation.3 | async-start | bytes 835584 | tf_op jit(solution)/shard_map/all_to_all | solution.py:29
  108.1 0.0 copy-done.2
  108.1 1.9 %collective-permute-start.1 = (bf16[264,1024]{1,0:T(8,128)(2,1)S(1)}, bf16[264,1024]{1,0:T(8,128)(2,1)S(1)}, u32[]{:S(2)}, u32[]{:S(2)}) collective-permute-start(bf16[264,1024]{1,0:T(8,128)(2,1)S(1)} %copy-done.2), channel_id=1, source_target_pairs={{0,1},{1,0},{2,3},{3,2},{4,5},{5,4},{6,7},{7,6},{8,9},{9,8},{10,11... | collective-permute-start | bytes 1622024 | tf_op jit(solution)/shard_map/ppermute | solution.py:34
  110.1 1.0 shard_map.63.here
  111.0 0.9 collective-permute-done.1.came
  112.0 0.7 shard_map.64
  112.7 2.5 %collective-permute-start.2 = (bf16[136,1024]{1,0:T(8,128)(2,1)S(1)}, bf16[136,1024]{1,0:T(8,128)(2,1)S(1)}, u32[]{:S(2)}, u32[]{:S(2)}) collective-permute-start(bf16[136,1024]{1,0:T(8,128)(2,1)S(1)} %get-tuple-element.37), channel_id=1, source_target_pairs={{0,2},{2,0},{1,3},{3,1},{4,6},{6,4},{5,7},{7,5},{8,10},{10,8},{9,1... | collective-permute-start | bytes 835592 | tf_op jit(solution)/shard_map/ppermute | solution.py:34
  115.3 9.5 %collective-permute-done.2.got = bf16[136,1024]{1,0:T(8,128)(2,1)S(1)} collective-permute-done((bf16[136,1024]{1,0:T(8,128)(2,1)S(1)}, bf16[136,1024]{1,0:T(8,128)(2,1)S(1)}, u32[]{:S(2)}, u32[]{:S(2)}) %collective-permute-start.2) | collective-permute-done | bytes 278560 | tf_op jit(solution)/shard_map/ppermute | solution.py:34
  124.8 0.7 shard_map.65
  125.5 2.5 %collective-permute-start.3 = (bf16[48,1024]{1,0:T(8,128)(2,1)S(1)}, bf16[48,1024]{1,0:T(8,128)(2,1)S(1)}, u32[]{:S(2)}, u32[]{:S(2)}) collective-permute-start(bf16[48,1024]{1,0:T(8,128)(2,1)S(1)} %get-tuple-element.41), channel_id=1, source_target_pairs={{0,4},{4,8},{8,12},{12,16},{16,20},{20,24},{24,28},{28,0},{1,5},{5... | collective-permute-start | bytes 294920 | tf_op jit(solution)/shard_map/ppermute | solution.py:34
  127.9 3.4 %collective-permute-start.4 = (bf16[32,1024]{1,0:T(8,128)(2,1)S(1)}, bf16[32,1024]{1,0:T(8,128)(2,1)S(1)}, u32[]{:S(2)}, u32[]{:S(2)}) collective-permute-start(bf16[32,1024]{1,0:T(8,128)(2,1)S(1)} %get-tuple-element.42), channel_id=1, source_target_pairs={{0,28},{4,0},{8,4},{12,8},{16,12},{20,16},{24,20},{28,24},{1,29},{... | collective-permute-start | bytes 196616 | tf_op jit(solution)/shard_map/ppermute | solution.py:34
  131.3 2.8 %collective-permute-done.4.high = bf16[32,1024]{1,0:T(8,128)(2,1)S(1)} collective-permute-done((bf16[32,1024]{1,0:T(8,128)(2,1)S(1)}, bf16[32,1024]{1,0:T(8,128)(2,1)S(1)}, u32[]{:S(2)}, u32[]{:S(2)}) %collective-permute-start.4) | collective-permute-done | bytes 65568 | tf_op jit(solution)/shard_map/ppermute | solution.py:34
  134.1 0.0 collective-permute-done.3.low
  134.2 3.4 %collective-permute-start.5 = (bf16[16,1024]{1,0:T(8,128)(2,1)S(1)}, bf16[16,1024]{1,0:T(8,128)(2,1)S(1)}, u32[]{:S(2)}, u32[]{:S(2)}) collective-permute-start(bf16[16,1024]{1,0:T(8,128)(2,1)S(1)} %get-tuple-element.44), channel_id=1, source_target_pairs={{0,12},{4,16},{8,20},{12,24},{16,28},{20,0},{24,4},{28,8},{1,13},{... | collective-permute-start | bytes 98312 | tf_op jit(solution)/shard_map/ppermute | solution.py:34
  137.5 5.5 %collective-permute-start.6 = (bf16[16,1024]{1,0:T(8,128)(2,1)S(1)}, bf16[16,1024]{1,0:T(8,128)(2,1)S(1)}, u32[]{:S(2)}, u32[]{:S(2)}) collective-permute-start(bf16[16,1024]{1,0:T(8,128)(2,1)S(1)} %get-tuple-element.45), channel_id=1, source_target_pairs={{0,20},{4,24},{8,28},{12,0},{16,4},{20,8},{24,12},{28,16},{1,21},{... | collective-permute-start | bytes 98312 | tf_op jit(solution)/shard_map/ppermute | solution.py:34
  143.0 0.2 collective-permute-done.5.left
  143.2 3.7 %collective-permute-done.6.right = bf16[16,1024]{1,0:T(8,128)(2,1)S(1)} collective-permute-done((bf16[16,1024]{1,0:T(8,128)(2,1)S(1)}, bf16[16,1024]{1,0:T(8,128)(2,1)S(1)}, u32[]{:S(2)}, u32[]{:S(2)}) %collective-permute-start.6) | collective-permute-done | bytes 32800 | tf_op jit(solution)/shard_map/ppermute | solution.py:34
  146.9 0.7 shard_map.68
  147.6 0.0 all-to-all-done.3.got
  147.6 0.7 shard_map.66
  (1 shorter events, 0.0 us)
Async XLA Ops:
  0.6 0.8 copy-start
  2.5 53.5 %all-to-all-start = ((bf16[32,16,1024]{2,1,0:T(8,128)(2,1)}), bf16[32,16,1024]{2,1,0:T(8,128)(2,1)S(1)}, u32[]{:S(2)}, u32[]{:S(2)}) async-start(bf16[32,16,1024]{2,1,0:T(8,128)(2,1)} %shard_map.58), calls=%async_computation | async-start | bytes 2097152 | tf_op jit(solution)/shard_map/all_to_all | solution.py:29
  12.6 0.8 copy-start.3
  58.2 15.4 %all-to-all-start.1 = ((f32[24,8,128]{2,1,0:T(8,128)}), f32[24,8,128]{2,1,0:T(8,128)S(1)}, u32[]{:S(2)}, u32[]{:S(2)}) async-start(f32[24,8,128]{2,1,0:T(8,128)} %get-tuple-element.26), calls=%async_computation.1 | async-start | bytes 196608 | tf_op jit(solution)/shard_map/all_to_all | solution.py:29
  88.6 0.8 copy-start.1
  89.4 9.8 %collective-permute-start = (bf16[200,1024]{1,0:T(8,128)(2,1)S(1)}, bf16[200,1024]{1,0:T(8,128)(2,1)S(1)}, u32[]{:S(2)}, u32[]{:S(2)}) collective-permute-start(bf16[200,1024]{1,0:T(8,128)(2,1)S(1)} %get-tuple-element.32), channel_id=1, source_target_pairs={{0,384},{384,0},{1,385},{385,1},{2,386},{386,2},{3,387},{387,3},{4... | collective-permute-start | bytes 1228808 | tf_op jit(solution)/shard_map/ppermute | solution.py:34
  100.2 7.9 %copy-start.2 = (bf16[264,1024]{1,0:T(8,128)(2,1)S(1)}, bf16[264,1024]{1,0:T(8,128)(2,1)}, u32[]{:S(2)}) copy-start(bf16[264,1024]{1,0:T(8,128)(2,1)} %copy-done.1) | copy-start | bytes 1622020
  100.2 47.4 %all-to-all-start.3 = ((bf16[12,136,128]{2,1,0:T(8,128)(2,1)}), bf16[12,136,128]{2,1,0:T(8,128)(2,1)S(1)}, u32[]{:S(2)}, u32[]{:S(2)}) async-start(bf16[12,136,128]{2,1,0:T(8,128)(2,1)} %shard_map.62), calls=%async_computation.3 | async-start | bytes 835584 | tf_op jit(solution)/shard_map/all_to_all | solution.py:29
  108.1 3.8 %collective-permute-start.1 = (bf16[264,1024]{1,0:T(8,128)(2,1)S(1)}, bf16[264,1024]{1,0:T(8,128)(2,1)S(1)}, u32[]{:S(2)}, u32[]{:S(2)}) collective-permute-start(bf16[264,1024]{1,0:T(8,128)(2,1)S(1)} %copy-done.2), channel_id=1, source_target_pairs={{0,1},{1,0},{2,3},{3,2},{4,5},{5,4},{6,7},{7,6},{8,9},{9,8},{10,11... | collective-permute-start | bytes 1622024 | tf_op jit(solution)/shard_map/ppermute | solution.py:34
  112.7 12.1 %collective-permute-start.2 = (bf16[136,1024]{1,0:T(8,128)(2,1)S(1)}, bf16[136,1024]{1,0:T(8,128)(2,1)S(1)}, u32[]{:S(2)}, u32[]{:S(2)}) collective-permute-start(bf16[136,1024]{1,0:T(8,128)(2,1)S(1)} %get-tuple-element.37), channel_id=1, source_target_pairs={{0,2},{2,0},{1,3},{3,1},{4,6},{6,4},{5,7},{7,5},{8,10},{10,8},{9,1... | collective-permute-start | bytes 835592 | tf_op jit(solution)/shard_map/ppermute | solution.py:34
  125.5 8.6 %collective-permute-start.3 = (bf16[48,1024]{1,0:T(8,128)(2,1)S(1)}, bf16[48,1024]{1,0:T(8,128)(2,1)S(1)}, u32[]{:S(2)}, u32[]{:S(2)}) collective-permute-start(bf16[48,1024]{1,0:T(8,128)(2,1)S(1)} %get-tuple-element.41), channel_id=1, source_target_pairs={{0,4},{4,8},{8,12},{12,16},{16,20},{20,24},{24,28},{28,0},{1,5},{5... | collective-permute-start | bytes 294920 | tf_op jit(solution)/shard_map/ppermute | solution.py:34
  127.9 6.2 %collective-permute-start.4 = (bf16[32,1024]{1,0:T(8,128)(2,1)S(1)}, bf16[32,1024]{1,0:T(8,128)(2,1)S(1)}, u32[]{:S(2)}, u32[]{:S(2)}) collective-permute-start(bf16[32,1024]{1,0:T(8,128)(2,1)S(1)} %get-tuple-element.42), channel_id=1, source_target_pairs={{0,28},{4,0},{8,4},{12,8},{16,12},{20,16},{24,20},{28,24},{1,29},{... | collective-permute-start | bytes 196616 | tf_op jit(solution)/shard_map/ppermute | solution.py:34
  134.2 9.1 %collective-permute-start.5 = (bf16[16,1024]{1,0:T(8,128)(2,1)S(1)}, bf16[16,1024]{1,0:T(8,128)(2,1)S(1)}, u32[]{:S(2)}, u32[]{:S(2)}) collective-permute-start(bf16[16,1024]{1,0:T(8,128)(2,1)S(1)} %get-tuple-element.44), channel_id=1, source_target_pairs={{0,12},{4,16},{8,20},{12,24},{16,28},{20,0},{24,4},{28,8},{1,13},{... | collective-permute-start | bytes 98312 | tf_op jit(solution)/shard_map/ppermute | solution.py:34
  137.5 9.4 %collective-permute-start.6 = (bf16[16,1024]{1,0:T(8,128)(2,1)S(1)}, bf16[16,1024]{1,0:T(8,128)(2,1)S(1)}, u32[]{:S(2)}, u32[]{:S(2)}) collective-permute-start(bf16[16,1024]{1,0:T(8,128)(2,1)S(1)} %get-tuple-element.45), channel_id=1, source_target_pairs={{0,20},{4,24},{8,28},{12,0},{16,4},{20,8},{24,12},{28,16},{1,21},{... | collective-permute-start | bytes 98312 | tf_op jit(solution)/shard_map/ppermute | solution.py:34

commit v7 on v6

--- a/solution.py
+++ b/solution.py
@@ -64,6 +64,16 @@
     return jnp.where(at == 0, hi, jnp.where(at == 1, mid, jnp.where(at == 2, low, 0.0))).astype(BF16)
 
 
+def lane_pieces(v, lane):
+    v = jnp.broadcast_to(v, (TAIL, LANES))
+    hi = v.astype(BF16).astype(F32)
+    mid = (v - hi).astype(BF16).astype(F32)
+    low = v - hi - mid
+    row = lax.broadcasted_iota(jnp.int32, (TAIL, LANES), 0)
+    part = jnp.where(row == 0, hi, jnp.where(row == 1, mid, jnp.where(row == 2, low, 0.0)))
+    return jnp.where(lanes((TAIL, LANES)) == lane, part, 0.0)
+
+
 def value(tile):
     row = tile.astype(F32)[0:1]
     return jnp.sum(jnp.where(lanes((1, LANES)) < 3, row, 0.0))
@@ -96,8 +106,8 @@
     peak = jnp.max(s, axis=0, keepdims=True)
     col = peak + jnp.log(jnp.sum(jnp.exp(s - peak), axis=0, keepdims=True))
     for k in range(COLS // LANES):
-        tile = jnp.broadcast_to(col[:, k * LANES : (k + 1) * LANES], (N_ROW, LANES))
-        for n in range(N_ROW):
+        tile = jnp.broadcast_to(col[:, k * LANES : (k + 1) * LANES], (N_Z, LANES))
+        for n in range(N_Z):
             cpack[n, k : k + 1, :] = tile[n : n + 1]
     peak = jnp.max(s, axis=1, keepdims=True)
     row = peak + jnp.log(jnp.sum(jnp.exp(s - peak), axis=1, keepdims=True))
@@ -108,30 +118,25 @@
     rpack[4:5, :] = jnp.full((1, LANES), diag)
 
 
-def merge_kernel(col, near, clse, pack):
-    lse = merged([col[n] for n in range(N_ROW)])
-    total = jnp.zeros((1, LANES), F32)
-    for k in range(COLS // LANES):
-        clse[:, k * LANES : (k + 1) * LANES] = jnp.broadcast_to(lse[k : k + 1], (8, LANES))
-        total = total + lse[k : k + 1]
-    total = jnp.full((1, LANES), jnp.sum(total))
+def merge_kernel(col, near, xpack, pack):
+    xpack[0:3, :] = merged([col[n] for n in range(N_Z)])[0:3]
     rows = merged([near[n] for n in range(N_XH * N_C)])
     diag = sum(near[n, 4:5, :] for n in range(N_XH * N_C))
     for n in range(N_Y):
         pack[n, 0:4, :] = rows[0:4]
         pack[n, 4:5, :] = diag
-        pack[n, 5:6, :] = total
-
-
-def grad_kernel(idx, fac, sc, im, tx, got, clse, iaway, taway, there, scal, delta, part):
+
+
+def grad_kernel(idx, fac, sc, im, tx, got, gotx, iaway, taway, there, scal, delta, part):
     rows = merged([got[n] for n in range(N_Y)])[0:4]
     diag = sum(got[n, 4:5, :] for n in range(N_Y))
-    total = sum(got[n, 5:6, :] for n in range(N_Y))
+    cols = merged([gotx[n] for n in range(N_XL)])[0:3]
+    total = jnp.full((1, LANES), jnp.sum(cols))
     row_loss = jnp.full((1, LANES), jnp.sum(rows)) - 2.0 * diag
     scal[0:8, :] = jnp.broadcast_to(row_loss, (8, LANES))
     scal[8:16, :] = jnp.broadcast_to(total, (8, LANES))
     c, xl = idx[2], idx[5]
-    col = clse[0:1, :]
+    col = jnp.concatenate([cols[k : k + 1] for k in range(COLS // LANES)], axis=1)
     for k in range(ROWS // LANES):
         s = sc[k * LANES : (k + 1) * LANES, :]
         tile = jnp.broadcast_to(rows[k : k + 1], (LANES, LANES)).T
@@ -178,10 +183,15 @@
         out[z, SLABS * EACH :, :] = tile
 
 
-def ring_kernel(idx, total, keep, got, ahead, behind, near, out):
+def ring_kernel(idx, total, keep, got, ahead, behind, near, vec):
     y = idx[4]
     half = ROWS // 4
-    out[...] = total[...] + value(got[half : half + TAIL, 0:LANES])
+    whole = total[0:1, :] + value(got[half : half + TAIL, 0:LANES])
+    tile = lane_pieces(whole, y)
+    vec[...] = tile
+    for ref, at in ((ahead, 3 * EACH), (behind, 2 * EACH)):
+        ref[at:, :] = jnp.zeros((TAIL, WIDTH), BF16)
+        ref[at:, 0:LANES] = tile.astype(BF16)
 
     def block(k):
         at = pl.multiple_of(((y + k) & (N_Y - 1)) * EACH, EACH)
@@ -195,26 +205,33 @@
         near[n * EACH : (n + 1) * EACH, :] = block(k)
 
 
-def side_kernel(near, low, high, up, down, mid):
+def side_kernel(near, vec, low, high, up, down, mid, out):
     e = EACH
     mid[...] = near[0:e, :] + low[0:e, :].astype(F32) + high[0:e, :].astype(F32)
-    up[...] = (near[e : 2 * e, :] + low[e : 2 * e, :].astype(F32) + high[e:, :].astype(F32)).astype(BF16)
-    down[...] = (near[2 * e :, :] + low[2 * e :, :].astype(F32)).astype(BF16)
-
-
-def image_kernel(mid, left, right, out):
-    out[...] = (mid[...] + left[...].astype(F32) + right[...].astype(F32)).reshape(EACH, 1, WIDTH)
-
-
-def final_kernel(got, total, out, loss):
+    up[0:e, :] = (near[e : 2 * e, :] + low[e : 2 * e, :].astype(F32) + high[e : 2 * e, :].astype(F32)).astype(BF16)
+    down[0:e, :] = (near[2 * e :, :] + low[2 * e : 3 * e, :].astype(F32)).astype(BF16)
+    tile = vec[...] + low[3 * e :, 0:LANES].astype(F32) + high[2 * e :, 0:LANES].astype(F32)
+    out[...] = tile
+    for ref in (up, down):
+        ref[e:, :] = jnp.zeros((TAIL, WIDTH), BF16)
+        ref[e:, 0:LANES] = tile.astype(BF16)
+
+
+def final_kernel(idx, mid, vec, left, right, got, image, text, loss):
+    e = EACH
+    image[...] = (mid[...] + left[0:e, :].astype(F32) + right[0:e, :].astype(F32)).reshape(e, 1, WIDTH)
+    far = (idx[4] + N_Y // 2) & (N_Y - 1)
+    new = jnp.where(lanes((TAIL, LANES)) == far, 0.0, left[e:, 0:LANES].astype(F32))
+    tile = vec[...] + new + right[e:, 0:LANES].astype(F32)
+    col_total = jnp.sum(tile[0:1] + tile[1:2] + tile[2:3])
     acc = got[0].astype(F32)
     for z in range(1, N_Z):
         acc = acc + got[z].astype(F32)
-    row = acc[SLABS * EACH :]
-    acc = jnp.concatenate([acc[k * EACH : (k + 1) * EACH] for k in range(SLABS)], axis=1)
-    out[...] = acc.reshape(EACH, 1, WIDTH)
-    whole = jnp.sum(jnp.where(lanes((1, LANES)) < 3, row[0:1], 0.0))
-    loss[0, 0] = (jnp.max(total[...]) + whole) / (2.0 * PAIRS)
+    row = acc[SLABS * e :]
+    acc = jnp.concatenate([acc[k * e : (k + 1) * e] for k in range(SLABS)], axis=1)
+    text[...] = acc.reshape(e, 1, WIDTH)
+    row_total = jnp.sum(jnp.where(lanes((1, LANES)) < 3, row[0:1], 0.0))
+    loss[0, 0] = (col_total + row_total) / (2.0 * PAIRS)
 
 
 def body(image_emb, text_emb, logit_scale):
@@ -226,14 +243,15 @@
     texts = lax.all_gather(texts, "z").reshape(COLS, WIDTH)
     scores, cpack, rpack = call(
         score_kernel,
-        [((ROWS, COLS), F32), ((N_ROW, 8, LANES), F32), ((8, LANES), F32)],
+        [((ROWS, COLS), F32), ((N_Z, 8, LANES), F32), ((8, LANES), F32)],
         [],
         idx, logit_scale, images, texts,
     )
-    col_got = exchange(cpack, ROW)
+    col_got = exchange(cpack, "z")
     near = lax.all_gather(rpack, ("xh", "c"))
-    col_lse, ypack = call(merge_kernel, [((8, COLS), F32), ((N_Y, 8, LANES), F32)], [], col_got, near)
+    xpack, ypack = call(merge_kernel, [((8, LANES), F32), ((N_Y, 8, LANES), F32)], [], col_got, near)
     row_got = exchange(ypack, "y")
+    col_got = lax.all_gather(xpack, "xl")
     iaway, taway, there, scal, delta = call(
         grad_kernel,
         [
@@ -244,7 +262,7 @@
             ((N_C, ROWS // 2, COLS), BF16),
         ],
         [((N_Z, N_XL, EACH, WIDTH), F32)],
-        idx, logit_scale, scores, images, texts, row_got, col_lse,
+        idx, logit_scale, scores, images, texts, row_got, col_got,
     )
     tcame = shift(taway, "xl", 1)
     icame = shift(iaway, "c", 1)
@@ -258,24 +276,33 @@
     xcame = shift(xaway, "xh", 1)
     (tpack,) = call(text_kernel, [((N_Z, SLABS * EACH + TAIL, LANES), BF16)], [], scal, there, tcame)
     text_got = exchange(tpack, "z")
-    ahead, behind, near3, total = call(
+    ahead, behind, near3, vec = call(
         ring_kernel,
-        [((3 * EACH, WIDTH), BF16), ((2 * EACH, WIDTH), BF16), ((3 * EACH, WIDTH), F32), ((8, LANES), F32)],
+        [
+            ((3 * EACH + TAIL, WIDTH), BF16),
+            ((2 * EACH + TAIL, WIDTH), BF16),
+            ((3 * EACH, WIDTH), F32),
+            ((TAIL, LANES), F32),
+        ],
         [],
         idx, total, keep, xcame,
     )
     low = shift(ahead, "y", 1)
     high = shift(behind, "y", 7)
-    up, down, mid = call(
+    up, down, mid, vec = call(
         side_kernel,
-        [((EACH, WIDTH), BF16), ((EACH, WIDTH), BF16), ((EACH, WIDTH), F32)],
-        [],
-        near3, low, high,
+        [((EACH + TAIL, WIDTH), BF16), ((EACH + TAIL, WIDTH), BF16), ((EACH, WIDTH), F32), ((TAIL, LANES), F32)],
+        [],
+        near3, vec, low, high,
     )
     left = shift(up, "y", 3)
     right = shift(down, "y", 5)
-    (image_grad,) = call(image_kernel, [((EACH, 1, WIDTH), F32)], [], mid, left, right)
-    text_grad, loss = call(final_kernel, [((EACH, 1, WIDTH), F32), ((1, 1), F32)], [], text_got, total)
+    image_grad, text_grad, loss = call(
+        final_kernel,
+        [((EACH, 1, WIDTH), F32), ((EACH, 1, WIDTH), F32), ((1, 1), F32)],
+        [],
+        idx, mid, vec, left, right, text_got,
+    )
     return loss[0, 0], image_grad, text_grad
 
 

time: 149 us -> 151 us (1.013)
  the two profiles are of different devices: /device:TPU:14 before, /device:TPU:4 now
where the time goes in v7:
time: 151 us
  starting transfers between devices  54.3 us (36%)
  blocking collectives  50.1 us (33%)
  waiting for transfers between devices  32.5 us (22%)
  Pallas kernels  10.5 us (7%)
  local copies, waits for them, and re-layouts  1.64 us (1%)
    all_gather x1, blocking collectives, body(): texts = lax.all_gather(texts, 'z').reshape(COLS, WIDTH)  34.4 us
    all_to_all x4, starting transfers between devices, exchange(): return lax.all_to_all(x, axes, 0, 0, tiled=False)  31.6 us
    ppermute x7, waiting for transfers between devices, shift(): return lax.ppermute(x, axis, [(i, (i + k) % n) for i in range(n)])  24.8 us
    ppermute x7, starting transfers between devices, shift(): return lax.ppermute(x, axis, [(i, (i + k) % n) for i in range(n)])  22.7 us
    pallas_call x10, Pallas kernels, call(): pl.pallas_call(kernel, out_shape=[jax.ShapeDtypeStruct(s, d) for s, d in...  10.5 us
    all_to_all x4, waiting for transfers between devices, exchange(): return lax.all_to_all(x, axes, 0, 0, tiled=False)  7.72 us
    all_gather x1, blocking collectives, body(): near = lax.all_gather(rpack, ('xh', 'c'))  6.71 us
    all_gather x1, blocking collectives, body(): texts = lax.all_gather(text_emb.reshape(EACH, WIDTH), 'xl')  4.65 us
  transfers between devices with their start and end apart: 11, of which 8 were waited for; matrix products, arithmetic and copies ran while one was open for 0% of the time, Pallas kernels for 2%

profile of v7, /device:TPU:4, one launch (start us, length us, event | category | flops | bytes accessed | tf_op | source)
XLA Modules:
  0.0 150.6 jit_solution(6617695667006773780)
XLA Ops:
  0.6 0.0 copy-start
  0.6 0.7 copy-done
  1.4 1.1 shard_map.58
  2.5 13.1 %all-to-all-start = ((bf16[32,16,1024]{2,1,0:T(8,128)(2,1)}), bf16[32,16,1024]{2,1,0:T(8,128)(2,1)S(1)}, u32[]{:S(2)}, u32[]{:S(2)}) async-start(bf16[32,16,1024]{2,1,0:T(8,128)(2,1)} %shard_map.58), calls=%async_computation | async-start | bytes 2097152 | tf_op jit(solution)/shard_map/all_to_all | solution.py:29
  15.6 0.0 copy-start.3
  16.3 0.1 stack.27.idx
  16.4 0.0 copy-done.3
  16.4 4.6 %all-gather = bf16[32,1,1024]{2,0,1:T(8,128)(2,1)S(1)} all-gather(bf16[16,1,1024]{2,0,1:T(8,128)(2,1)S(1)} %copy-done.3), channel_id=2, replica_groups=mesh['xl'=2,'z'=12,'y'=8,'xh'=2,'c'=2] {'xl'}, dimensions={0}, use_global_device_ids=true | all-gather | bytes 98304 | tf_op jit(solution)/shard_map/all_gather | solution.py:242
  21.1 34.4 %all-gather.1 = bf16[24,16,1024]{2,1,0:T(8,128)(2,1)S(1)} all-gather(bf16[2,16,1024]{2,1,0:T(8,128)(2,1)S(1)} %bitcast.21), channel_id=3, replica_groups=mesh['xl'=2,'z'=12,'y'=8,'xh'=2,'c'=2] {'z'}, dimensions={0}, use_global_device_ids=true | all-gather | bytes 851968 | tf_op jit(solution)/shard_map/all_gather | solution.py:243
  55.5 0.0 all-to-all-done
  55.5 2.2 %shard_map.59 = (f32[512,384]{1,0:T(8,128)S(1)}, f32[12,8,128]{2,1,0:T(8,128)}, f32[8,128]{1,0:T(8,128)S(1)}) custom-call(s32[6]{0:T(128)S(1)} %stack.27.idx, f32[1]{0:T(128)S(6)} %copy.6.fac, bf16[512,1024]{1,0:T(8,128)(2,1)S(1)} %bitcast.16, bf16[384,1024]{1,0:T(8,128)(2,1)S(1)} %bitcast.13), custom_call_target="tpu_custom_call" | custom-call | tf_op jit(solution)/shard_map/pallas_call | solution.py:39
  57.6 3.5 %all-to-all-start.1 = ((f32[12,8,128]{2,1,0:T(8,128)}), f32[12,8,128]{2,1,0:T(8,128)S(1)}, u32[]{:S(2)}, u32[]{:S(2)}) async-start(f32[12,8,128]{2,1,0:T(8,128)} %get-tuple-element.28), calls=%async_computation.1 | async-start | bytes 98304 | tf_op jit(solution)/shard_map/all_to_all | solution.py:29
  61.2 6.7 %all-gather.2 = f32[32,128]{1,0:T(8,128)S(1)} all-gather(f32[8,128]{1,0:T(8,128)S(1)} %get-tuple-element.29), channel_id=4, replica_groups=mesh['xl'=2,'z'=12,'y'=8,'xh'=2,'c'=2] {'xh','c'}, dimensions={0}, use_global_device_ids=true | all-gather | bytes 20480 | tf_op jit(solution)/shard_map/all_gather | solution.py:251
  67.9 4.0 %all-to-all-done.1.col = f32[12,8,128]{2,1,0:T(8,128)S(1)} async-done(((f32[12,8,128]{2,1,0:T(8,128)}), f32[12,8,128]{2,1,0:T(8,128)S(1)}, u32[]{:S(2)}, u32[]{:S(2)}) %all-to-all-start.1) | async-done | bytes 49184 | tf_op jit(solution)/shard_map/all_to_all | solution.py:29
  71.9 0.6 shard_map.60
  72.5 7.1 %all-to-all-start.2 = ((f32[8,8,128]{2,1,0:T(8,128)}), f32[8,8,128]{2,1,0:T(8,128)S(1)}, u32[]{:S(2)}, u32[]{:S(2)}) async-start(f32[8,8,128]{2,1,0:T(8,128)} %get-tuple-element.30), calls=%async_computation.2 | async-start | bytes 65536 | tf_op jit(solution)/shard_map/all_to_all | solution.py:29
  79.6 4.3 %all-gather.3 = f32[16,128]{1,0:T(8,128)S(1)} all-gather(f32[8,128]{1,0:T(8,128)S(1)} %get-tuple-element.31), channel_id=5, replica_groups=mesh['xl'=2,'z'=12,'y'=8,'xh'=2,'c'=2] {'xl'}, dimensions={0}, use_global_device_ids=true | all-gather | bytes 12288 | tf_op jit(solution)/shard_map/all_gather | solution.py:254
  84.0 3.7 %all-to-all-done.2.got = f32[8,8,128]{2,1,0:T(8,128)S(1)} async-done(((f32[8,8,128]{2,1,0:T(8,128)}), f32[8,8,128]{2,1,0:T(8,128)S(1)}, u32[]{:S(2)}, u32[]{:S(2)}) %all-to-all-start.2) | async-done | bytes 32800 | tf_op jit(solution)/shard_map/all_to_all | solution.py:29
  87.6 1.9 %shard_map.61 = (bf16[264,1024]{1,0:T(8,128)(2,1)S(1)}, bf16[200,1024]{1,0:T(8,128)(2,1)S(1)}, f32[192,1024]{1,0:T(8,128)S(1)}, f32[16,128]{1,0:T(8,128)S(1)}, bf16[2,256,384]{2,1,0:T(8,128)(2,1)S(1)}) custom-call(s32[6]{0:T(128)S(1)} %stack.27.idx, f32[1]{0:T(128)S(6)} %copy.6.fac, f32[512,384]{1,0:T(8,128)S(1)} %get-tuple-element.27.sc, ...), custom_call_target="tpu_custom_call" | custom-call | tf_op jit(solution)/shard_map/pallas_call | solution.py:39
  89.6 0.0 copy-start.1
  89.6 0.8 copy-done.1
  90.4 2.9 %collective-permute-start.6 = (bf16[200,1024]{1,0:T(8,128)(2,1)S(1)}, bf16[200,1024]{1,0:T(8,128)(2,1)S(1)}, u32[]{:S(2)}, u32[]{:S(2)}) collective-permute-start(bf16[200,1024]{1,0:T(8,128)(2,1)S(1)} %get-tuple-element.47), channel_id=1, source_target_pairs={{0,384},{384,0},{1,385},{385,1},{2,386},{386,2},{3,387},{387,3},{4... | collective-permute-start | bytes 1228808 | tf_op jit(solution)/shard_map/ppermute | solution.py:34
  93.3 6.9 %collective-permute-done.6.came = bf16[200,1024]{1,0:T(8,128)(2,1)S(1)} collective-permute-done((bf16[200,1024]{1,0:T(8,128)(2,1)S(1)}, bf16[200,1024]{1,0:T(8,128)(2,1)S(1)}, u32[]{:S(2)}, u32[]{:S(2)}) %collective-permute-start.6) | collective-permute-done | bytes 409632 | tf_op jit(solution)/shard_map/ppermute | solution.py:34
  100.2 1.0 shard_map.66
  101.2 0.0 copy-start.2
  101.2 7.9 %all-to-all-start.3 = ((bf16[12,136,128]{2,1,0:T(8,128)(2,1)}), bf16[12,136,128]{2,1,0:T(8,128)(2,1)S(1)}, u32[]{:S(2)}, u32[]{:S(2)}) async-start(bf16[12,136,128]{2,1,0:T(8,128)(2,1)} %shard_map.66), calls=%async_computation.3 | async-start | bytes 835584 | tf_op jit(solution)/shard_map/all_to_all | solution.py:29
  109.1 0.0 copy-done.2
  109.1 1.9 %collective-permute-start = (bf16[264,1024]{1,0:T(8,128)(2,1)S(1)}, bf16[264,1024]{1,0:T(8,128)(2,1)S(1)}, u32[]{:S(2)}, u32[]{:S(2)}) collective-permute-start(bf16[264,1024]{1,0:T(8,128)(2,1)S(1)} %copy-done.2), channel_id=1, source_target_pairs={{0,1},{1,0},{2,3},{3,2},{4,5},{5,4},{6,7},{7,6},{8,9},{9,8},{10,11... | collective-permute-start | bytes 1622024 | tf_op jit(solution)/shard_map/ppermute | solution.py:34
  111.1 1.0 shard_map.62.here
  112.0 0.9 collective-permute-done.came
  113.0 0.7 shard_map.63
  113.7 2.0 %collective-permute-start.1 = (bf16[136,1024]{1,0:T(8,128)(2,1)S(1)}, bf16[136,1024]{1,0:T(8,128)(2,1)S(1)}, u32[]{:S(2)}, u32[]{:S(2)}) collective-permute-start(bf16[136,1024]{1,0:T(8,128)(2,1)S(1)} %get-tuple-element.37), channel_id=1, source_target_pairs={{0,2},{2,0},{1,3},{3,1},{4,6},{6,4},{5,7},{7,5},{8,10},{10,8},{9,1... | collective-permute-start | bytes 835592 | tf_op jit(solution)/shard_map/ppermute | solution.py:34
  115.7 10.1 %collective-permute-done.1.got = bf16[136,1024]{1,0:T(8,128)(2,1)S(1)} collective-permute-done((bf16[136,1024]{1,0:T(8,128)(2,1)S(1)}, bf16[136,1024]{1,0:T(8,128)(2,1)S(1)}, u32[]{:S(2)}, u32[]{:S(2)}) %collective-permute-start.1) | collective-permute-done | bytes 278560 | tf_op jit(solution)/shard_map/ppermute | solution.py:34
  125.8 0.7 shard_map.64
  126.5 2.6 %collective-permute-start.2 = (bf16[56,1024]{1,0:T(8,128)(2,1)S(1)}, bf16[56,1024]{1,0:T(8,128)(2,1)S(1)}, u32[]{:S(2)}, u32[]{:S(2)}) collective-permute-start(bf16[56,1024]{1,0:T(8,128)(2,1)S(1)} %get-tuple-element.40), channel_id=1, source_target_pairs={{0,4},{4,8},{8,12},{12,16},{16,20},{20,24},{24,28},{28,0},{1,5},{5... | collective-permute-start | bytes 344072 | tf_op jit(solution)/shard_map/ppermute | solution.py:34
  129.1 4.5 %collective-permute-start.3 = (bf16[40,1024]{1,0:T(8,128)(2,1)S(1)}, bf16[40,1024]{1,0:T(8,128)(2,1)S(1)}, u32[]{:S(2)}, u32[]{:S(2)}) collective-permute-start(bf16[40,1024]{1,0:T(8,128)(2,1)S(1)} %get-tuple-element.41), channel_id=1, source_target_pairs={{0,28},{4,0},{8,4},{12,8},{16,12},{20,16},{24,20},{28,24},{1,29},{... | collective-permute-start | bytes 245768 | tf_op jit(solution)/shard_map/ppermute | solution.py:34
  133.6 2.0 %collective-permute-done.3.high = bf16[40,1024]{1,0:T(8,128)(2,1)S(1)} collective-permute-done((bf16[40,1024]{1,0:T(8,128)(2,1)S(1)}, bf16[40,1024]{1,0:T(8,128)(2,1)S(1)}, u32[]{:S(2)}, u32[]{:S(2)}) %collective-permute-start.3) | collective-permute-done | bytes 81952 | tf_op jit(solution)/shard_map/ppermute | solution.py:34
  135.6 0.0 collective-permute-done.2.low
  135.6 4.8 %collective-permute-start.4 = (bf16[24,1024]{1,0:T(8,128)(2,1)S(1)}, bf16[24,1024]{1,0:T(8,128)(2,1)S(1)}, u32[]{:S(2)}, u32[]{:S(2)}) collective-permute-start(bf16[24,1024]{1,0:T(8,128)(2,1)S(1)} %get-tuple-element.44), channel_id=1, source_target_pairs={{0,12},{4,16},{8,20},{12,24},{16,28},{20,0},{24,4},{28,8},{1,13},{... | collective-permute-start | bytes 147464 | tf_op jit(solution)/shard_map/ppermute | solution.py:34
  140.5 4.1 %collective-permute-start.5 = (bf16[24,1024]{1,0:T(8,128)(2,1)S(1)}, bf16[24,1024]{1,0:T(8,128)(2,1)S(1)}, u32[]{:S(2)}, u32[]{:S(2)}) collective-permute-start(bf16[24,1024]{1,0:T(8,128)(2,1)S(1)} %get-tuple-element.45), channel_id=1, source_target_pairs={{0,20},{4,24},{8,28},{12,0},{16,4},{20,8},{24,12},{28,16},{1,21},{... | collective-permute-start | bytes 147464 | tf_op jit(solution)/shard_map/ppermute | solution.py:34
  144.5 0.1 collective-permute-done.4.left
  144.6 4.7 %collective-permute-done.5.right = bf16[24,1024]{1,0:T(8,128)(2,1)S(1)} collective-permute-done((bf16[24,1024]{1,0:T(8,128)(2,1)S(1)}, bf16[24,1024]{1,0:T(8,128)(2,1)S(1)}, u32[]{:S(2)}, u32[]{:S(2)}) %collective-permute-start.5) | collective-permute-done | bytes 49184 | tf_op jit(solution)/shard_map/ppermute | solution.py:34
  149.3 0.0 all-to-all-done.3.got
  149.3 1.3 shard_map.67
  (1 shorter events, 0.0 us)
Async XLA Ops:
  0.6 0.8 copy-start
  2.5 53.0 %all-to-all-start = ((bf16[32,16,1024]{2,1,0:T(8,128)(2,1)}), bf16[32,16,1024]{2,1,0:T(8,128)(2,1)S(1)}, u32[]{:S(2)}, u32[]{:S(2)}) async-start(bf16[32,16,1024]{2,1,0:T(8,128)(2,1)} %shard_map.58), calls=%async_computation | async-start | bytes 2097152 | tf_op jit(solution)/shard_map/all_to_all | solution.py:29
  15.6 0.8 copy-start.3
  57.6 14.2 %all-to-all-start.1 = ((f32[12,8,128]{2,1,0:T(8,128)}), f32[12,8,128]{2,1,0:T(8,128)S(1)}, u32[]{:S(2)}, u32[]{:S(2)}) async-start(f32[12,8,128]{2,1,0:T(8,128)} %get-tuple-element.28), calls=%async_computation.1 | async-start | bytes 98304 | tf_op jit(solution)/shard_map/all_to_all | solution.py:29
  72.5 15.1 %all-to-all-start.2 = ((f32[8,8,128]{2,1,0:T(8,128)}), f32[8,8,128]{2,1,0:T(8,128)S(1)}, u32[]{:S(2)}, u32[]{:S(2)}) async-start(f32[8,8,128]{2,1,0:T(8,128)} %get-tuple-element.30), calls=%async_computation.2 | async-start | bytes 65536 | tf_op jit(solution)/shard_map/all_to_all | solution.py:29
  89.6 0.8 copy-start.1
  90.4 9.8 %collective-permute-start.6 = (bf16[200,1024]{1,0:T(8,128)(2,1)S(1)}, bf16[200,1024]{1,0:T(8,128)(2,1)S(1)}, u32[]{:S(2)}, u32[]{:S(2)}) collective-permute-start(bf16[200,1024]{1,0:T(8,128)(2,1)S(1)} %get-tuple-element.47), channel_id=1, source_target_pairs={{0,384},{384,0},{1,385},{385,1},{2,386},{386,2},{3,387},{387,3},{4... | collective-permute-start | bytes 1228808 | tf_op jit(solution)/shard_map/ppermute | solution.py:34
  101.2 7.9 %copy-start.2 = (bf16[264,1024]{1,0:T(8,128)(2,1)S(1)}, bf16[264,1024]{1,0:T(8,128)(2,1)}, u32[]{:S(2)}) copy-start(bf16[264,1024]{1,0:T(8,128)(2,1)} %copy-done.1) | copy-start | bytes 1622020
  101.2 48.1 %all-to-all-start.3 = ((bf16[12,136,128]{2,1,0:T(8,128)(2,1)}), bf16[12,136,128]{2,1,0:T(8,128)(2,1)S(1)}, u32[]{:S(2)}, u32[]{:S(2)}) async-start(bf16[12,136,128]{2,1,0:T(8,128)(2,1)} %shard_map.66), calls=%async_computation.3 | async-start | bytes 835584 | tf_op jit(solution)/shard_map/all_to_all | solution.py:29
  109.1 3.8 %collective-permute-start = (bf16[264,1024]{1,0:T(8,128)(2,1)S(1)}, bf16[264,1024]{1,0:T(8,128)(2,1)S(1)}, u32[]{:S(2)}, u32[]{:S(2)}) collective-permute-start(bf16[264,1024]{1,0:T(8,128)(2,1)S(1)} %copy-done.2), channel_id=1, source_target_pairs={{0,1},{1,0},{2,3},{3,2},{4,5},{5,4},{6,7},{7,6},{8,9},{9,8},{10,11... | collective-permute-start | bytes 1622024 | tf_op jit(solution)/shard_map/ppermute | solution.py:34
  113.7 12.1 %collective-permute-start.1 = (bf16[136,1024]{1,0:T(8,128)(2,1)S(1)}, bf16[136,1024]{1,0:T(8,128)(2,1)S(1)}, u32[]{:S(2)}, u32[]{:S(2)}) collective-permute-start(bf16[136,1024]{1,0:T(8,128)(2,1)S(1)} %get-tuple-element.37), channel_id=1, source_target_pairs={{0,2},{2,0},{1,3},{3,1},{4,6},{6,4},{5,7},{7,5},{8,10},{10,8},{9,1... | collective-permute-start | bytes 835592 | tf_op jit(solution)/shard_map/ppermute | solution.py:34
  126.5 9.1 %collective-permute-start.2 = (bf16[56,1024]{1,0:T(8,128)(2,1)S(1)}, bf16[56,1024]{1,0:T(8,128)(2,1)S(1)}, u32[]{:S(2)}, u32[]{:S(2)}) collective-permute-start(bf16[56,1024]{1,0:T(8,128)(2,1)S(1)} %get-tuple-element.40), channel_id=1, source_target_pairs={{0,4},{4,8},{8,12},{12,16},{16,20},{20,24},{24,28},{28,0},{1,5},{5... | collective-permute-start | bytes 344072 | tf_op jit(solution)/shard_map/ppermute | solution.py:34
  129.1 6.5 %collective-permute-start.3 = (bf16[40,1024]{1,0:T(8,128)(2,1)S(1)}, bf16[40,1024]{1,0:T(8,128)(2,1)S(1)}, u32[]{:S(2)}, u32[]{:S(2)}) collective-permute-start(bf16[40,1024]{1,0:T(8,128)(2,1)S(1)} %get-tuple-element.41), channel_id=1, source_target_pairs={{0,28},{4,0},{8,4},{12,8},{16,12},{20,16},{24,20},{28,24},{1,29},{... | collective-permute-start | bytes 245768 | tf_op jit(solution)/shard_map/ppermute | solution.py:34
  135.6 9.0 %collective-permute-start.4 = (bf16[24,1024]{1,0:T(8,128)(2,1)S(1)}, bf16[24,1024]{1,0:T(8,128)(2,1)S(1)}, u32[]{:S(2)}, u32[]{:S(2)}) collective-permute-start(bf16[24,1024]{1,0:T(8,128)(2,1)S(1)} %get-tuple-element.44), channel_id=1, source_target_pairs={{0,12},{4,16},{8,20},{12,24},{16,28},{20,0},{24,4},{28,8},{1,13},{... | collective-permute-start | bytes 147464 | tf_op jit(solution)/shard_map/ppermute | solution.py:34
  140.5 8.8 %collective-permute-start.5 = (bf16[24,1024]{1,0:T(8,128)(2,1)S(1)}, bf16[24,1024]{1,0:T(8,128)(2,1)S(1)}, u32[]{:S(2)}, u32[]{:S(2)}) collective-permute-start(bf16[24,1024]{1,0:T(8,128)(2,1)S(1)} %get-tuple-element.45), channel_id=1, source_target_pairs={{0,20},{4,24},{8,28},{12,0},{16,4},{20,8},{24,12},{28,16},{1,21},{... | collective-permute-start | bytes 147464 | tf_op jit(solution)/shard_map/ppermute | solution.py:34

commit v8 on v6

--- a/solution.py
+++ b/solution.py
@@ -75,12 +75,15 @@
 
 
 def diagonal(idx, start, count):
+    z, c, y, xh, xl = (idx[n] for n in range(5))
     i = lax.broadcasted_iota(jnp.int32, (count, COLS), 0) + start
     j = lax.broadcasted_iota(jnp.int32, (count, COLS), 1)
-    i_dev = ((i >> 4) & 7) * (N_XH * N_C) + ((i >> 7) & 1) * N_C + (i >> 8)
-    j_dev = ((j >> 4) & 1) * N_Z + (j >> 5)
-    row_ids = (EACH * idx[0] + (i & 15)) * N_COL + i_dev
-    col_ids = (EACH * idx[1] + (j & 15)) * N_ROW + j_dev
+    i_dev = ((i >> 4) & 7) * (N_XH * N_C) + ((i >> 7) & 1) * N_C + c
+    i_row = (i >> 8) * N_Z + z
+    j_dev = xl * N_Z + (j >> 5)
+    j_col = y * (N_XH * N_C) + xh * N_C + ((j >> 4) & 1)
+    row_ids = (EACH * i_row + (i & 15)) * N_COL + i_dev
+    col_ids = (EACH * j_col + (j & 15)) * N_ROW + j_dev
     return row_ids == col_ids
 
 
@@ -115,8 +118,8 @@
         clse[:, k * LANES : (k + 1) * LANES] = jnp.broadcast_to(lse[k : k + 1], (8, LANES))
         total = total + lse[k : k + 1]
     total = jnp.full((1, LANES), jnp.sum(total))
-    rows = merged([near[n] for n in range(N_XH * N_C)])
-    diag = sum(near[n, 4:5, :] for n in range(N_XH * N_C))
+    rows = merged([near[n] for n in range(N_XL * N_XH)])
+    diag = sum(near[n, 4:5, :] for n in range(N_XL * N_XH))
     for n in range(N_Y):
         pack[n, 0:4, :] = rows[0:4]
         pack[n, 4:5, :] = diag
@@ -130,7 +133,7 @@
     row_loss = jnp.full((1, LANES), jnp.sum(rows)) - 2.0 * diag
     scal[0:8, :] = jnp.broadcast_to(row_loss, (8, LANES))
     scal[8:16, :] = jnp.broadcast_to(total, (8, LANES))
-    c, xl = idx[2], idx[5]
+    c, xl = idx[1], idx[4]
     col = clse[0:1, :]
     for k in range(ROWS // LANES):
         s = sc[k * LANES : (k + 1) * LANES, :]
@@ -139,20 +142,20 @@
         eye = diagonal(idx, k * LANES, LANES)
         d = jnp.exp(s - lse) + jnp.exp(s - col) - jnp.where(eye, 2.0, 0.0)
         delta[k // 2, (k % 2) * LANES : (k % 2 + 1) * LANES, :] = (fac[0] * d).astype(BF16)
-    iaway[0 : ROWS // 2, :] = jnp.dot(delta[1 - c], tx[...], preferred_element_type=F32).astype(BF16)
+    iaway[0 : ROWS // 2, :] = jnp.dot(delta[1 - xl], tx[...], preferred_element_type=F32).astype(BF16)
     put_tail(iaway, ROWS // 2, total)
     whole = delta[...].reshape(ROWS, COLS)
     part[...] = lax.dot_general(
         whole, im[...], (((0,), (0,)), ((), ())), preferred_element_type=F32
-    ).reshape(N_Z, N_XL, EACH, WIDTH)
+    ).reshape(N_Z, N_C, EACH, WIDTH)
     for z in range(N_Z):
-        taway[z * EACH : (z + 1) * EACH, :] = part[z, 1 - xl].astype(BF16)
-        there[z * EACH : (z + 1) * EACH, :] = part[z, xl]
+        taway[z * EACH : (z + 1) * EACH, :] = part[z, 1 - c].astype(BF16)
+        there[z * EACH : (z + 1) * EACH, :] = part[z, c]
     put_tail(taway, COLS // 2, row_loss)
 
 
 def keep_kernel(idx, delta, tx, ihere):
-    ihere[...] = jnp.dot(delta[idx[2]], tx[...], preferred_element_type=F32)
+    ihere[...] = jnp.dot(delta[idx[4]], tx[...], preferred_element_type=F32)
 
 
 def across_kernel(idx, scal, here, came, away, keep, out):
@@ -178,32 +181,17 @@
         out[z, SLABS * EACH :, :] = tile
 
 
-def ring_kernel(idx, total, keep, got, ahead, behind, near, out):
-    y = idx[4]
+def pack_kernel(total, keep, got, pack, out):
     half = ROWS // 4
     out[...] = total[...] + value(got[half : half + TAIL, 0:LANES])
-
-    def block(k):
-        at = pl.multiple_of(((y + k) & (N_Y - 1)) * EACH, EACH)
-        return keep[pl.ds(at, EACH), :] + got[pl.ds(at, EACH), :].astype(F32)
-
-    for n, k in enumerate((1, 4, 6)):
-        ahead[n * EACH : (n + 1) * EACH, :] = block(k).astype(BF16)
-    for n, k in enumerate((7, 2)):
-        behind[n * EACH : (n + 1) * EACH, :] = block(k).astype(BF16)
-    for n, k in enumerate((0, 3, 5)):
-        near[n * EACH : (n + 1) * EACH, :] = block(k)
-
-
-def side_kernel(near, low, high, up, down, mid):
-    e = EACH
-    mid[...] = near[0:e, :] + low[0:e, :].astype(F32) + high[0:e, :].astype(F32)
-    up[...] = (near[e : 2 * e, :] + low[e : 2 * e, :].astype(F32) + high[e:, :].astype(F32)).astype(BF16)
-    down[...] = (near[2 * e :, :] + low[2 * e :, :].astype(F32)).astype(BF16)
-
-
-def image_kernel(mid, left, right, out):
-    out[...] = (mid[...] + left[...].astype(F32) + right[...].astype(F32)).reshape(EACH, 1, WIDTH)
+    pack[...] = (keep[...] + got[0:half, :].astype(F32)).astype(BF16).reshape(N_Y, EACH, WIDTH)
+
+
+def image_kernel(got, out):
+    acc = got[0].astype(F32)
+    for n in range(1, N_Y):
+        acc = acc + got[n].astype(F32)
+    out[...] = acc.reshape(EACH, 1, WIDTH)
 
 
 def final_kernel(got, total, out, loss):
@@ -218,11 +206,11 @@
 
 
 def body(image_emb, text_emb, logit_scale):
-    places = [lax.axis_index(a) for a in (ROW, COL, "c", "xh", "y", "xl")]
+    places = [lax.axis_index(a) for a in ("z", "c", "y", "xh", "xl")]
     idx = jnp.stack(places).astype(jnp.int32)
     (spread,) = call(spread_kernel, [((N_COL, EACH, WIDTH), BF16)], [], image_emb.reshape(EACH, WIDTH))
-    images = exchange(spread, ("c", "xh", "y")).reshape(ROWS, WIDTH)
-    texts = lax.all_gather(text_emb.reshape(EACH, WIDTH), "xl")
+    images = exchange(spread, ("xl", "xh", "y")).reshape(ROWS, WIDTH)
+    texts = lax.all_gather(text_emb.reshape(EACH, WIDTH), "c")
     texts = lax.all_gather(texts, "z").reshape(COLS, WIDTH)
     scores, cpack, rpack = call(
         score_kernel,
@@ -230,8 +218,8 @@
         [],
         idx, logit_scale, images, texts,
     )
-    col_got = exchange(cpack, ROW)
-    near = lax.all_gather(rpack, ("xh", "c"))
+    col_got = exchange(cpack, ("z", "c"))
+    near = lax.all_gather(rpack, ("xl", "xh"))
     col_lse, ypack = call(merge_kernel, [((8, COLS), F32), ((N_Y, 8, LANES), F32)], [], col_got, near)
     row_got = exchange(ypack, "y")
     iaway, taway, there, scal, delta = call(
@@ -241,13 +229,13 @@
             ((COLS // 2 + TAIL, WIDTH), BF16),
             ((COLS // 2, WIDTH), F32),
             ((16, LANES), F32),
-            ((N_C, ROWS // 2, COLS), BF16),
+            ((N_XL, ROWS // 2, COLS), BF16),
         ],
-        [((N_Z, N_XL, EACH, WIDTH), F32)],
+        [((N_Z, N_C, EACH, WIDTH), F32)],
         idx, logit_scale, scores, images, texts, row_got, col_lse,
     )
-    tcame = shift(taway, "xl", 1)
-    icame = shift(iaway, "c", 1)
+    tcame = shift(taway, "c", 1)
+    icame = shift(iaway, "xl", 1)
     (ihere,) = call(keep_kernel, [((ROWS // 2, WIDTH), F32)], [], idx, delta, texts)
     xaway, keep, total = call(
         across_kernel,
@@ -258,23 +246,9 @@
     xcame = shift(xaway, "xh", 1)
     (tpack,) = call(text_kernel, [((N_Z, SLABS * EACH + TAIL, LANES), BF16)], [], scal, there, tcame)
     text_got = exchange(tpack, "z")
-    ahead, behind, near3, total = call(
-        ring_kernel,
-        [((3 * EACH, WIDTH), BF16), ((2 * EACH, WIDTH), BF16), ((3 * EACH, WIDTH), F32), ((8, LANES), F32)],
-        [],
-        idx, total, keep, xcame,
-    )
-    low = shift(ahead, "y", 1)
-    high = shift(behind, "y", 7)
-    up, down, mid = call(
-        side_kernel,
-        [((EACH, WIDTH), BF16), ((EACH, WIDTH), BF16), ((EACH, WIDTH), F32)],
-        [],
-        near3, low, high,
-    )
-    left = shift(up, "y", 3)
-    right = shift(down, "y", 5)
-    (image_grad,) = call(image_kernel, [((EACH, 1, WIDTH), F32)], [], mid, left, right)
+    ypack, total = call(pack_kernel, [((N_Y, EACH, WIDTH), BF16), ((8, LANES), F32)], [], total, keep, xcame)
+    image_got = exchange(ypack, "y")
+    (image_grad,) = call(image_kernel, [((EACH, 1, WIDTH), F32)], [], image_got)
     text_grad, loss = call(final_kernel, [((EACH, 1, WIDTH), F32), ((1, 1), F32)], [], text_got, total)
     return loss[0, 0], image_grad, text_grad
 

time: 149 us -> 154 us (1.034)
  the two profiles are of different devices: /device:TPU:14 before, /device:TPU:8 now
where the time goes in v8:
time: 154 us
  blocking collectives  62.3 us (40%)
  starting transfers between devices  40.7 us (26%)
  waiting for transfers between devices  37.2 us (24%)
  Pallas kernels  10.4 us (7%)
  local copies, waits for them, and re-layouts  1.59 us (1%)
    all_gather x1, blocking collectives, body(): texts = lax.all_gather(texts, 'z').reshape(COLS, WIDTH)  34.3 us
    all_to_all x4, starting transfers between devices, exchange(): return lax.all_to_all(x, axes, 0, 0, tiled=False)  31.2 us
    all_to_all x4, waiting for transfers between devices, exchange(): return lax.all_to_all(x, axes, 0, 0, tiled=False)  21.4 us
    ppermute x3, waiting for transfers between devices, shift(): return lax.ppermute(x, axis, [(i, (i + k) % n) for i in range(n)])  15.8 us
    all_to_all x1, blocking collectives, exchange(): return lax.all_to_all(x, axes, 0, 0, tiled=False)  13.5 us
    all_gather x1, blocking collectives, body(): near = lax.all_gather(rpack, ('xl', 'xh'))  12.7 us
    pallas_call x10, Pallas kernels, call(): pl.pallas_call(kernel, out_shape=[jax.ShapeDtypeStruct(s, d) for s, d in...  10.4 us
    ppermute x3, starting transfers between devices, shift(): return lax.ppermute(x, axis, [(i, (i + k) % n) for i in range(n)])  9.46 us
  transfers between devices with their start and end apart: 7, of which 5 were waited for; matrix products, arithmetic and copies ran while one was open for 0% of the time, Pallas kernels for 2%

profile of v8, /device:TPU:8, one launch (start us, length us, event | category | flops | bytes accessed | tf_op | source)
XLA Modules:
  0.0 153.6 jit_solution(1530674098063137568)
XLA Ops:
  0.6 0.0 copy-start
  0.6 0.7 copy-done
  1.4 1.1 shard_map.58
  2.5 13.0 %all-to-all-start = ((bf16[32,16,1024]{2,1,0:T(8,128)(2,1)}), bf16[32,16,1024]{2,1,0:T(8,128)(2,1)S(1)}, u32[]{:S(2)}, u32[]{:S(2)}) async-start(bf16[32,16,1024]{2,1,0:T(8,128)(2,1)} %shard_map.58), calls=%async_computation | async-start | bytes 2097152 | tf_op jit(solution)/shard_map/all_to_all | solution.py:29
  15.5 0.0 copy-start.3
  16.2 0.1 stack.23.idx
  16.3 0.0 copy-done.3
  16.3 1.8 %all-gather = bf16[32,1,1024]{2,0,1:T(8,128)(2,1)S(1)} all-gather(bf16[16,1,1024]{2,0,1:T(8,128)(2,1)S(1)} %copy-done.3), channel_id=2, replica_groups=mesh['xl'=2,'z'=12,'y'=8,'xh'=2,'c'=2] {'c'}, dimensions={0}, use_global_device_ids=true | all-gather | bytes 98304 | tf_op jit(solution)/shard_map/all_gather | solution.py:213
  18.1 34.3 %all-gather.1 = bf16[24,16,1024]{2,1,0:T(8,128)(2,1)S(1)} all-gather(bf16[2,16,1024]{2,1,0:T(8,128)(2,1)S(1)} %bitcast.18), channel_id=3, replica_groups=mesh['xl'=2,'z'=12,'y'=8,'xh'=2,'c'=2] {'z'}, dimensions={0}, use_global_device_ids=true | all-gather | bytes 851968 | tf_op jit(solution)/shard_map/all_gather | solution.py:214
  52.5 0.0 all-to-all-done
  52.5 2.2 %shard_map.59 = (f32[512,384]{1,0:T(8,128)S(1)}, f32[24,8,128]{2,1,0:T(8,128)}, f32[8,128]{1,0:T(8,128)S(1)}) custom-call(s32[5]{0:T(128)S(1)} %stack.23.idx, f32[1]{0:T(128)S(6)} %copy.6.fac, bf16[512,1024]{1,0:T(8,128)(2,1)S(1)} %bitcast.14, bf16[384,1024]{1,0:T(8,128)(2,1)S(1)} %bitcast.11), custom_call_target="tpu_custom_call" | custom-call | tf_op jit(solution)/shard_map/pallas_call | solution.py:39
  54.7 4.5 %all-to-all-start.1 = ((f32[24,8,128]{2,1,0:T(8,128)}), f32[24,8,128]{2,1,0:T(8,128)S(1)}, u32[]{:S(2)}, u32[]{:S(2)}) async-start(f32[24,8,128]{2,1,0:T(8,128)} %get-tuple-element.21), calls=%async_computation.1 | async-start | bytes 196608 | tf_op jit(solution)/shard_map/all_to_all | solution.py:29
  59.2 12.7 %all-gather.2 = f32[32,128]{1,0:T(8,128)S(1)} all-gather(f32[8,128]{1,0:T(8,128)S(1)} %get-tuple-element.22), channel_id=4, replica_groups=mesh['xl'=2,'z'=12,'y'=8,'xh'=2,'c'=2] {'xl','xh'}, dimensions={0}, use_global_device_ids=true | all-gather | bytes 20480 | tf_op jit(solution)/shard_map/all_gather | solution.py:222
  71.8 0.0 all-to-all-done.1.col
  71.9 0.2 shard_map.60
  72.0 13.5 %all_to_all.25.got = f32[8,8,128]{2,1,0:T(8,128)S(1)} all-to-all(f32[8,8,128]{2,1,0:T(8,128)S(1)} %get-tuple-element.23), channel_id=1, replica_groups=mesh['xl'=2,'z'=12,'y'=8,'xh'=2,'c'=2] {'y'}, dimensions={0} | all-to-all | bytes 65536 | tf_op jit(solution)/shard_map/all_to_all | solution.py:29
  85.5 1.9 %shard_map.61 = (bf16[264,1024]{1,0:T(8,128)(2,1)S(1)}, bf16[200,1024]{1,0:T(8,128)(2,1)S(1)}, f32[192,1024]{1,0:T(8,128)S(1)}, f32[16,128]{1,0:T(8,128)S(1)}, bf16[2,256,384]{2,1,0:T(8,128)(2,1)S(1)}) custom-call(s32[5]{0:T(128)S(1)} %stack.23.idx, f32[1]{0:T(128)S(6)} %copy.6.fac, f32[512,384]{1,0:T(8,128)S(1)} %get-tuple-element.20.sc, ...), custom_call_target="tpu_custom_call" | custom-call | tf_op jit(solution)/shard_map/pallas_call | solution.py:39
  87.5 0.0 copy-start.1
  87.5 0.7 copy-done.1
  88.2 2.7 %collective-permute-start.1 = (bf16[264,1024]{1,0:T(8,128)(2,1)S(1)}, bf16[264,1024]{1,0:T(8,128)(2,1)S(1)}, u32[]{:S(2)}, u32[]{:S(2)}) collective-permute-start(bf16[264,1024]{1,0:T(8,128)(2,1)S(1)} %get-tuple-element.29), channel_id=1, source_target_pairs={{0,384},{384,0},{1,385},{385,1},{2,386},{386,2},{3,387},{387,3},{4... | collective-permute-start | bytes 1622024 | tf_op jit(solution)/shard_map/ppermute | solution.py:34
  91.0 1.0 shard_map.63.here
  92.0 9.0 %collective-permute-done.1.came = bf16[264,1024]{1,0:T(8,128)(2,1)S(1)} collective-permute-done((bf16[264,1024]{1,0:T(8,128)(2,1)S(1)}, bf16[264,1024]{1,0:T(8,128)(2,1)S(1)}, u32[]{:S(2)}, u32[]{:S(2)}) %collective-permute-start.1) | collective-permute-done | bytes 540704 | tf_op jit(solution)/shard_map/ppermute | solution.py:34
  100.9 0.7 shard_map.64
  101.7 4.8 %collective-permute-start.2 = (bf16[136,1024]{1,0:T(8,128)(2,1)S(1)}, bf16[136,1024]{1,0:T(8,128)(2,1)S(1)}, u32[]{:S(2)}, u32[]{:S(2)}) collective-permute-start(bf16[136,1024]{1,0:T(8,128)(2,1)S(1)} %get-tuple-element.32), channel_id=1, source_target_pairs={{0,2},{2,0},{1,3},{3,1},{4,6},{6,4},{5,7},{7,5},{8,10},{10,8},{9,1... | collective-permute-start | bytes 835592 | tf_op jit(solution)/shard_map/ppermute | solution.py:34
  106.5 5.1 %collective-permute-done.2.got = bf16[136,1024]{1,0:T(8,128)(2,1)S(1)} collective-permute-done((bf16[136,1024]{1,0:T(8,128)(2,1)S(1)}, bf16[136,1024]{1,0:T(8,128)(2,1)S(1)}, u32[]{:S(2)}, u32[]{:S(2)}) %collective-permute-start.2) | collective-permute-done | bytes 278560 | tf_op jit(solution)/shard_map/ppermute | solution.py:34
  111.6 0.9 shard_map.65
  112.5 0.0 copy-start.2
  112.5 4.9 %all-to-all-start.4 = ((bf16[8,16,1024]{2,1,0:T(8,128)(2,1)}), bf16[8,16,1024]{2,1,0:T(8,128)(2,1)S(1)}, u32[]{:S(2)}, u32[]{:S(2)}) async-start(bf16[8,16,1024]{2,1,0:T(8,128)(2,1)} %get-tuple-element.35), calls=%async_computation.4 | async-start | bytes 524288 | tf_op jit(solution)/shard_map/all_to_all | solution.py:29
  117.4 0.0 copy-done.2
  117.4 1.9 %collective-permute-start = (bf16[200,1024]{1,0:T(8,128)(2,1)S(1)}, bf16[200,1024]{1,0:T(8,128)(2,1)S(1)}, u32[]{:S(2)}, u32[]{:S(2)}) collective-permute-start(bf16[200,1024]{1,0:T(8,128)(2,1)S(1)} %copy-done.2), channel_id=1, source_target_pairs={{0,1},{1,0},{2,3},{3,2},{4,5},{5,4},{6,7},{7,6},{8,9},{9,8},{10,11... | collective-permute-start | bytes 1228808 | tf_op jit(solution)/shard_map/ppermute | solution.py:34
  119.3 1.7 %collective-permute-done.came = bf16[200,1024]{1,0:T(8,128)(2,1)S(1)} collective-permute-done((bf16[200,1024]{1,0:T(8,128)(2,1)S(1)}, bf16[200,1024]{1,0:T(8,128)(2,1)S(1)}, u32[]{:S(2)}, u32[]{:S(2)}) %collective-permute-start) | collective-permute-done | bytes 409632 | tf_op jit(solution)/shard_map/ppermute | solution.py:34
  121.0 1.0 shard_map.62
  122.0 4.5 %all-to-all-done.4.got = bf16[8,16,1024]{2,1,0:T(8,128)(2,1)S(1)} async-done(((bf16[8,16,1024]{2,1,0:T(8,128)(2,1)}), bf16[8,16,1024]{2,1,0:T(8,128)(2,1)S(1)}, u32[]{:S(2)}, u32[]{:S(2)}) %all-to-all-start.4) | async-done | bytes 262176 | tf_op jit(solution)/shard_map/all_to_all | solution.py:29
  126.5 8.8 %all-to-all-start.3 = ((bf16[12,136,128]{2,1,0:T(8,128)(2,1)}), bf16[12,136,128]{2,1,0:T(8,128)(2,1)S(1)}, u32[]{:S(2)}, u32[]{:S(2)}) async-start(bf16[12,136,128]{2,1,0:T(8,128)(2,1)} %shard_map.62), calls=%async_computation.3 | async-start | bytes 835584 | tf_op jit(solution)/shard_map/all_to_all | solution.py:29
  135.3 0.7 shard_map.67
  135.9 16.9 %all-to-all-done.3.got = bf16[12,136,128]{2,1,0:T(8,128)(2,1)S(1)} async-done(((bf16[12,136,128]{2,1,0:T(8,128)(2,1)}), bf16[12,136,128]{2,1,0:T(8,128)(2,1)S(1)}, u32[]{:S(2)}, u32[]{:S(2)}) %all-to-all-start.3) | async-done | bytes 417824 | tf_op jit(solution)/shard_map/all_to_all | solution.py:29
  152.8 0.7 shard_map.66
Async XLA Ops:
  0.6 0.8 copy-start
  2.5 50.0 %all-to-all-start = ((bf16[32,16,1024]{2,1,0:T(8,128)(2,1)}), bf16[32,16,1024]{2,1,0:T(8,128)(2,1)S(1)}, u32[]{:S(2)}, u32[]{:S(2)}) async-start(bf16[32,16,1024]{2,1,0:T(8,128)(2,1)} %shard_map.58), calls=%async_computation | async-start | bytes 2097152 | tf_op jit(solution)/shard_map/all_to_all | solution.py:29
  15.5 0.8 copy-start.3
  54.7 17.2 %all-to-all-start.1 = ((f32[24,8,128]{2,1,0:T(8,128)}), f32[24,8,128]{2,1,0:T(8,128)S(1)}, u32[]{:S(2)}, u32[]{:S(2)}) async-start(f32[24,8,128]{2,1,0:T(8,128)} %get-tuple-element.21), calls=%async_computation.1 | async-start | bytes 196608 | tf_op jit(solution)/shard_map/all_to_all | solution.py:29
  87.5 0.8 copy-start.1
  88.2 12.7 %collective-permute-start.1 = (bf16[264,1024]{1,0:T(8,128)(2,1)S(1)}, bf16[264,1024]{1,0:T(8,128)(2,1)S(1)}, u32[]{:S(2)}, u32[]{:S(2)}) collective-permute-start(bf16[264,1024]{1,0:T(8,128)(2,1)S(1)} %get-tuple-element.29), channel_id=1, source_target_pairs={{0,384},{384,0},{1,385},{385,1},{2,386},{386,2},{3,387},{387,3},{4... | collective-permute-start | bytes 1622024 | tf_op jit(solution)/shard_map/ppermute | solution.py:34
  101.7 9.9 %collective-permute-start.2 = (bf16[136,1024]{1,0:T(8,128)(2,1)S(1)}, bf16[136,1024]{1,0:T(8,128)(2,1)S(1)}, u32[]{:S(2)}, u32[]{:S(2)}) collective-permute-start(bf16[136,1024]{1,0:T(8,128)(2,1)S(1)} %get-tuple-element.32), channel_id=1, source_target_pairs={{0,2},{2,0},{1,3},{3,1},{4,6},{6,4},{5,7},{7,5},{8,10},{10,8},{9,1... | collective-permute-start | bytes 835592 | tf_op jit(solution)/shard_map/ppermute | solution.py:34
  112.5 4.9 %copy-start.2 = (bf16[200,1024]{1,0:T(8,128)(2,1)S(1)}, bf16[200,1024]{1,0:T(8,128)(2,1)}, u32[]{:S(2)}) copy-start(bf16[200,1024]{1,0:T(8,128)(2,1)} %copy-done.1) | copy-start | bytes 1228804
  112.5 14.0 %all-to-all-start.4 = ((bf16[8,16,1024]{2,1,0:T(8,128)(2,1)}), bf16[8,16,1024]{2,1,0:T(8,128)(2,1)S(1)}, u32[]{:S(2)}, u32[]{:S(2)}) async-start(bf16[8,16,1024]{2,1,0:T(8,128)(2,1)} %get-tuple-element.35), calls=%async_computation.4 | async-start | bytes 524288 | tf_op jit(solution)/shard_map/all_to_all | solution.py:29
  117.4 3.6 %collective-permute-start = (bf16[200,1024]{1,0:T(8,128)(2,1)S(1)}, bf16[200,1024]{1,0:T(8,128)(2,1)S(1)}, u32[]{:S(2)}, u32[]{:S(2)}) collective-permute-start(bf16[200,1024]{1,0:T(8,128)(2,1)S(1)} %copy-done.2), channel_id=1, source_target_pairs={{0,1},{1,0},{2,3},{3,2},{4,5},{5,4},{6,7},{7,6},{8,9},{9,8},{10,11... | collective-permute-start | bytes 1228808 | tf_op jit(solution)/shard_map/ppermute | solution.py:34
  126.5 26.4 %all-to-all-start.3 = ((bf16[12,136,128]{2,1,0:T(8,128)(2,1)}), bf16[12,136,128]{2,1,0:T(8,128)(2,1)S(1)}, u32[]{:S(2)}, u32[]{:S(2)}) async-start(bf16[12,136,128]{2,1,0:T(8,128)(2,1)} %shard_map.62), calls=%async_computation.3 | async-start | bytes 835584 | tf_op jit(solution)/shard_map/all_to_all | solution.py:29

commit v9 on v6

--- a/solution.py
+++ b/solution.py
@@ -123,7 +123,7 @@
         pack[n, 5:6, :] = total
 
 
-def grad_kernel(idx, fac, sc, im, tx, got, clse, iaway, taway, there, scal, delta, part):
+def grad_kernel(idx, fac, sc, im, tx, got, clse, iaway, taway, there, scal, ihere, delta, part):
     rows = merged([got[n] for n in range(N_Y)])[0:4]
     diag = sum(got[n, 4:5, :] for n in range(N_Y))
     total = sum(got[n, 5:6, :] for n in range(N_Y))
@@ -149,10 +149,7 @@
         taway[z * EACH : (z + 1) * EACH, :] = part[z, 1 - xl].astype(BF16)
         there[z * EACH : (z + 1) * EACH, :] = part[z, xl]
     put_tail(taway, COLS // 2, row_loss)
-
-
-def keep_kernel(idx, delta, tx, ihere):
-    ihere[...] = jnp.dot(delta[idx[2]], tx[...], preferred_element_type=F32)
+    ihere[...] = jnp.dot(delta[c], tx[...], preferred_element_type=F32)
 
 
 def across_kernel(idx, scal, here, came, away, keep, out):
@@ -234,21 +231,20 @@
     near = lax.all_gather(rpack, ("xh", "c"))
     col_lse, ypack = call(merge_kernel, [((8, COLS), F32), ((N_Y, 8, LANES), F32)], [], col_got, near)
     row_got = exchange(ypack, "y")
-    iaway, taway, there, scal, delta = call(
+    iaway, taway, there, scal, ihere = call(
         grad_kernel,
         [
             ((ROWS // 2 + TAIL, WIDTH), BF16),
             ((COLS // 2 + TAIL, WIDTH), BF16),
             ((COLS // 2, WIDTH), F32),
             ((16, LANES), F32),
-            ((N_C, ROWS // 2, COLS), BF16),
+            ((ROWS // 2, WIDTH), F32),
         ],
-        [((N_Z, N_XL, EACH, WIDTH), F32)],
+        [((N_C, ROWS // 2, COLS), BF16), ((N_Z, N_XL, EACH, WIDTH), F32)],
         idx, logit_scale, scores, images, texts, row_got, col_lse,
     )
     tcame = shift(taway, "xl", 1)
     icame = shift(iaway, "c", 1)
-    (ihere,) = call(keep_kernel, [((ROWS // 2, WIDTH), F32)], [], idx, delta, texts)
     xaway, keep, total = call(
         across_kernel,
         [((ROWS // 4 + TAIL, WIDTH), BF16), ((ROWS // 4, WIDTH), F32), ((8, LANES), F32)],
@@ -274,8 +270,8 @@
     )
     left = shift(up, "y", 3)
     right = shift(down, "y", 5)
+    text_grad, loss = call(final_kernel, [((EACH, 1, WIDTH), F32), ((1, 1), F32)], [], text_got, total)
     (image_grad,) = call(image_kernel, [((EACH, 1, WIDTH), F32)], [], mid, left, right)
-    text_grad, loss = call(final_kernel, [((EACH, 1, WIDTH), F32), ((1, 1), F32)], [], text_got, total)
     return loss[0, 0], image_grad, text_grad
 
 

time: 149 us -> 150 us (level)
    pallas_call x11 -> x10, Pallas kernels: 10.2 us -> 9.48 us  [call(): pl.pallas_call(kernel, out_shape=[jax.ShapeDtypeStruct(s, d) for s, d in...]
  transfers between devices with their start and end apart: 10 -> 10, of which waited for: 7 -> 7; matrix products, arithmetic and copies ran while one was open for 0% -> 0% of each run, Pallas kernels for 2% -> 1%
where the time goes in v9:
time: 150 us
  blocking collectives  62.2 us (41%)
  starting transfers between devices  44.8 us (30%)
  waiting for transfers between devices  28.9 us (19%)
  Pallas kernels  9.48 us (6%)
  local copies, waits for them, and re-layouts  2.86 us (2%)
    all_gather x1, blocking collectives, body(): texts = lax.all_gather(texts, 'z').reshape(COLS, WIDTH)  36.4 us
    ppermute x7, waiting for transfers between devices, shift(): return lax.ppermute(x, axis, [(i, (i + k) % n) for i in range(n)])  25.3 us
    all_to_all x3, starting transfers between devices, exchange(): return lax.all_to_all(x, axes, 0, 0, tiled=False)  23 us
    ppermute x7, starting transfers between devices, shift(): return lax.ppermute(x, axis, [(i, (i + k) % n) for i in range(n)])  21.8 us
    all_to_all x1, blocking collectives, exchange(): return lax.all_to_all(x, axes, 0, 0, tiled=False)  12.8 us
    pallas_call x10, Pallas kernels, call(): pl.pallas_call(kernel, out_shape=[jax.ShapeDtypeStruct(s, d) for s, d in...  9.48 us
    all_gather x1, blocking collectives, body(): near = lax.all_gather(rpack, ('xh', 'c'))  6.71 us
    all_gather x1, blocking collectives, body(): texts = lax.all_gather(text_emb.reshape(EACH, WIDTH), 'xl')  6.26 us
  transfers between devices with their start and end apart: 10, of which 7 were waited for; matrix products, arithmetic and copies ran while one was open for 0% of the time, Pallas kernels for 1%

profile of v9, /device:TPU:14, one launch (start us, length us, event | category | flops | bytes accessed | tf_op | source)
XLA Modules:
  0.0 149.7 jit_solution(8924128557345707505)
XLA Ops:
  0.6 0.0 copy-start.2
  0.6 0.7 copy-done.2
  1.4 1.1 shard_map.58
  2.5 10.1 %all-to-all-start = ((bf16[32,16,1024]{2,1,0:T(8,128)(2,1)}), bf16[32,16,1024]{2,1,0:T(8,128)(2,1)S(1)}, u32[]{:S(2)}, u32[]{:S(2)}) async-start(bf16[32,16,1024]{2,1,0:T(8,128)(2,1)} %shard_map.58), calls=%async_computation | async-start | bytes 2097152 | tf_op jit(solution)/shard_map/all_to_all | solution.py:29
  12.6 0.0 copy-start.3
  13.3 0.1 stack.27.idx
  13.4 0.0 copy-done.3
  13.4 6.3 %all-gather = bf16[32,1,1024]{2,0,1:T(8,128)(2,1)S(1)} all-gather(bf16[16,1,1024]{2,0,1:T(8,128)(2,1)S(1)} %copy-done.3), channel_id=2, replica_groups=mesh['xl'=2,'z'=12,'y'=8,'xh'=2,'c'=2] {'xl'}, dimensions={0}, use_global_device_ids=true | all-gather | bytes 98304 | tf_op jit(solution)/shard_map/all_gather | solution.py:222
  19.7 36.4 %all-gather.1 = bf16[24,16,1024]{2,1,0:T(8,128)(2,1)S(1)} all-gather(bf16[2,16,1024]{2,1,0:T(8,128)(2,1)S(1)} %bitcast.18), channel_id=3, replica_groups=mesh['xl'=2,'z'=12,'y'=8,'xh'=2,'c'=2] {'z'}, dimensions={0}, use_global_device_ids=true | all-gather | bytes 851968 | tf_op jit(solution)/shard_map/all_gather | solution.py:223
  56.0 0.0 all-to-all-done
  56.0 2.2 %shard_map.59 = (f32[512,384]{1,0:T(8,128)S(1)}, f32[24,8,128]{2,1,0:T(8,128)}, f32[8,128]{1,0:T(8,128)S(1)}) custom-call(s32[6]{0:T(128)S(1)} %stack.27.idx, f32[1]{0:T(128)S(6)} %copy.6.fac, bf16[512,1024]{1,0:T(8,128)(2,1)S(1)} %bitcast.12, bf16[384,1024]{1,0:T(8,128)(2,1)S(1)} %bitcast.14), custom_call_target="tpu_custom_call" | custom-call | tf_op jit(solution)/shard_map/pallas_call | solution.py:39
  58.2 0.0 copy-start
  58.2 0.9 copy-done
  59.1 5.1 %all-to-all-start.1 = ((f32[24,8,128]{2,1,0:T(8,128)}), f32[24,8,128]{2,1,0:T(8,128)S(1)}, u32[]{:S(2)}, u32[]{:S(2)}) async-start(f32[24,8,128]{2,1,0:T(8,128)} %get-tuple-element.26), calls=%async_computation.1 | async-start | bytes 196608 | tf_op jit(solution)/shard_map/all_to_all | solution.py:29
  64.3 6.7 %all-gather.2 = f32[32,128]{1,0:T(8,128)S(1)} all-gather(f32[8,128]{1,0:T(8,128)S(1)} %get-tuple-element.27), channel_id=4, replica_groups=mesh['xl'=2,'z'=12,'y'=8,'xh'=2,'c'=2] {'xh','c'}, dimensions={0}, use_global_device_ids=true | all-gather | bytes 20480 | tf_op jit(solution)/shard_map/all_gather | solution.py:231
  71.0 3.6 %all-to-all-done.1.col = f32[24,8,128]{2,1,0:T(8,128)S(1)} async-done(((f32[24,8,128]{2,1,0:T(8,128)}), f32[24,8,128]{2,1,0:T(8,128)S(1)}, u32[]{:S(2)}, u32[]{:S(2)}) %all-to-all-start.1) | async-done | bytes 98336 | tf_op jit(solution)/shard_map/all_to_all | solution.py:29
  74.5 0.2 shard_map.60
  74.7 12.8 %all_to_all.20.got = f32[8,8,128]{2,1,0:T(8,128)S(1)} all-to-all(f32[8,8,128]{2,1,0:T(8,128)S(1)} %get-tuple-element.28), channel_id=1, replica_groups=mesh['xl'=2,'z'=12,'y'=8,'xh'=2,'c'=2] {'y'}, dimensions={0} | all-to-all | bytes 65536 | tf_op jit(solution)/shard_map/all_to_all | solution.py:29
  87.5 0.0 copy-start.1
  87.5 1.1 copy-done.1
  88.7 2.2 %shard_map.61 = (bf16[264,1024]{1,0:T(8,128)(2,1)S(1)}, bf16[200,1024]{1,0:T(8,128)(2,1)S(1)}, f32[192,1024]{1,0:T(8,128)S(1)}, f32[16,128]{1,0:T(8,128)S(1)}, f32[256,1024]{1,0:T(8,128)S(1)}) custom-call(s32[6]{0:T(128)S(1)} %stack.27.idx, f32[1]{0:T(128)S(6)} %copy.6.fac, f32[512,384]{1,0:T(8,128)S(1)} %copy-done.1, bf16[512,1024]{1,0:T(8,128)(2,1)S(1)} %bitcast.13, ...), custom_call_target="tpu_custom_call" | custom-call | tf_op jit(solution)/shard_map/pallas_call | solution.py:39
  90.9 2.6 %collective-permute-start = (bf16[200,1024]{1,0:T(8,128)(2,1)S(1)}, bf16[200,1024]{1,0:T(8,128)(2,1)S(1)}, u32[]{:S(2)}, u32[]{:S(2)}) collective-permute-start(bf16[200,1024]{1,0:T(8,128)(2,1)S(1)} %get-tuple-element.32), channel_id=1, source_target_pairs={{0,384},{384,0},{1,385},{385,1},{2,386},{386,2},{3,387},{387,3},{4... | collective-permute-start | bytes 1228808 | tf_op jit(solution)/shard_map/ppermute | solution.py:34
  93.5 7.2 %collective-permute-done.came = bf16[200,1024]{1,0:T(8,128)(2,1)S(1)} collective-permute-done((bf16[200,1024]{1,0:T(8,128)(2,1)S(1)}, bf16[200,1024]{1,0:T(8,128)(2,1)S(1)}, u32[]{:S(2)}, u32[]{:S(2)}) %collective-permute-start) | collective-permute-done | bytes 409632 | tf_op jit(solution)/shard_map/ppermute | solution.py:34
  100.7 1.0 shard_map.62
  101.7 7.8 %all-to-all-start.3 = ((bf16[12,136,128]{2,1,0:T(8,128)(2,1)}), bf16[12,136,128]{2,1,0:T(8,128)(2,1)S(1)}, u32[]{:S(2)}, u32[]{:S(2)}) async-start(bf16[12,136,128]{2,1,0:T(8,128)(2,1)} %shard_map.62), calls=%async_computation.3 | async-start | bytes 835584 | tf_op jit(solution)/shard_map/all_to_all | solution.py:29
  109.5 1.9 %collective-permute-start.1 = (bf16[264,1024]{1,0:T(8,128)(2,1)S(1)}, bf16[264,1024]{1,0:T(8,128)(2,1)S(1)}, u32[]{:S(2)}, u32[]{:S(2)}) collective-permute-start(bf16[264,1024]{1,0:T(8,128)(2,1)S(1)} %get-tuple-element.34), channel_id=1, source_target_pairs={{0,1},{1,0},{2,3},{3,2},{4,5},{5,4},{6,7},{7,6},{8,9},{9,8},{10,11... | collective-permute-start | bytes 1622024 | tf_op jit(solution)/shard_map/ppermute | solution.py:34
  111.4 1.9 %collective-permute-done.1.came = bf16[264,1024]{1,0:T(8,128)(2,1)S(1)} collective-permute-done((bf16[264,1024]{1,0:T(8,128)(2,1)S(1)}, bf16[264,1024]{1,0:T(8,128)(2,1)S(1)}, u32[]{:S(2)}, u32[]{:S(2)}) %collective-permute-start.1) | collective-permute-done | bytes 540704 | tf_op jit(solution)/shard_map/ppermute | solution.py:34
  113.3 0.7 shard_map.63
  114.1 2.5 %collective-permute-start.2 = (bf16[136,1024]{1,0:T(8,128)(2,1)S(1)}, bf16[136,1024]{1,0:T(8,128)(2,1)S(1)}, u32[]{:S(2)}, u32[]{:S(2)}) collective-permute-start(bf16[136,1024]{1,0:T(8,128)(2,1)S(1)} %get-tuple-element.37), channel_id=1, source_target_pairs={{0,2},{2,0},{1,3},{3,1},{4,6},{6,4},{5,7},{7,5},{8,10},{10,8},{9,1... | collective-permute-start | bytes 835592 | tf_op jit(solution)/shard_map/ppermute | solution.py:34
  116.6 9.5 %collective-permute-done.2.got = bf16[136,1024]{1,0:T(8,128)(2,1)S(1)} collective-permute-done((bf16[136,1024]{1,0:T(8,128)(2,1)S(1)}, bf16[136,1024]{1,0:T(8,128)(2,1)S(1)}, u32[]{:S(2)}, u32[]{:S(2)}) %collective-permute-start.2) | collective-permute-done | bytes 278560 | tf_op jit(solution)/shard_map/ppermute | solution.py:34
  126.2 0.7 shard_map.64
  126.8 2.5 %collective-permute-start.3 = (bf16[48,1024]{1,0:T(8,128)(2,1)S(1)}, bf16[48,1024]{1,0:T(8,128)(2,1)S(1)}, u32[]{:S(2)}, u32[]{:S(2)}) collective-permute-start(bf16[48,1024]{1,0:T(8,128)(2,1)S(1)} %get-tuple-element.41), channel_id=1, source_target_pairs={{0,4},{4,8},{8,12},{12,16},{16,20},{20,24},{24,28},{28,0},{1,5},{5... | collective-permute-start | bytes 294920 | tf_op jit(solution)/shard_map/ppermute | solution.py:34
  129.3 3.4 %collective-permute-start.4 = (bf16[32,1024]{1,0:T(8,128)(2,1)S(1)}, bf16[32,1024]{1,0:T(8,128)(2,1)S(1)}, u32[]{:S(2)}, u32[]{:S(2)}) collective-permute-start(bf16[32,1024]{1,0:T(8,128)(2,1)S(1)} %get-tuple-element.42), channel_id=1, source_target_pairs={{0,28},{4,0},{8,4},{12,8},{16,12},{20,16},{24,20},{28,24},{1,29},{... | collective-permute-start | bytes 196616 | tf_op jit(solution)/shard_map/ppermute | solution.py:34
  132.7 2.8 %collective-permute-done.4.high = bf16[32,1024]{1,0:T(8,128)(2,1)S(1)} collective-permute-done((bf16[32,1024]{1,0:T(8,128)(2,1)S(1)}, bf16[32,1024]{1,0:T(8,128)(2,1)S(1)}, u32[]{:S(2)}, u32[]{:S(2)}) %collective-permute-start.4) | collective-permute-done | bytes 65568 | tf_op jit(solution)/shard_map/ppermute | solution.py:34
  135.5 0.0 collective-permute-done.3.low
  135.5 3.4 %collective-permute-start.5 = (bf16[16,1024]{1,0:T(8,128)(2,1)S(1)}, bf16[16,1024]{1,0:T(8,128)(2,1)S(1)}, u32[]{:S(2)}, u32[]{:S(2)}) collective-permute-start(bf16[16,1024]{1,0:T(8,128)(2,1)S(1)} %get-tuple-element.44), channel_id=1, source_target_pairs={{0,12},{4,16},{8,20},{12,24},{16,28},{20,0},{24,4},{28,8},{1,13},{... | collective-permute-start | bytes 98312 | tf_op jit(solution)/shard_map/ppermute | solution.py:34
  138.9 5.5 %collective-permute-start.6 = (bf16[16,1024]{1,0:T(8,128)(2,1)S(1)}, bf16[16,1024]{1,0:T(8,128)(2,1)S(1)}, u32[]{:S(2)}, u32[]{:S(2)}) collective-permute-start(bf16[16,1024]{1,0:T(8,128)(2,1)S(1)} %get-tuple-element.45), channel_id=1, source_target_pairs={{0,20},{4,24},{8,28},{12,0},{16,4},{20,8},{24,12},{28,16},{1,21},{... | collective-permute-start | bytes 98312 | tf_op jit(solution)/shard_map/ppermute | solution.py:34
  144.4 0.2 collective-permute-done.5.left
  144.6 3.7 %collective-permute-done.6.right = bf16[16,1024]{1,0:T(8,128)(2,1)S(1)} collective-permute-done((bf16[16,1024]{1,0:T(8,128)(2,1)S(1)}, bf16[16,1024]{1,0:T(8,128)(2,1)S(1)}, u32[]{:S(2)}, u32[]{:S(2)}) %collective-permute-start.6) | collective-permute-done | bytes 32800 | tf_op jit(solution)/shard_map/ppermute | solution.py:34
  148.3 0.7 shard_map.67
  148.9 0.0 all-to-all-done.3.got
  148.9 0.7 shard_map.65
  (1 shorter events, 0.0 us)
Async XLA Ops:
  0.6 0.8 copy-start.2
  2.5 53.5 %all-to-all-start = ((bf16[32,16,1024]{2,1,0:T(8,128)(2,1)}), bf16[32,16,1024]{2,1,0:T(8,128)(2,1)S(1)}, u32[]{:S(2)}, u32[]{:S(2)}) async-start(bf16[32,16,1024]{2,1,0:T(8,128)(2,1)} %shard_map.58), calls=%async_computation | async-start | bytes 2097152 | tf_op jit(solution)/shard_map/all_to_all | solution.py:29
  12.6 0.8 copy-start.3
  58.2 0.9 copy-start
  59.1 15.4 %all-to-all-start.1 = ((f32[24,8,128]{2,1,0:T(8,128)}), f32[24,8,128]{2,1,0:T(8,128)S(1)}, u32[]{:S(2)}, u32[]{:S(2)}) async-start(f32[24,8,128]{2,1,0:T(8,128)} %get-tuple-element.26), calls=%async_computation.1 | async-start | bytes 196608 | tf_op jit(solution)/shard_map/all_to_all | solution.py:29
  87.5 1.1 copy-start.1
  90.9 9.8 %collective-permute-start = (bf16[200,1024]{1,0:T(8,128)(2,1)S(1)}, bf16[200,1024]{1,0:T(8,128)(2,1)S(1)}, u32[]{:S(2)}, u32[]{:S(2)}) collective-permute-start(bf16[200,1024]{1,0:T(8,128)(2,1)S(1)} %get-tuple-element.32), channel_id=1, source_target_pairs={{0,384},{384,0},{1,385},{385,1},{2,386},{386,2},{3,387},{387,3},{4... | collective-permute-start | bytes 1228808 | tf_op jit(solution)/shard_map/ppermute | solution.py:34
  101.7 47.3 %all-to-all-start.3 = ((bf16[12,136,128]{2,1,0:T(8,128)(2,1)}), bf16[12,136,128]{2,1,0:T(8,128)(2,1)S(1)}, u32[]{:S(2)}, u32[]{:S(2)}) async-start(bf16[12,136,128]{2,1,0:T(8,128)(2,1)} %shard_map.62), calls=%async_computation.3 | async-start | bytes 835584 | tf_op jit(solution)/shard_map/all_to_all | solution.py:29
  109.5 3.8 %collective-permute-start.1 = (bf16[264,1024]{1,0:T(8,128)(2,1)S(1)}, bf16[264,1024]{1,0:T(8,128)(2,1)S(1)}, u32[]{:S(2)}, u32[]{:S(2)}) collective-permute-start(bf16[264,1024]{1,0:T(8,128)(2,1)S(1)} %get-tuple-element.34), channel_id=1, source_target_pairs={{0,1},{1,0},{2,3},{3,2},{4,5},{5,4},{6,7},{7,6},{8,9},{9,8},{10,11... | collective-permute-start | bytes 1622024 | tf_op jit(solution)/shard_map/ppermute | solution.py:34
  114.1 12.1 %collective-permute-start.2 = (bf16[136,1024]{1,0:T(8,128)(2,1)S(1)}, bf16[136,1024]{1,0:T(8,128)(2,1)S(1)}, u32[]{:S(2)}, u32[]{:S(2)}) collective-permute-start(bf16[136,1024]{1,0:T(8,128)(2,1)S(1)} %get-tuple-element.37), channel_id=1, source_target_pairs={{0,2},{2,0},{1,3},{3,1},{4,6},{6,4},{5,7},{7,5},{8,10},{10,8},{9,1... | collective-permute-start | bytes 835592 | tf_op jit(solution)/shard_map/ppermute | solution.py:34
  126.8 8.6 %collective-permute-start.3 = (bf16[48,1024]{1,0:T(8,128)(2,1)S(1)}, bf16[48,1024]{1,0:T(8,128)(2,1)S(1)}, u32[]{:S(2)}, u32[]{:S(2)}) collective-permute-start(bf16[48,1024]{1,0:T(8,128)(2,1)S(1)} %get-tuple-element.41), channel_id=1, source_target_pairs={{0,4},{4,8},{8,12},{12,16},{16,20},{20,24},{24,28},{28,0},{1,5},{5... | collective-permute-start | bytes 294920 | tf_op jit(solution)/shard_map/ppermute | solution.py:34
  129.3 6.2 %collective-permute-start.4 = (bf16[32,1024]{1,0:T(8,128)(2,1)S(1)}, bf16[32,1024]{1,0:T(8,128)(2,1)S(1)}, u32[]{:S(2)}, u32[]{:S(2)}) collective-permute-start(bf16[32,1024]{1,0:T(8,128)(2,1)S(1)} %get-tuple-element.42), channel_id=1, source_target_pairs={{0,28},{4,0},{8,4},{12,8},{16,12},{20,16},{24,20},{28,24},{1,29},{... | collective-permute-start | bytes 196616 | tf_op jit(solution)/shard_map/ppermute | solution.py:34
  135.5 9.1 %collective-permute-start.5 = (bf16[16,1024]{1,0:T(8,128)(2,1)S(1)}, bf16[16,1024]{1,0:T(8,128)(2,1)S(1)}, u32[]{:S(2)}, u32[]{:S(2)}) collective-permute-start(bf16[16,1024]{1,0:T(8,128)(2,1)S(1)} %get-tuple-element.44), channel_id=1, source_target_pairs={{0,12},{4,16},{8,20},{12,24},{16,28},{20,0},{24,4},{28,8},{1,13},{... | collective-permute-start | bytes 98312 | tf_op jit(solution)/shard_map/ppermute | solution.py:34
  138.9 9.4 %collective-permute-start.6 = (bf16[16,1024]{1,0:T(8,128)(2,1)S(1)}, bf16[16,1024]{1,0:T(8,128)(2,1)S(1)}, u32[]{:S(2)}, u32[]{:S(2)}) collective-permute-start(bf16[16,1024]{1,0:T(8,128)(2,1)S(1)} %get-tuple-element.45), channel_id=1, source_target_pairs={{0,20},{4,24},{8,28},{12,0},{16,4},{20,8},{24,12},{28,16},{1,21},{... | collective-permute-start | bytes 98312 | tf_op jit(solution)/shard_map/ppermute | solution.py:34

commit v10 on v6

--- a/solution.py
+++ b/solution.py
@@ -88,6 +88,12 @@
     tile = block[...]
     for n in range(N_COL):
         out[n] = tile
+
+
+def stack_kernel(idx, own, came, out):
+    xl = idx[5]
+    out[xl] = own[...]
+    out[1 - xl] = came[...]
 
 
 def score_kernel(idx, fac, im, tx, sc, cpack, rpack):
@@ -222,7 +228,9 @@
     idx = jnp.stack(places).astype(jnp.int32)
     (spread,) = call(spread_kernel, [((N_COL, EACH, WIDTH), BF16)], [], image_emb.reshape(EACH, WIDTH))
     images = exchange(spread, ("c", "xh", "y")).reshape(ROWS, WIDTH)
-    texts = lax.all_gather(text_emb.reshape(EACH, WIDTH), "xl")
+    own = text_emb.reshape(EACH, WIDTH)
+    came = shift(own, "xl", 1)
+    (texts,) = call(stack_kernel, [((N_XL, EACH, WIDTH), BF16)], [], idx, own, came)
     texts = lax.all_gather(texts, "z").reshape(COLS, WIDTH)
     scores, cpack, rpack = call(
         score_kernel,
@@ -274,8 +282,8 @@
     )
     left = shift(up, "y", 3)
     right = shift(down, "y", 5)
+    text_grad, loss = call(final_kernel, [((EACH, 1, WIDTH), F32), ((1, 1), F32)], [], text_got, total)
     (image_grad,) = call(image_kernel, [((EACH, 1, WIDTH), F32)], [], mid, left, right)
-    text_grad, loss = call(final_kernel, [((EACH, 1, WIDTH), F32), ((1, 1), F32)], [], text_got, total)
     return loss[0, 0], image_grad, text_grad
 
 

time: 149 us -> 150 us (level)
  blocking collectives: 62.2 us -> 55.2 us
  starting transfers between devices: 45 us -> 50.9 us
  waiting for transfers between devices: 27.9 us -> 29.4 us
    all_gather x1 -> x0, blocking collectives: 6.26 us -> none  [body(): texts = lax.all_gather(text_emb.reshape(EACH, WIDTH), 'xl')]
    ppermute x7 -> x8, starting transfers between devices: 21.8 us -> 27.4 us  [shift(): return lax.ppermute(x, axis, [(i, (i + k) % n) for i in range(n)])]
    ppermute x7 -> x8, waiting for transfers between devices: 24.4 us -> 25.9 us  [shift(): return lax.ppermute(x, axis, [(i, (i + k) % n) for i in range(n)])]
    pallas_call x11 -> x12, Pallas kernels: 10.2 us -> 10.7 us  [call(): pl.pallas_call(kernel, out_shape=[jax.ShapeDtypeStruct(s, d) for s, d in...]
  transfers between devices with their start and end apart: 10 -> 11, of which waited for: 7 -> 8; matrix products, arithmetic and copies ran while one was open for 0% -> 0% of each run, Pallas kernels for 2% -> 2%
where the time goes in v10:
time: 150 us; the launch traced here: 149 us
  blocking collectives  55.2 us (37%)
  starting transfers between devices  50.9 us (34%)
  waiting for transfers between devices  29.4 us (20%)
  Pallas kernels  10.7 us (7%)
  local copies, waits for them, and re-layouts  1.64 us (1%)
    all_gather x1, blocking collectives, body(): texts = lax.all_gather(texts, 'z').reshape(COLS, WIDTH)  35.8 us
    ppermute x8, starting transfers between devices, shift(): return lax.ppermute(x, axis, [(i, (i + k) % n) for i in range(n)])  27.4 us
    ppermute x8, waiting for transfers between devices, shift(): return lax.ppermute(x, axis, [(i, (i + k) % n) for i in range(n)])  25.9 us
    all_to_all x3, starting transfers between devices, exchange(): return lax.all_to_all(x, axes, 0, 0, tiled=False)  23.4 us
    all_to_all x1, blocking collectives, exchange(): return lax.all_to_all(x, axes, 0, 0, tiled=False)  12.8 us
    pallas_call x12, Pallas kernels, call(): pl.pallas_call(kernel, out_shape=[jax.ShapeDtypeStruct(s, d) for s, d in...  10.7 us
    all_gather x1, blocking collectives, body(): near = lax.all_gather(rpack, ('xh', 'c'))  6.71 us
    all_to_all x3, waiting for transfers between devices, exchange(): return lax.all_to_all(x, axes, 0, 0, tiled=False)  3.56 us
  transfers between devices with their start and end apart: 11, of which 8 were waited for; matrix products, arithmetic and copies ran while one was open for 0% of the time, Pallas kernels for 2%

profile of v10, /device:TPU:14, one launch (start us, length us, event | category | flops | bytes accessed | tf_op | source)
XLA Modules:
  0.0 149.3 jit_solution(16347882998504647166)
XLA Ops:
  0.6 0.0 copy-start
  0.6 0.7 copy-done
  1.4 1.1 shard_map.58
  2.5 0.0 copy-start.1
  2.5 10.2 %all-to-all-start = ((bf16[32,16,1024]{2,1,0:T(8,128)(2,1)}), bf16[32,16,1024]{2,1,0:T(8,128)(2,1)S(1)}, u32[]{:S(2)}, u32[]{:S(2)}) async-start(bf16[32,16,1024]{2,1,0:T(8,128)(2,1)} %shard_map.58), calls=%async_computation | async-start | bytes 2097152 | tf_op jit(solution)/shard_map/all_to_all | solution.py:29
  12.8 0.0 copy-done.1
  12.8 5.6 %collective-permute-start = (bf16[16,1024]{1,0:T(8,128)(2,1)S(1)}, bf16[16,1024]{1,0:T(8,128)(2,1)S(1)}, u32[]{:S(2)}, u32[]{:S(2)}) collective-permute-start(bf16[16,1024]{1,0:T(8,128)(2,1)S(1)} %bitcast.19), channel_id=1, source_target_pairs={{0,384},{384,0},{1,385},{385,1},{2,386},{386,2},{3,387},{387,3},{4... | collective-permute-start | bytes 98312 | tf_op jit(solution)/shard_map/ppermute | solution.py:34
  19.1 0.1 stack.27.idx
  19.2 1.5 collective-permute-done.came
  20.6 0.5 shard_map.59
  21.2 35.8 %all-gather = bf16[24,16,1024]{2,1,0:T(8,128)(2,1)S(1)} all-gather(bf16[2,16,1024]{2,1,0:T(8,128)(2,1)S(1)} %shard_map.59), channel_id=2, replica_groups=mesh['xl'=2,'z'=12,'y'=8,'xh'=2,'c'=2] {'z'}, dimensions={0}, use_global_device_ids=true | all-gather | bytes 851968 | tf_op jit(solution)/shard_map/all_gather | solution.py:234
  56.9 0.0 all-to-all-done
  56.9 2.2 %shard_map.60 = (f32[512,384]{1,0:T(8,128)S(1)}, f32[24,8,128]{2,1,0:T(8,128)}, f32[8,128]{1,0:T(8,128)S(1)}) custom-call(s32[6]{0:T(128)S(1)} %stack.27.idx, f32[1]{0:T(128)S(6)} %copy.6.fac, bf16[512,1024]{1,0:T(8,128)(2,1)S(1)} %bitcast.15, bf16[384,1024]{1,0:T(8,128)(2,1)S(1)} %bitcast.12), custom_call_target="tpu_custom_call" | custom-call | tf_op jit(solution)/shard_map/pallas_call | solution.py:39
  59.1 5.3 %all-to-all-start.1 = ((f32[24,8,128]{2,1,0:T(8,128)}), f32[24,8,128]{2,1,0:T(8,128)S(1)}, u32[]{:S(2)}, u32[]{:S(2)}) async-start(f32[24,8,128]{2,1,0:T(8,128)} %get-tuple-element.26), calls=%async_computation.1 | async-start | bytes 196608 | tf_op jit(solution)/shard_map/all_to_all | solution.py:29
  64.4 6.7 %all-gather.1 = f32[32,128]{1,0:T(8,128)S(1)} all-gather(f32[8,128]{1,0:T(8,128)S(1)} %get-tuple-element.27), channel_id=3, replica_groups=mesh['xl'=2,'z'=12,'y'=8,'xh'=2,'c'=2] {'xh','c'}, dimensions={0}, use_global_device_ids=true | all-gather | bytes 20480 | tf_op jit(solution)/shard_map/all_gather | solution.py:242
  71.2 3.6 %all-to-all-done.1.col = f32[24,8,128]{2,1,0:T(8,128)S(1)} async-done(((f32[24,8,128]{2,1,0:T(8,128)}), f32[24,8,128]{2,1,0:T(8,128)S(1)}, u32[]{:S(2)}, u32[]{:S(2)}) %all-to-all-start.1) | async-done | bytes 98336 | tf_op jit(solution)/shard_map/all_to_all | solution.py:29
  74.7 0.2 shard_map.61
  74.9 12.8 %all_to_all.20.got = f32[8,8,128]{2,1,0:T(8,128)S(1)} all-to-all(f32[8,8,128]{2,1,0:T(8,128)S(1)} %get-tuple-element.28), channel_id=1, replica_groups=mesh['xl'=2,'z'=12,'y'=8,'xh'=2,'c'=2] {'y'}, dimensions={0} | all-to-all | bytes 65536 | tf_op jit(solution)/shard_map/all_to_all | solution.py:29
  87.7 1.9 %shard_map.62 = (bf16[264,1024]{1,0:T(8,128)(2,1)S(1)}, bf16[200,1024]{1,0:T(8,128)(2,1)S(1)}, f32[192,1024]{1,0:T(8,128)S(1)}, f32[16,128]{1,0:T(8,128)S(1)}, bf16[2,256,384]{2,1,0:T(8,128)(2,1)S(1)}) custom-call(s32[6]{0:T(128)S(1)} %stack.27.idx, f32[1]{0:T(128)S(6)} %copy.6.fac, f32[512,384]{1,0:T(8,128)S(1)} %get-tuple-element.25.sc, ...), custom_call_target="tpu_custom_call" | custom-call | tf_op jit(solution)/shard_map/pallas_call | solution.py:39
  89.6 0.0 copy-start.2
  89.6 0.8 copy-done.2
  90.4 2.6 %collective-permute-start.1 = (bf16[200,1024]{1,0:T(8,128)(2,1)S(1)}, bf16[200,1024]{1,0:T(8,128)(2,1)S(1)}, u32[]{:S(2)}, u32[]{:S(2)}) collective-permute-start(bf16[200,1024]{1,0:T(8,128)(2,1)S(1)} %get-tuple-element.32), channel_id=1, source_target_pairs={{0,384},{384,0},{1,385},{385,1},{2,386},{386,2},{3,387},{387,3},{4... | collective-permute-start | bytes 1228808 | tf_op jit(solution)/shard_map/ppermute | solution.py:34
  93.0 7.3 %collective-permute-done.1.came = bf16[200,1024]{1,0:T(8,128)(2,1)S(1)} collective-permute-done((bf16[200,1024]{1,0:T(8,128)(2,1)S(1)}, bf16[200,1024]{1,0:T(8,128)(2,1)S(1)}, u32[]{:S(2)}, u32[]{:S(2)}) %collective-permute-start.1) | collective-permute-done | bytes 409632 | tf_op jit(solution)/shard_map/ppermute | solution.py:34
  100.2 1.0 shard_map.63
  101.2 0.0 copy-start.3
  101.2 7.9 %all-to-all-start.3 = ((bf16[12,136,128]{2,1,0:T(8,128)(2,1)}), bf16[12,136,128]{2,1,0:T(8,128)(2,1)S(1)}, u32[]{:S(2)}, u32[]{:S(2)}) async-start(bf16[12,136,128]{2,1,0:T(8,128)(2,1)} %shard_map.63), calls=%async_computation.3 | async-start | bytes 835584 | tf_op jit(solution)/shard_map/all_to_all | solution.py:29
  109.1 0.0 copy-done.3
  109.1 1.9 %collective-permute-start.2 = (bf16[264,1024]{1,0:T(8,128)(2,1)S(1)}, bf16[264,1024]{1,0:T(8,128)(2,1)S(1)}, u32[]{:S(2)}, u32[]{:S(2)}) collective-permute-start(bf16[264,1024]{1,0:T(8,128)(2,1)S(1)} %copy-done.3), channel_id=1, source_target_pairs={{0,1},{1,0},{2,3},{3,2},{4,5},{5,4},{6,7},{7,6},{8,9},{9,8},{10,11... | collective-permute-start | bytes 1622024 | tf_op jit(solution)/shard_map/ppermute | solution.py:34
  111.0 1.0 shard_map.64.here
  112.0 0.9 collective-permute-done.2.came
  112.9 0.7 shard_map.65
  113.7 2.6 %collective-permute-start.3 = (bf16[136,1024]{1,0:T(8,128)(2,1)S(1)}, bf16[136,1024]{1,0:T(8,128)(2,1)S(1)}, u32[]{:S(2)}, u32[]{:S(2)}) collective-permute-start(bf16[136,1024]{1,0:T(8,128)(2,1)S(1)} %get-tuple-element.37), channel_id=1, source_target_pairs={{0,2},{2,0},{1,3},{3,1},{4,6},{6,4},{5,7},{7,5},{8,10},{10,8},{9,1... | collective-permute-start | bytes 835592 | tf_op jit(solution)/shard_map/ppermute | solution.py:34
  116.3 9.5 %collective-permute-done.3.got = bf16[136,1024]{1,0:T(8,128)(2,1)S(1)} collective-permute-done((bf16[136,1024]{1,0:T(8,128)(2,1)S(1)}, bf16[136,1024]{1,0:T(8,128)(2,1)S(1)}, u32[]{:S(2)}, u32[]{:S(2)}) %collective-permute-start.3) | collective-permute-done | bytes 278560 | tf_op jit(solution)/shard_map/ppermute | solution.py:34
  125.8 0.7 shard_map.66
  126.5 2.5 %collective-permute-start.4 = (bf16[48,1024]{1,0:T(8,128)(2,1)S(1)}, bf16[48,1024]{1,0:T(8,128)(2,1)S(1)}, u32[]{:S(2)}, u32[]{:S(2)}) collective-permute-start(bf16[48,1024]{1,0:T(8,128)(2,1)S(1)} %get-tuple-element.41), channel_id=1, source_target_pairs={{0,4},{4,8},{8,12},{12,16},{16,20},{20,24},{24,28},{28,0},{1,5},{5... | collective-permute-start | bytes 294920 | tf_op jit(solution)/shard_map/ppermute | solution.py:34
  128.9 3.4 %collective-permute-start.5 = (bf16[32,1024]{1,0:T(8,128)(2,1)S(1)}, bf16[32,1024]{1,0:T(8,128)(2,1)S(1)}, u32[]{:S(2)}, u32[]{:S(2)}) collective-permute-start(bf16[32,1024]{1,0:T(8,128)(2,1)S(1)} %get-tuple-element.42), channel_id=1, source_target_pairs={{0,28},{4,0},{8,4},{12,8},{16,12},{20,16},{24,20},{28,24},{1,29},{... | collective-permute-start | bytes 196616 | tf_op jit(solution)/shard_map/ppermute | solution.py:34
  132.3 2.8 %collective-permute-done.5.high = bf16[32,1024]{1,0:T(8,128)(2,1)S(1)} collective-permute-done((bf16[32,1024]{1,0:T(8,128)(2,1)S(1)}, bf16[32,1024]{1,0:T(8,128)(2,1)S(1)}, u32[]{:S(2)}, u32[]{:S(2)}) %collective-permute-start.5) | collective-permute-done | bytes 65568 | tf_op jit(solution)/shard_map/ppermute | solution.py:34
  135.1 0.0 collective-permute-done.4.low
  135.1 3.4 %collective-permute-start.6 = (bf16[16,1024]{1,0:T(8,128)(2,1)S(1)}, bf16[16,1024]{1,0:T(8,128)(2,1)S(1)}, u32[]{:S(2)}, u32[]{:S(2)}) collective-permute-start(bf16[16,1024]{1,0:T(8,128)(2,1)S(1)} %get-tuple-element.44), channel_id=1, source_target_pairs={{0,12},{4,16},{8,20},{12,24},{16,28},{20,0},{24,4},{28,8},{1,13},{... | collective-permute-start | bytes 98312 | tf_op jit(solution)/shard_map/ppermute | solution.py:34
  138.5 5.5 %collective-permute-start.7 = (bf16[16,1024]{1,0:T(8,128)(2,1)S(1)}, bf16[16,1024]{1,0:T(8,128)(2,1)S(1)}, u32[]{:S(2)}, u32[]{:S(2)}) collective-permute-start(bf16[16,1024]{1,0:T(8,128)(2,1)S(1)} %get-tuple-element.45), channel_id=1, source_target_pairs={{0,20},{4,24},{8,28},{12,0},{16,4},{20,8},{24,12},{28,16},{1,21},{... | collective-permute-start | bytes 98312 | tf_op jit(solution)/shard_map/ppermute | solution.py:34
  144.0 0.2 collective-permute-done.6.left
  144.2 3.7 %collective-permute-done.7.right = bf16[16,1024]{1,0:T(8,128)(2,1)S(1)} collective-permute-done((bf16[16,1024]{1,0:T(8,128)(2,1)S(1)}, bf16[16,1024]{1,0:T(8,128)(2,1)S(1)}, u32[]{:S(2)}, u32[]{:S(2)}) %collective-permute-start.7) | collective-permute-done | bytes 32800 | tf_op jit(solution)/shard_map/ppermute | solution.py:34
  147.9 0.7 shard_map.69
  148.6 0.0 all-to-all-done.3.got
  148.6 0.7 shard_map.67
  (1 shorter events, 0.0 us)
Async XLA Ops:
  0.6 0.8 copy-start
  2.5 10.3 %copy-start.1 = (bf16[16,1,1024]{2,0,1:T(8,128)(2,1)S(1)}, bf16[16,1,1024]{2,0,1:T(8,128)(2,1)}, u32[]{:S(2)}) copy-start(bf16[16,1,1024]{2,0,1:T(8,128)(2,1)} %param.4) | copy-start | bytes 98308
  2.5 54.4 %all-to-all-start = ((bf16[32,16,1024]{2,1,0:T(8,128)(2,1)}), bf16[32,16,1024]{2,1,0:T(8,128)(2,1)S(1)}, u32[]{:S(2)}, u32[]{:S(2)}) async-start(bf16[32,16,1024]{2,1,0:T(8,128)(2,1)} %shard_map.58), calls=%async_computation | async-start | bytes 2097152 | tf_op jit(solution)/shard_map/all_to_all | solution.py:29
  12.8 7.9 %collective-permute-start = (bf16[16,1024]{1,0:T(8,128)(2,1)S(1)}, bf16[16,1024]{1,0:T(8,128)(2,1)S(1)}, u32[]{:S(2)}, u32[]{:S(2)}) collective-permute-start(bf16[16,1024]{1,0:T(8,128)(2,1)S(1)} %bitcast.19), channel_id=1, source_target_pairs={{0,384},{384,0},{1,385},{385,1},{2,386},{386,2},{3,387},{387,3},{4... | collective-permute-start | bytes 98312 | tf_op jit(solution)/shard_map/ppermute | solution.py:34
  59.1 15.6 %all-to-all-start.1 = ((f32[24,8,128]{2,1,0:T(8,128)}), f32[24,8,128]{2,1,0:T(8,128)S(1)}, u32[]{:S(2)}, u32[]{:S(2)}) async-start(f32[24,8,128]{2,1,0:T(8,128)} %get-tuple-element.26), calls=%async_computation.1 | async-start | bytes 196608 | tf_op jit(solution)/shard_map/all_to_all | solution.py:29
  89.6 0.8 copy-start.2
  90.4 9.8 %collective-permute-start.1 = (bf16[200,1024]{1,0:T(8,128)(2,1)S(1)}, bf16[200,1024]{1,0:T(8,128)(2,1)S(1)}, u32[]{:S(2)}, u32[]{:S(2)}) collective-permute-start(bf16[200,1024]{1,0:T(8,128)(2,1)S(1)} %get-tuple-element.32), channel_id=1, source_target_pairs={{0,384},{384,0},{1,385},{385,1},{2,386},{386,2},{3,387},{387,3},{4... | collective-permute-start | bytes 1228808 | tf_op jit(solution)/shard_map/ppermute | solution.py:34
  101.2 7.9 %copy-start.3 = (bf16[264,1024]{1,0:T(8,128)(2,1)S(1)}, bf16[264,1024]{1,0:T(8,128)(2,1)}, u32[]{:S(2)}) copy-start(bf16[264,1024]{1,0:T(8,128)(2,1)} %copy-done.2) | copy-start | bytes 1622020
  101.2 47.4 %all-to-all-start.3 = ((bf16[12,136,128]{2,1,0:T(8,128)(2,1)}), bf16[12,136,128]{2,1,0:T(8,128)(2,1)S(1)}, u32[]{:S(2)}, u32[]{:S(2)}) async-start(bf16[12,136,128]{2,1,0:T(8,128)(2,1)} %shard_map.63), calls=%async_computation.3 | async-start | bytes 835584 | tf_op jit(solution)/shard_map/all_to_all | solution.py:29
  109.1 3.8 %collective-permute-start.2 = (bf16[264,1024]{1,0:T(8,128)(2,1)S(1)}, bf16[264,1024]{1,0:T(8,128)(2,1)S(1)}, u32[]{:S(2)}, u32[]{:S(2)}) collective-permute-start(bf16[264,1024]{1,0:T(8,128)(2,1)S(1)} %copy-done.3), channel_id=1, source_target_pairs={{0,1},{1,0},{2,3},{3,2},{4,5},{5,4},{6,7},{7,6},{8,9},{9,8},{10,11... | collective-permute-start | bytes 1622024 | tf_op jit(solution)/shard_map/ppermute | solution.py:34
  113.7 12.1 %collective-permute-start.3 = (bf16[136,1024]{1,0:T(8,128)(2,1)S(1)}, bf16[136,1024]{1,0:T(8,128)(2,1)S(1)}, u32[]{:S(2)}, u32[]{:S(2)}) collective-permute-start(bf16[136,1024]{1,0:T(8,128)(2,1)S(1)} %get-tuple-element.37), channel_id=1, source_target_pairs={{0,2},{2,0},{1,3},{3,1},{4,6},{6,4},{5,7},{7,5},{8,10},{10,8},{9,1... | collective-permute-start | bytes 835592 | tf_op jit(solution)/shard_map/ppermute | solution.py:34
  126.5 8.6 %collective-permute-start.4 = (bf16[48,1024]{1,0:T(8,128)(2,1)S(1)}, bf16[48,1024]{1,0:T(8,128)(2,1)S(1)}, u32[]{:S(2)}, u32[]{:S(2)}) collective-permute-start(bf16[48,1024]{1,0:T(8,128)(2,1)S(1)} %get-tuple-element.41), channel_id=1, source_target_pairs={{0,4},{4,8},{8,12},{12,16},{16,20},{20,24},{24,28},{28,0},{1,5},{5... | collective-permute-start | bytes 294920 | tf_op jit(solution)/shard_map/ppermute | solution.py:34
  128.9 6.2 %collective-permute-start.5 = (bf16[32,1024]{1,0:T(8,128)(2,1)S(1)}, bf16[32,1024]{1,0:T(8,128)(2,1)S(1)}, u32[]{:S(2)}, u32[]{:S(2)}) collective-permute-start(bf16[32,1024]{1,0:T(8,128)(2,1)S(1)} %get-tuple-element.42), channel_id=1, source_target_pairs={{0,28},{4,0},{8,4},{12,8},{16,12},{20,16},{24,20},{28,24},{1,29},{... | collective-permute-start | bytes 196616 | tf_op jit(solution)/shard_map/ppermute | solution.py:34
  135.1 9.1 %collective-permute-start.6 = (bf16[16,1024]{1,0:T(8,128)(2,1)S(1)}, bf16[16,1024]{1,0:T(8,128)(2,1)S(1)}, u32[]{:S(2)}, u32[]{:S(2)}) collective-permute-start(bf16[16,1024]{1,0:T(8,128)(2,1)S(1)} %get-tuple-element.44), channel_id=1, source_target_pairs={{0,12},{4,16},{8,20},{12,24},{16,28},{20,0},{24,4},{28,8},{1,13},{... | collective-permute-start | bytes 98312 | tf_op jit(solution)/shard_map/ppermute | solution.py:34
  138.5 9.4 %collective-permute-start.7 = (bf16[16,1024]{1,0:T(8,128)(2,1)S(1)}, bf16[16,1024]{1,0:T(8,128)(2,1)S(1)}, u32[]{:S(2)}, u32[]{:S(2)}) collective-permute-start(bf16[16,1024]{1,0:T(8,128)(2,1)S(1)} %get-tuple-element.45), channel_id=1, source_target_pairs={{0,20},{4,24},{8,28},{12,0},{16,4},{20,8},{24,12},{28,16},{1,21},{... | collective-permute-start | bytes 98312 | tf_op jit(solution)/shard_map/ppermute | solution.py:34

commit v11 on v10

--- a/solution.py
+++ b/solution.py
@@ -84,7 +84,7 @@
     return row_ids == col_ids
 
 
-def spread_kernel(block, out):
+def spread_kernel(idx, block, out):
     tile = block[...]
     for n in range(N_COL):
         out[n] = tile
@@ -96,7 +96,7 @@
     out[1 - xl] = came[...]
 
 
-def score_kernel(idx, fac, im, tx, sc, cpack, rpack):
+def score_kernel(fac, im, tx, sc, cpack):
     s = fac[0] * lax.dot_general(im[...], tx[...], (((1,), (1,)), ((), ())), preferred_element_type=F32)
     sc[...] = s
     peak = jnp.max(s, axis=0, keepdims=True)
@@ -105,6 +105,10 @@
         tile = jnp.broadcast_to(col[:, k * LANES : (k + 1) * LANES], (N_ROW, LANES))
         for n in range(N_ROW):
             cpack[n, k : k + 1, :] = tile[n : n + 1]
+
+
+def row_kernel(idx, sc, rpack):
+    s = sc[...]
     peak = jnp.max(s, axis=1, keepdims=True)
     row = peak + jnp.log(jnp.sum(jnp.exp(s - peak), axis=1, keepdims=True))
     for k in range(ROWS // LANES):
@@ -226,19 +230,20 @@
 def body(image_emb, text_emb, logit_scale):
     places = [lax.axis_index(a) for a in (ROW, COL, "c", "xh", "y", "xl")]
     idx = jnp.stack(places).astype(jnp.int32)
-    (spread,) = call(spread_kernel, [((N_COL, EACH, WIDTH), BF16)], [], image_emb.reshape(EACH, WIDTH))
+    (spread,) = call(spread_kernel, [((N_COL, EACH, WIDTH), BF16)], [], idx, image_emb.reshape(EACH, WIDTH))
     images = exchange(spread, ("c", "xh", "y")).reshape(ROWS, WIDTH)
     own = text_emb.reshape(EACH, WIDTH)
     came = shift(own, "xl", 1)
     (texts,) = call(stack_kernel, [((N_XL, EACH, WIDTH), BF16)], [], idx, own, came)
     texts = lax.all_gather(texts, "z").reshape(COLS, WIDTH)
-    scores, cpack, rpack = call(
+    scores, cpack = call(
         score_kernel,
-        [((ROWS, COLS), F32), ((N_ROW, 8, LANES), F32), ((8, LANES), F32)],
+        [((ROWS, COLS), F32), ((N_ROW, COLS // LANES, LANES), F32)],
         [],
-        idx, logit_scale, images, texts,
+        logit_scale, images, texts,
     )
     col_got = exchange(cpack, ROW)
+    (rpack,) = call(row_kernel, [((8, LANES), F32)], [], idx, scores)
     near = lax.all_gather(rpack, ("xh", "c"))
     col_lse, ypack = call(merge_kernel, [((8, COLS), F32), ((N_Y, 8, LANES), F32)], [], col_got, near)
     row_got = exchange(ypack, "y")

time: 150 us -> 151 us (level)
  starting transfers between devices: 50.9 us -> 52.7 us
  waiting for transfers between devices: 29.4 us -> 27.8 us
    pallas_call x12 -> x13, Pallas kernels: 10.7 us -> 11.6 us  [call(): pl.pallas_call(kernel, out_shape=[jax.ShapeDtypeStruct(s, d) for s, d in...]
  transfers between devices with their start and end apart: 11 -> 11, of which waited for: 8 -> 8; matrix products, arithmetic and copies ran while one was open for 0% -> 0% of each run, Pallas kernels for 2% -> 3%
where the time goes in v11:
time: 151 us; the launch traced here: 150 us
  blocking collectives  55.1 us (36%)
  starting transfers between devices  52.7 us (35%)
  waiting for transfers between devices  27.8 us (18%)
  Pallas kernels  11.6 us (8%)
  local copies, waits for them, and re-layouts  1.54 us (1%)
    all_gather x1, blocking collectives, body(): texts = lax.all_gather(texts, 'z').reshape(COLS, WIDTH)  35.8 us
    ppermute x8, starting transfers between devices, shift(): return lax.ppermute(x, axis, [(i, (i + k) % n) for i in range(n)])  27.8 us
    ppermute x8, waiting for transfers between devices, shift(): return lax.ppermute(x, axis, [(i, (i + k) % n) for i in range(n)])  25.7 us
    all_to_all x3, starting transfers between devices, exchange(): return lax.all_to_all(x, axes, 0, 0, tiled=False)  24.9 us
    all_to_all x1, blocking collectives, exchange(): return lax.all_to_all(x, axes, 0, 0, tiled=False)  12.6 us
    pallas_call x13, Pallas kernels, call(): pl.pallas_call(kernel, out_shape=[jax.ShapeDtypeStruct(s, d) for s, d in...  11.6 us
    all_gather x1, blocking collectives, body(): near = lax.all_gather(rpack, ('xh', 'c'))  6.71 us
  transfers between devices with their start and end apart: 11, of which 8 were waited for; matrix products, arithmetic and copies ran while one was open for 0% of the time, Pallas kernels for 3%

profile of v11, /device:TPU:14, one launch (start us, length us, event | category | flops | bytes accessed | tf_op | source)
XLA Modules:
  0.0 150.2 jit_solution(14218243958587645391)
XLA Ops:
  0.6 0.0 copy-start
  0.7 0.1 stack.27.idx
  0.7 0.6 copy-done
  1.4 1.6 %shard_map.58 = bf16[32,16,1024]{2,1,0:T(8,128)(2,1)} custom-call(s32[6]{0:T(128)S(1)} %stack.27.idx, bf16[16,1024]{1,0:T(8,128)(2,1)S(1)} %bitcast.18), custom_call_target="tpu_custom_call" | custom-call | tf_op jit(solution)/shard_map/pallas_call | solution.py:39
  3.0 0.0 copy-start.1
  3.0 10.2 %all-to-all-start = ((bf16[32,16,1024]{2,1,0:T(8,128)(2,1)}), bf16[32,16,1024]{2,1,0:T(8,128)(2,1)S(1)}, u32[]{:S(2)}, u32[]{:S(2)}) async-start(bf16[32,16,1024]{2,1,0:T(8,128)(2,1)} %shard_map.58), calls=%async_computation | async-start | bytes 2097152 | tf_op jit(solution)/shard_map/all_to_all | solution.py:29
  13.3 0.0 copy-done.1
  13.3 5.6 %collective-permute-start = (bf16[16,1024]{1,0:T(8,128)(2,1)S(1)}, bf16[16,1024]{1,0:T(8,128)(2,1)S(1)}, u32[]{:S(2)}, u32[]{:S(2)}) collective-permute-start(bf16[16,1024]{1,0:T(8,128)(2,1)S(1)} %bitcast.19), channel_id=1, source_target_pairs={{0,384},{384,0},{1,385},{385,1},{2,386},{386,2},{3,387},{387,3},{4... | collective-permute-start | bytes 98312 | tf_op jit(solution)/shard_map/ppermute | solution.py:34
  19.6 1.6 %collective-permute-done.came = bf16[16,1024]{1,0:T(8,128)(2,1)S(1)} collective-permute-done((bf16[16,1024]{1,0:T(8,128)(2,1)S(1)}, bf16[16,1024]{1,0:T(8,128)(2,1)S(1)}, u32[]{:S(2)}, u32[]{:S(2)}) %collective-permute-start) | collective-permute-done | bytes 32800 | tf_op jit(solution)/shard_map/ppermute | solution.py:34
  21.2 0.5 shard_map.59
  21.7 35.8 %all-gather = bf16[24,16,1024]{2,1,0:T(8,128)(2,1)S(1)} all-gather(bf16[2,16,1024]{2,1,0:T(8,128)(2,1)S(1)} %shard_map.59), channel_id=2, replica_groups=mesh['xl'=2,'z'=12,'y'=8,'xh'=2,'c'=2] {'z'}, dimensions={0}, use_global_device_ids=true | all-gather | bytes 851968 | tf_op jit(solution)/shard_map/all_gather | solution.py:238
  57.5 0.0 all-to-all-done
  57.5 1.5 %shard_map.60 = (f32[512,384]{1,0:T(8,128)S(1)}, f32[24,3,128]{2,1,0:T(4,128)}) custom-call(f32[1]{0:T(128)S(6)} %copy.6.fac, bf16[512,1024]{1,0:T(8,128)(2,1)S(1)} %bitcast.15, bf16[384,1024]{1,0:T(8,128)(2,1)S(1)} %bitcast.12), custom_call_target="tpu_custom_call" | custom-call | tf_op jit(solution)/shard_map/pallas_call | solution.py:39
  59.0 5.3 %all-to-all-start.1 = ((f32[24,3,128]{2,1,0:T(4,128)}), f32[24,3,128]{2,1,0:T(4,128)S(1)}, u32[]{:S(2)}, u32[]{:S(2)}) async-start(f32[24,3,128]{2,1,0:T(4,128)} %get-tuple-element.25), calls=%async_computation.1 | async-start | bytes 98304 | tf_op jit(solution)/shard_map/all_to_all | solution.py:29
  64.3 1.0 shard_map.61
  65.3 6.7 %all-gather.1 = f32[32,128]{1,0:T(8,128)S(1)} all-gather(f32[8,128]{1,0:T(8,128)S(1)} %shard_map.61), channel_id=3, replica_groups=mesh['xl'=2,'z'=12,'y'=8,'xh'=2,'c'=2] {'xh','c'}, dimensions={0}, use_global_device_ids=true | all-gather | bytes 20480 | tf_op jit(solution)/shard_map/all_gather | solution.py:247
  72.0 2.2 %all-to-all-done.1.col = f32[24,3,128]{2,1,0:T(4,128)S(1)} async-done(((f32[24,3,128]{2,1,0:T(4,128)}), f32[24,3,128]{2,1,0:T(4,128)S(1)}, u32[]{:S(2)}, u32[]{:S(2)}) %all-to-all-start.1) | async-done | bytes 36896 | tf_op jit(solution)/shard_map/all_to_all | solution.py:29
  74.2 0.2 shard_map.62
  74.4 12.6 %all_to_all.20.got = f32[8,8,128]{2,1,0:T(8,128)S(1)} all-to-all(f32[8,8,128]{2,1,0:T(8,128)S(1)} %get-tuple-element.26), channel_id=1, replica_groups=mesh['xl'=2,'z'=12,'y'=8,'xh'=2,'c'=2] {'y'}, dimensions={0} | all-to-all | bytes 65536 | tf_op jit(solution)/shard_map/all_to_all | solution.py:29
  87.0 1.9 %shard_map.63 = (bf16[264,1024]{1,0:T(8,128)(2,1)S(1)}, bf16[200,1024]{1,0:T(8,128)(2,1)S(1)}, f32[192,1024]{1,0:T(8,128)S(1)}, f32[16,128]{1,0:T(8,128)S(1)}, bf16[2,256,384]{2,1,0:T(8,128)(2,1)S(1)}) custom-call(s32[6]{0:T(128)S(1)} %stack.27.idx, f32[1]{0:T(128)S(6)} %copy.6.fac, f32[512,384]{1,0:T(8,128)S(1)} %get-tuple-element.24.sc, ...), custom_call_target="tpu_custom_call" | custom-call | tf_op jit(solution)/shard_map/pallas_call | solution.py:39
  88.9 0.0 copy-start.2
  89.0 0.8 copy-done.2
  89.8 2.9 %collective-permute-start.1 = (bf16[200,1024]{1,0:T(8,128)(2,1)S(1)}, bf16[200,1024]{1,0:T(8,128)(2,1)S(1)}, u32[]{:S(2)}, u32[]{:S(2)}) collective-permute-start(bf16[200,1024]{1,0:T(8,128)(2,1)S(1)} %get-tuple-element.30), channel_id=1, source_target_pairs={{0,384},{384,0},{1,385},{385,1},{2,386},{386,2},{3,387},{387,3},{4... | collective-permute-start | bytes 1228808 | tf_op jit(solution)/shard_map/ppermute | solution.py:34
  92.7 7.0 %collective-permute-done.1.came = bf16[200,1024]{1,0:T(8,128)(2,1)S(1)} collective-permute-done((bf16[200,1024]{1,0:T(8,128)(2,1)S(1)}, bf16[200,1024]{1,0:T(8,128)(2,1)S(1)}, u32[]{:S(2)}, u32[]{:S(2)}) %collective-permute-start.1) | collective-permute-done | bytes 409632 | tf_op jit(solution)/shard_map/ppermute | solution.py:34
  99.7 1.0 shard_map.64
  100.7 0.0 copy-start.3
  100.7 9.3 %all-to-all-start.3 = ((bf16[12,136,128]{2,1,0:T(8,128)(2,1)}), bf16[12,136,128]{2,1,0:T(8,128)(2,1)S(1)}, u32[]{:S(2)}, u32[]{:S(2)}) async-start(bf16[12,136,128]{2,1,0:T(8,128)(2,1)} %shard_map.64), calls=%async_computation.3 | async-start | bytes 835584 | tf_op jit(solution)/shard_map/all_to_all | solution.py:29
  110.0 0.0 copy-done.3
  110.0 1.9 %collective-permute-start.2 = (bf16[264,1024]{1,0:T(8,128)(2,1)S(1)}, bf16[264,1024]{1,0:T(8,128)(2,1)S(1)}, u32[]{:S(2)}, u32[]{:S(2)}) collective-permute-start(bf16[264,1024]{1,0:T(8,128)(2,1)S(1)} %copy-done.3), channel_id=1, source_target_pairs={{0,1},{1,0},{2,3},{3,2},{4,5},{5,4},{6,7},{7,6},{8,9},{9,8},{10,11... | collective-permute-start | bytes 1622024 | tf_op jit(solution)/shard_map/ppermute | solution.py:34
  111.9 1.0 shard_map.65.here
  112.9 0.9 collective-permute-done.2.came
  113.8 0.7 shard_map.66
  114.6 2.6 %collective-permute-start.3 = (bf16[136,1024]{1,0:T(8,128)(2,1)S(1)}, bf16[136,1024]{1,0:T(8,128)(2,1)S(1)}, u32[]{:S(2)}, u32[]{:S(2)}) collective-permute-start(bf16[136,1024]{1,0:T(8,128)(2,1)S(1)} %get-tuple-element.35), channel_id=1, source_target_pairs={{0,2},{2,0},{1,3},{3,1},{4,6},{6,4},{5,7},{7,5},{8,10},{10,8},{9,1... | collective-permute-start | bytes 835592 | tf_op jit(solution)/shard_map/ppermute | solution.py:34
  117.2 9.5 %collective-permute-done.3.got = bf16[136,1024]{1,0:T(8,128)(2,1)S(1)} collective-permute-done((bf16[136,1024]{1,0:T(8,128)(2,1)S(1)}, bf16[136,1024]{1,0:T(8,128)(2,1)S(1)}, u32[]{:S(2)}, u32[]{:S(2)}) %collective-permute-start.3) | collective-permute-done | bytes 278560 | tf_op jit(solution)/shard_map/ppermute | solution.py:34
  126.7 0.7 shard_map.67
  127.4 2.5 %collective-permute-start.4 = (bf16[48,1024]{1,0:T(8,128)(2,1)S(1)}, bf16[48,1024]{1,0:T(8,128)(2,1)S(1)}, u32[]{:S(2)}, u32[]{:S(2)}) collective-permute-start(bf16[48,1024]{1,0:T(8,128)(2,1)S(1)} %get-tuple-element.39), channel_id=1, source_target_pairs={{0,4},{4,8},{8,12},{12,16},{16,20},{20,24},{24,28},{28,0},{1,5},{5... | collective-permute-start | bytes 294920 | tf_op jit(solution)/shard_map/ppermute | solution.py:34
  129.8 3.4 %collective-permute-start.5 = (bf16[32,1024]{1,0:T(8,128)(2,1)S(1)}, bf16[32,1024]{1,0:T(8,128)(2,1)S(1)}, u32[]{:S(2)}, u32[]{:S(2)}) collective-permute-start(bf16[32,1024]{1,0:T(8,128)(2,1)S(1)} %get-tuple-element.40), channel_id=1, source_target_pairs={{0,28},{4,0},{8,4},{12,8},{16,12},{20,16},{24,20},{28,24},{1,29},{... | collective-permute-start | bytes 196616 | tf_op jit(solution)/shard_map/ppermute | solution.py:34
  133.2 2.8 %collective-permute-done.5.high = bf16[32,1024]{1,0:T(8,128)(2,1)S(1)} collective-permute-done((bf16[32,1024]{1,0:T(8,128)(2,1)S(1)}, bf16[32,1024]{1,0:T(8,128)(2,1)S(1)}, u32[]{:S(2)}, u32[]{:S(2)}) %collective-permute-start.5) | collective-permute-done | bytes 65568 | tf_op jit(solution)/shard_map/ppermute | solution.py:34
  136.0 0.0 collective-permute-done.4.low
  136.0 3.4 %collective-permute-start.6 = (bf16[16,1024]{1,0:T(8,128)(2,1)S(1)}, bf16[16,1024]{1,0:T(8,128)(2,1)S(1)}, u32[]{:S(2)}, u32[]{:S(2)}) collective-permute-start(bf16[16,1024]{1,0:T(8,128)(2,1)S(1)} %get-tuple-element.42), channel_id=1, source_target_pairs={{0,12},{4,16},{8,20},{12,24},{16,28},{20,0},{24,4},{28,8},{1,13},{... | collective-permute-start | bytes 98312 | tf_op jit(solution)/shard_map/ppermute | solution.py:34
  139.4 5.5 %collective-permute-start.7 = (bf16[16,1024]{1,0:T(8,128)(2,1)S(1)}, bf16[16,1024]{1,0:T(8,128)(2,1)S(1)}, u32[]{:S(2)}, u32[]{:S(2)}) collective-permute-start(bf16[16,1024]{1,0:T(8,128)(2,1)S(1)} %get-tuple-element.43), channel_id=1, source_target_pairs={{0,20},{4,24},{8,28},{12,0},{16,4},{20,8},{24,12},{28,16},{1,21},{... | collective-permute-start | bytes 98312 | tf_op jit(solution)/shard_map/ppermute | solution.py:34
  144.9 0.2 collective-permute-done.6.left
  145.1 3.7 %collective-permute-done.7.right = bf16[16,1024]{1,0:T(8,128)(2,1)S(1)} collective-permute-done((bf16[16,1024]{1,0:T(8,128)(2,1)S(1)}, bf16[16,1024]{1,0:T(8,128)(2,1)S(1)}, u32[]{:S(2)}, u32[]{:S(2)}) %collective-permute-start.7) | collective-permute-done | bytes 32800 | tf_op jit(solution)/shard_map/ppermute | solution.py:34
  148.8 0.7 shard_map.70
  149.5 0.0 all-to-all-done.3.got
  149.5 0.7 shard_map.68
  (1 shorter events, 0.0 us)
Async XLA Ops:
  0.6 0.8 copy-start
  3.0 10.3 %copy-start.1 = (bf16[16,1,1024]{2,0,1:T(8,128)(2,1)S(1)}, bf16[16,1,1024]{2,0,1:T(8,128)(2,1)}, u32[]{:S(2)}) copy-start(bf16[16,1,1024]{2,0,1:T(8,128)(2,1)} %param.4) | copy-start | bytes 98308
  3.0 54.4 %all-to-all-start = ((bf16[32,16,1024]{2,1,0:T(8,128)(2,1)}), bf16[32,16,1024]{2,1,0:T(8,128)(2,1)S(1)}, u32[]{:S(2)}, u32[]{:S(2)}) async-start(bf16[32,16,1024]{2,1,0:T(8,128)(2,1)} %shard_map.58), calls=%async_computation | async-start | bytes 2097152 | tf_op jit(solution)/shard_map/all_to_all | solution.py:29
  13.3 7.9 %collective-permute-start = (bf16[16,1024]{1,0:T(8,128)(2,1)S(1)}, bf16[16,1024]{1,0:T(8,128)(2,1)S(1)}, u32[]{:S(2)}, u32[]{:S(2)}) collective-permute-start(bf16[16,1024]{1,0:T(8,128)(2,1)S(1)} %bitcast.19), channel_id=1, source_target_pairs={{0,384},{384,0},{1,385},{385,1},{2,386},{386,2},{3,387},{387,3},{4... | collective-permute-start | bytes 98312 | tf_op jit(solution)/shard_map/ppermute | solution.py:34
  59.0 15.2 %all-to-all-start.1 = ((f32[24,3,128]{2,1,0:T(4,128)}), f32[24,3,128]{2,1,0:T(4,128)S(1)}, u32[]{:S(2)}, u32[]{:S(2)}) async-start(f32[24,3,128]{2,1,0:T(4,128)} %get-tuple-element.25), calls=%async_computation.1 | async-start | bytes 98304 | tf_op jit(solution)/shard_map/all_to_all | solution.py:29
  88.9 0.8 copy-start.2
  89.8 9.9 %collective-permute-start.1 = (bf16[200,1024]{1,0:T(8,128)(2,1)S(1)}, bf16[200,1024]{1,0:T(8,128)(2,1)S(1)}, u32[]{:S(2)}, u32[]{:S(2)}) collective-permute-start(bf16[200,1024]{1,0:T(8,128)(2,1)S(1)} %get-tuple-element.30), channel_id=1, source_target_pairs={{0,384},{384,0},{1,385},{385,1},{2,386},{386,2},{3,387},{387,3},{4... | collective-permute-start | bytes 1228808 | tf_op jit(solution)/shard_map/ppermute | solution.py:34
  100.7 9.3 %copy-start.3 = (bf16[264,1024]{1,0:T(8,128)(2,1)S(1)}, bf16[264,1024]{1,0:T(8,128)(2,1)}, u32[]{:S(2)}) copy-start(bf16[264,1024]{1,0:T(8,128)(2,1)} %copy-done.2) | copy-start | bytes 1622020
  100.7 48.8 %all-to-all-start.3 = ((bf16[12,136,128]{2,1,0:T(8,128)(2,1)}), bf16[12,136,128]{2,1,0:T(8,128)(2,1)S(1)}, u32[]{:S(2)}, u32[]{:S(2)}) async-start(bf16[12,136,128]{2,1,0:T(8,128)(2,1)} %shard_map.64), calls=%async_computation.3 | async-start | bytes 835584 | tf_op jit(solution)/shard_map/all_to_all | solution.py:29
  110.0 3.8 %collective-permute-start.2 = (bf16[264,1024]{1,0:T(8,128)(2,1)S(1)}, bf16[264,1024]{1,0:T(8,128)(2,1)S(1)}, u32[]{:S(2)}, u32[]{:S(2)}) collective-permute-start(bf16[264,1024]{1,0:T(8,128)(2,1)S(1)} %copy-done.3), channel_id=1, source_target_pairs={{0,1},{1,0},{2,3},{3,2},{4,5},{5,4},{6,7},{7,6},{8,9},{9,8},{10,11... | collective-permute-start | bytes 1622024 | tf_op jit(solution)/shard_map/ppermute | solution.py:34
  114.6 12.1 %collective-permute-start.3 = (bf16[136,1024]{1,0:T(8,128)(2,1)S(1)}, bf16[136,1024]{1,0:T(8,128)(2,1)S(1)}, u32[]{:S(2)}, u32[]{:S(2)}) collective-permute-start(bf16[136,1024]{1,0:T(8,128)(2,1)S(1)} %get-tuple-element.35), channel_id=1, source_target_pairs={{0,2},{2,0},{1,3},{3,1},{4,6},{6,4},{5,7},{7,5},{8,10},{10,8},{9,1... | collective-permute-start | bytes 835592 | tf_op jit(solution)/shard_map/ppermute | solution.py:34
  127.4 8.6 %collective-permute-start.4 = (bf16[48,1024]{1,0:T(8,128)(2,1)S(1)}, bf16[48,1024]{1,0:T(8,128)(2,1)S(1)}, u32[]{:S(2)}, u32[]{:S(2)}) collective-permute-start(bf16[48,1024]{1,0:T(8,128)(2,1)S(1)} %get-tuple-element.39), channel_id=1, source_target_pairs={{0,4},{4,8},{8,12},{12,16},{16,20},{20,24},{24,28},{28,0},{1,5},{5... | collective-permute-start | bytes 294920 | tf_op jit(solution)/shard_map/ppermute | solution.py:34
  129.8 6.2 %collective-permute-start.5 = (bf16[32,1024]{1,0:T(8,128)(2,1)S(1)}, bf16[32,1024]{1,0:T(8,128)(2,1)S(1)}, u32[]{:S(2)}, u32[]{:S(2)}) collective-permute-start(bf16[32,1024]{1,0:T(8,128)(2,1)S(1)} %get-tuple-element.40), channel_id=1, source_target_pairs={{0,28},{4,0},{8,4},{12,8},{16,12},{20,16},{24,20},{28,24},{1,29},{... | collective-permute-start | bytes 196616 | tf_op jit(solution)/shard_map/ppermute | solution.py:34
  136.0 9.1 %collective-permute-start.6 = (bf16[16,1024]{1,0:T(8,128)(2,1)S(1)}, bf16[16,1024]{1,0:T(8,128)(2,1)S(1)}, u32[]{:S(2)}, u32[]{:S(2)}) collective-permute-start(bf16[16,1024]{1,0:T(8,128)(2,1)S(1)} %get-tuple-element.42), channel_id=1, source_target_pairs={{0,12},{4,16},{8,20},{12,24},{16,28},{20,0},{24,4},{28,8},{1,13},{... | collective-permute-start | bytes 98312 | tf_op jit(solution)/shard_map/ppermute | solution.py:34
  139.4 9.4 %collective-permute-start.7 = (bf16[16,1024]{1,0:T(8,128)(2,1)S(1)}, bf16[16,1024]{1,0:T(8,128)(2,1)S(1)}, u32[]{:S(2)}, u32[]{:S(2)}) collective-permute-start(bf16[16,1024]{1,0:T(8,128)(2,1)S(1)} %get-tuple-element.43), channel_id=1, source_target_pairs={{0,20},{4,24},{8,28},{12,0},{16,4},{20,8},{24,12},{28,16},{1,21},{... | collective-permute-start | bytes 98312 | tf_op jit(solution)/shard_map/ppermute | solution.py:34
